TPU v7x, 32 devices: a whole 2x2x4 slice. The times are simulated.
32 devices in a mesh: mesh: 8 (over y, x, core), state: 4 (over z).
Axes of the slice: x: 2, y: 2, z: 4, core: 2. Of those that a mesh axis runs over, the one named last changes fastest.
Arguments:
- kern_blocks: bfloat16 [192, 16, 128, 128], P('mesh'), may hold values from 4.296875e-06 to 0.13744531
- kern_cols: int32 [192, 16], P('mesh'), may hold values from 0 to 191, as said below
- state_kernel: bfloat16 [512, 512], replicated, may hold values from 0 to 0.61, as said below
- start_v: float32 [24576, 512], P('mesh', 'state'), may hold values from 0.5 to 5
- mu: float32 [24576, 512], P(('mesh', 'state')), may hold values from 0.2 to 2
- nu: float32 [24576, 512], P('mesh', 'state'), may hold values from 0.2 to 2
Outputs:
- potential_u: float32 [24576, 512], P(('mesh', 'state'))
- potential_v: float32 [24576, 512], P('mesh', 'state')
Inputs may be any that keep to these rules, and one draw needn't show every extreme that they name: `kern_cols`: each block row names 16 different block columns, its own block among them. The block rows held by index d of mesh (rows d * 24 to (d + 1) * 24 - 1) refer, among the blocks of index d - 1 and d + 1 (wrapping around 8), only to the last 6 blocks of d - 1 and the first 6 blocks of d + 1, and to all of them; among the blocks of every other index, to at most 2 distinct blocks, and to exactly 2 of index d + 2. How many other indices they reach differs from index to index. `state_kernel`: each row has a positive diagonal entry.
All inputs are finite; a program needn't handle non-finite values.
Results may differ from a plain program's by a relative error of at most 0.0033.
Values may be sent and summed in bfloat16 or wider, within the bound.
No kernel may reach another device: no remote copies, remote signals or barrier semaphores. Data moves between devices by JAX's collectives and lax.ppermute only.
A program may use at most 192 MiB of HBM per device.

v0:
```python
import jax
import jax.numpy as jnp
from jax import lax
from jax.experimental import pallas as pl
from jax.experimental.pallas import tpu as pltpu
from jax.sharding import PartitionSpec as P

CAP_FAR = 2
ITERS = 2
CAP_NEAR = 6


VMEM = pl.BlockSpec(memory_space=pltpu.VMEM)
SMEM = pl.BlockSpec(memory_space=pltpu.SMEM)
INDEX = pl.BlockSpec(memory_space=pltpu.SMEM)
ANY = pl.BlockSpec(memory_space=pl.ANY)
PARAMS = pltpu.CompilerParams(vmem_limit_bytes=16 << 20)
F32, BF16 = jnp.float32, jnp.bfloat16
MOST_SHIFTS = 8


def in_smem(value):
    return pltpu.with_memory_space_constraint(value, pltpu.SMEM)


def here(value):
    return pltpu.with_memory_space_constraint(value, pltpu.VMEM)


def shifted(value, axis, steps):
    count = lax.axis_size(axis)
    return lax.ppermute(value, axis, [(i, (i + steps) % count) for i in range(count)])


def swapped(value, axis):
    return lax.all_to_all(value, axis, split_axis=0, concat_axis=0, tiled=True)


class Plan:
    def __init__(self, kern_blocks, start_v):
        self.rows, self.degree, self.size, _ = kern_blocks.shape
        self.cols = start_v.shape[1]
        self.peers = lax.axis_size("mesh")
        self.states = lax.axis_size("state")
        self.near, self.far = CAP_NEAR, CAP_FAR
        self.far_base = self.rows + 2 * self.near
        self.table = self.far_base + self.peers * self.far
        self.share = self.rows // self.states
        self.shifts = range(2, self.peers - 1) if self.peers <= MOST_SHIFTS else None
        self.order = sorted(range(1, self.states), key=lambda p: abs(2 * p - self.states))

    def blocks(self, count, dtype):
        return pltpu.VMEM((count, self.size, self.cols), dtype)

    def far_blocks(self):
        if self.shifts is None:
            return [self.blocks(self.peers * self.far, BF16)]
        return [self.blocks(self.far, BF16)] * len(self.shifts)

    def far_slots(self, way):
        if self.shifts is None:
            return [(t, 0, t) for t in range(self.peers * self.far)]
        slots = []
        for i, shift in enumerate(self.shifts):
            peer = lax.rem(lax.axis_index("mesh") + way * shift + self.peers, self.peers)
            slots += [(peer * self.far + t, i, t) for t in range(self.far)]
        return slots

    def cost(self, matmul_blocks, nbytes):
        flops = 2 * matmul_blocks * self.size * self.size * self.cols
        return pl.CostEstimate(flops=flops, bytes_accessed=nbytes, transcendentals=0)

    def rows_of(self, p):
        return lax.rem(lax.axis_index("state") - p + self.states, self.states) * self.share


def call(kernel, out_shape, in_specs, args, cost, scratch=(), aliases={}, out_specs=None):
    args = [here(a) if spec is VMEM else a for spec, a in zip(in_specs, args)]
    args = [in_smem(a) if spec is INDEX else a for spec, a in zip(in_specs, args)]
    return pl.pallas_call(
        kernel,
        out_shape=out_shape,
        in_specs=in_specs,
        out_specs=[VMEM] * len(out_shape) if out_specs is None else out_specs,
        scratch_shapes=list(scratch),
        input_output_aliases=aliases,
        compiler_params=PARAMS,
        cost_estimate=cost,
    )(*args)


def begin(plan, kern_cols, start_v):
    rows, near, peers, far = plan.rows, plan.near, plan.peers, plan.far
    n_ask = 1 if plan.shifts is None else len(plan.shifts)

    def kernel(cols_ref, v_hbm, src_ref, *rest):
        asks, (own, head, tail, buf, src_buf, sem) = rest[:n_ask], rest[n_ask:]
        load = pltpu.make_async_copy(v_hbm, buf, sem)
        load.start()
        me = lax.axis_index("mesh")
        cols = cols_ref[...]
        before, after = lax.rem(me + peers - 1, peers), lax.rem(me + 1, peers)
        src = cols - me * rows + near
        src = jnp.where(cols // rows == before, cols - before * rows - (rows - near), src)
        src = jnp.where(cols // rows == after, cols - after * rows + near + rows, src)
        for d in range(peers) if plan.shifts is None else plan.shifts:
            peer = d if plan.shifts is None else lax.rem(me + d, peers)
            place = cols - peer * rows
            of_peer = (place >= 0) & (place < rows)
            if plan.shifts is None:
                of_peer &= (peer != me) & (peer != before) & (peer != after)
            least = jnp.min(jnp.where(of_peer, place, rows))
            most = jnp.max(jnp.where(of_peer, place, 0))
            slot = plan.far_base + peer * far
            src = jnp.where(of_peer, slot + (place != least).astype(jnp.int32), src)
            ask, at = (asks[0], d * far) if plan.shifts is None else (asks[d - 2], 0)
            ask[at] = jnp.minimum(least, most)
            ask[at + 1] = most
        src_buf[...] = src
        load.wait()
        index = pltpu.make_async_copy(src_buf, src_ref, sem)
        index.start()
        for t in range(rows):
            value = buf[t].astype(BF16)
            own[t] = value
            if t < near:
                head[t] = value
            if t >= rows - near:
                tail[t - rows + near] = value
        index.wait()

    ask = jax.ShapeDtypeStruct((peers * far if plan.shifts is None else far,), jnp.int32)
    out = call(
        kernel,
        [pltpu.SMEM(kern_cols.shape, jnp.int32)]
        + [ask] * n_ask
        + [plan.blocks(n, BF16) for n in (rows, near, near)],
        [VMEM, ANY],
        [kern_cols, start_v],
        plan.cost(0, 3 << 20),
        [
            pltpu.VMEM(start_v.shape, F32),
            pltpu.VMEM(kern_cols.shape, jnp.int32),
            pltpu.SemaphoreType.DMA,
        ],
        out_specs=[INDEX] + [SMEM] * n_ask + [VMEM] * 3,
    )
    return out[0], list(out[1 : 1 + n_ask]), out[1 + n_ask :]


def forward(plan, p, sources, kern, inputs, table, first_time):
    share, degree, near, rows = plan.share, plan.degree, plan.near, plan.rows
    gathers = table is None
    n_in = len(inputs) if gathers else 1

    def kernel(src, kern_ref, *rest):
        ins, outs = rest[:n_in], rest[n_in:]
        out, tbl = outs[0], outs[1] if gathers else ins[0]
        first = plan.rows_of(p)
        held = kern_ref
        if first_time:
            held, sem = outs[-2:]
            loads = [
                pltpu.make_async_copy(kern_ref.at[first + g], held.at[g], sem.at[g])
                for g in range(share)
            ]
            for load in loads:
                load.start()
        if gathers:
            own_ref, left_ref, right_ref = ins[:3]
            far_refs = ins[3:]
            for t in range(near):
                tbl[t] = left_ref[t]
                tbl[near + rows + t] = right_ref[t]
            for t in range(rows):
                tbl[near + t] = own_ref[t]
            for slot, i, t in plan.far_slots(-1):
                tbl[plan.far_base + slot] = far_refs[i][t]
        for g in range(share):
            if first_time:
                loads[g].wait()
            row = first + g
            lhs = jnp.concatenate([held[g, k] for k in range(degree)], axis=1)
            rhs = jnp.concatenate([tbl[src[row, k]] for k in range(degree)], axis=0)
            out[g] = jnp.dot(lhs, rhs, preferred_element_type=F32).astype(BF16)

    out_shape = [plan.blocks(share, BF16)]
    if gathers:
        out_shape.append(plan.blocks(plan.table, BF16))
    if first_time:
        out_shape.append(pltpu.VMEM((share, *kern.shape[1:]), BF16))
    out = call(
        kernel,
        out_shape,
        [INDEX, ANY if first_time else VMEM] + [VMEM] * n_in,
        [sources, kern] + (list(inputs) if gathers else [table]),
        plan.cost(share * degree, 4 << 20),
        [pltpu.SemaphoreType.DMA((share,))] if first_time else (),
    )
    return out[0], out[1] if gathers else table, out[-1] if first_time else kern


def turned(plan, k_ref, p):
    at = lax.rem(lax.axis_index("state") + p, plan.states) * plan.cols
    return k_ref[:, pl.ds(pl.multiple_of(at, plan.cols), plan.cols)]


def mix(plan, pieces, state_kernel, mu, p_first, final):
    states, share, size = plan.states, plan.share, plan.size

    def kernel(*refs):
        a_refs, (k_ref, mu_ref), rest = refs[:states], refs[states : states + 2], refs[states + 2 :]
        rounded, out = rest[:2]
        k_in = jnp.concatenate([turned(plan, k_ref, p) for p in range(states)], axis=1)
        k_out = turned(plan, k_ref, p_first)
        copies = []
        for g in range(share):
            a = jnp.concatenate([ref[g] for ref in a_refs], axis=1)
            mixed = lax.dot_general(a, k_in, (((1,), (1,)), ((), ())), preferred_element_type=F32)
            u = mu_ref[pl.ds(g * size, size), :] / mixed
            if final:
                u_ref, u_buf, sem = rest[2:]
                u_buf[g] = u
                copy = pltpu.make_async_copy(
                    u_buf.at[g], u_ref.at[pl.ds(g * size, size), :], sem.at[g]
                )
                copy.start()
                copies.append(copy)
            u = u.astype(BF16)
            rounded[g] = u
            out[g] = jnp.dot(u, k_out, preferred_element_type=F32).astype(BF16)
        for copy in copies:
            copy.wait()

    width = mu.shape[1]
    out_shape = [pltpu.VMEM((share, size, width), BF16), plan.blocks(share, BF16)]
    out_specs, scratch = [VMEM] * 2, []
    if final:
        out_shape.append(jax.ShapeDtypeStruct(mu.shape, F32))
        out_specs.append(ANY)
        scratch = [pltpu.VMEM((share, size, width), F32), pltpu.SemaphoreType.DMA((share,))]
    return call(
        kernel,
        out_shape,
        [VMEM] * (states + 2),
        [*pieces, state_kernel, mu],
        plan.cost(share * states * (states + 1), 4 << 20),
        scratch,
        out_specs=out_specs,
    )


def mix_back(plan, p, rounded, state_kernel):
    def kernel(u_ref, k_ref, out):
        k_out = turned(plan, k_ref, p)
        for g in range(plan.share):
            out[g] = jnp.dot(u_ref[g], k_out, preferred_element_type=F32).astype(BF16)

    return call(
        kernel,
        [plan.blocks(plan.share, BF16)],
        [VMEM] * 2,
        [rounded, state_kernel],
        plan.cost(plan.share * plan.states, 1 << 20),
    )[0]


def backward(plan, p, sources, kern, piece, so_far, last):
    share, degree, near, rows = plan.share, plan.degree, plan.near, plan.rows
    n_acc = 0 if so_far is None else 1

    def kernel(src, kern_ref, b_ref, *rest):
        rest = rest[n_acc:]
        acc = rest[-1]
        if not n_acc:
            acc[...] = jnp.zeros_like(acc)
        first = plan.rows_of(p)
        for g in range(share):
            row = first + g
            b = b_ref[g]
            for k in range(degree):
                part = lax.dot_general(
                    kern_ref[g, k], b, (((0,), (0,)), ((), ())), preferred_element_type=F32
                )
                acc[src[row, k]] += part
        if not last:
            return
        own, left, right, far = rest[0], rest[1], rest[2], rest[3:-1]
        for t in range(near):
            left[t] = acc[t].astype(BF16)
            right[t] = acc[near + rows + t].astype(BF16)
        for slot, i, t in plan.far_slots(1):
            far[i][t] = acc[plan.far_base + slot].astype(BF16)
        for t in range(rows):
            own[t] = acc[near + t].astype(BF16)

    out_shape = []
    if last:
        out_shape = [plan.blocks(n, BF16) for n in (rows, near, near)] + plan.far_blocks()
    return call(
        kernel,
        out_shape + [plan.blocks(plan.table, F32)],
        [INDEX] + [VMEM] * (2 + n_acc),
        [sources, kern, piece] + ([] if so_far is None else [so_far]),
        plan.cost(share * degree, 5 << 20),
        (),
        {3: len(out_shape)} if n_acc else {},
    )


def first_far(plan, asked, own):
    def kernel(own_ref, *rest):
        asked_refs, outs = rest[: len(asked)], rest[len(asked) :]
        for _, i, t in plan.far_slots(1):
            outs[i][t] = own_ref[asked_refs[i][t]]

    return call(
        kernel,
        plan.far_blocks(),
        [VMEM] + [SMEM] * len(asked),
        [own, *asked],
        plan.cost(0, 2 << 20),
    )


def divide(plan, asked, own, from_right, from_left, arrived, nu, final):
    near, rows, n_far = plan.near, plan.rows, len(arrived)

    def kernel(own_ref, right_ref, left_ref, nu_ref, *rest):
        far_refs, asked_refs, outs, acc = (
            rest[:n_far],
            rest[n_far : 2 * n_far],
            rest[2 * n_far : -1],
            rest[-1],
        )
        for t in range(rows):
            value = own_ref[t].astype(F32)
            if t < near:
                value = value + left_ref[t].astype(F32)
            if t >= rows - near:
                value = value + right_ref[t - rows + near].astype(F32)
            acc[t] = value
        for _, i, t in plan.far_slots(-1):
            acc[asked_refs[n_far - 1 - i][t]] += far_refs[i][t].astype(F32)
        for t in range(rows):
            value = nu_ref[t] / acc[t]
            if final:
                outs[0][t] = value
            else:
                value = value.astype(BF16)
                outs[0][t] = value
                if t < near:
                    outs[1][t] = value
                if t >= rows - near:
                    outs[2][t - rows + near] = value
        if not final:
            for _, i, t in plan.far_slots(1):
                outs[3 + i][t] = outs[0][asked_refs[i][t]]

    if final:
        out_shape = [jax.ShapeDtypeStruct((rows, plan.size, plan.cols), F32)]
    else:
        out_shape = [plan.blocks(n, BF16) for n in (rows, near, near)] + plan.far_blocks()
    return call(
        kernel,
        out_shape,
        [VMEM] * (4 + n_far) + [SMEM] * n_far,
        [own, from_right, from_left, nu, *arrived, *asked],
        plan.cost(0, 6 << 20),
        [pltpu.VMEM((rows, plan.size, plan.cols), F32)],
    )


def send_far(plan, pieces):
    if plan.shifts is None:
        return [swapped(pieces[0], "mesh")]
    out = []
    for d, piece in zip(plan.shifts, pieces):
        out.append(shifted(piece, "mesh", d))
    return out


def send_asks(plan, asks):
    if plan.shifts is None:
        pairs = asks[0].reshape(plan.peers, plan.far)
        return [swapped(pairs, "mesh").reshape(-1)]
    return send_far(plan, asks)[::-1]


def send_near(to_left, to_right):
    from_left = shifted(to_right, "mesh", 1)
    from_right = shifted(to_left, "mesh", -1)
    return from_left, from_right


def sweep_once(plan, state, sources, asked, kern, kept, state_kernel, mu, nu, first_time, final):
    own, head, tail, far = state
    from_left, from_right = send_near(head, tail)
    far = send_far(plan, far)
    inputs, table = [own, from_left, from_right, *far], None
    pieces = [None] * plan.states
    for p in [*plan.order, 0]:
        part, table, kept[p] = forward(
            plan, p, sources, kern if first_time else kept[p], inputs, table, first_time
        )
        pieces[p] = shifted(part, "state", -p) if p else part
    out = mix(plan, pieces, state_kernel, mu, plan.order[0], final)
    rounded, part, potential_u = out[0], out[1], out[-1]
    pieces = [None] * plan.states
    for p in [*plan.order, 0]:
        if p != plan.order[0]:
            part = mix_back(plan, p, rounded, state_kernel)
        pieces[p] = shifted(part, "state", p) if p else part
    total = None
    for p in [0, *plan.order]:
        out = backward(
            plan, p, sources, kept[p], pieces[p], total, p == plan.order[-1]
        )
        total = out[-1]
    own_part, to_left, to_right, to_far = out[0], out[1], out[2], out[3:-1]
    from_left, from_right = send_near(to_left, to_right)
    arrived = send_far(plan, to_far)
    out = divide(plan, asked, own_part, from_right, from_left, arrived, nu, final)
    return potential_u, out


def per_device(kern_blocks, kern_cols, state_kernel, start_v, mu, nu):
    plan = Plan(kern_blocks, start_v)
    shape = (plan.rows, plan.size, plan.cols)
    nu = nu.reshape(shape)
    kept = [None] * plan.states
    for sweep in range(ITERS):
        if sweep == 0:
            sources, asks, (own, head, tail) = begin(plan, kern_cols, start_v.reshape(shape))
            asked = send_asks(plan, asks)
            state = (own, head, tail, first_far(plan, asked, own))
        potential_u, out = sweep_once(
            plan,
            state,
            sources,
            asked,
            kern_blocks,
            kept,
            state_kernel,
            mu,
            nu,
            sweep == 0,
            sweep == ITERS - 1,
        )
        state = (out[0], *out[1:3], out[3:])
    return (potential_u, out[0].reshape(start_v.shape))


def solution(mesh):
    placed = (
        P("mesh", None, None, None),
        P("mesh", None),
        P(),
        P("mesh", "state"),
        P(("mesh", "state"), None),
        P("mesh", "state"),
    )
    return jax.shard_map(
        per_device,
        mesh=mesh,
        in_specs=placed,
        out_specs=(P(("mesh", "state"), None), P("mesh", "state")),
        check_vma=False,
    )
```

profile of v0, /device:TPU:0, one launch (start us, length us, event | category | flops | bytes accessed | tf_op | source)
XLA Modules:
  0.0 178.2 jit_solution(16268351102712098519)
XLA Ops:
  1.4 1.4 copy-done.5
  2.8 1.7 shard_map.77
  5.1 2.9 %collective-permute-start.1 = (bf16[6,128,128]{2,1,0:T(8,128)(2,1)S(1)}, bf16[6,128,128]{2,1,0:T(8,128)(2,1)S(1)}, u32[]{:S(2)}, u32[]{:S(2)}) collective-permute-start(bf16[6,128,128]{2,1,0:T(8,128)(2,1)S(1)} %get-tuple-element.59), channel_id=1, source_target_pairs={{0,28},{4,0},{8,4},{12,8},{16,12},{20,16},{24,20},{28,24},{1,29},{... | collective-permute-start | bytes 589832 | tf_op jit(solution)/shard_map/ppermute | solution.py:32
  8.0 2.2 %collective-permute-start.2 = (s32[2]{0:T(128)S(1)}, s32[2]{0:T(128)S(1)}, u32[]{:S(2)}, u32[]{:S(2)}) collective-permute-start(s32[2]{0:T(128)S(1)} %get-tuple-element.60), channel_id=1, source_target_pairs={{0,24},{4,28},{8,0},{12,4},{16,8},{20,12},{24,16},{28,20},{1,25},{... | collective-permute-start | bytes 32 | tf_op jit(solution)/shard_map/ppermute | solution.py:32
  10.8 3.5 %collective-permute-done.2.rest_0_.rest_5_ = s32[2]{0:T(128)S(1)} collective-permute-done((s32[2]{0:T(128)S(1)}, s32[2]{0:T(128)S(1)}, u32[]{:S(2)}, u32[]{:S(2)}) %collective-permute-start.2) | collective-permute-done | bytes 40 | tf_op jit(solution)/shard_map/ppermute | solution.py:32
  14.2 1.5 collective-permute-start.6
  15.7 1.5 collective-permute-done.5.rest_3_.rest_8_
  17.2 1.5 collective-permute-done.6.rest_4_.rest_9_
  20.0 1.2 collective-permute-start.8
  21.5 3.2 %collective-permute-done.7.rest_3_ = bf16[2,128,128]{2,1,0:T(8,128)(2,1)S(1)} collective-permute-done((bf16[2,128,128]{2,1,0:T(8,128)(2,1)S(1)}, bf16[2,128,128]{2,1,0:T(8,128)(2,1)S(1)}, u32[]{:S(2)}, u32[]{:S(2)}) %collective-permute-start.7) | collective-permute-done | bytes 65568 | tf_op jit(solution)/shard_map/ppermute | solution.py:32
  24.7 1.4 collective-permute-start.11
  26.5 2.0 %collective-permute-done.10.rest_6_ = bf16[2,128,128]{2,1,0:T(8,128)(2,1)S(1)} collective-permute-done((bf16[2,128,128]{2,1,0:T(8,128)(2,1)S(1)}, bf16[2,128,128]{2,1,0:T(8,128)(2,1)S(1)}, u32[]{:S(2)}, u32[]{:S(2)}) %collective-permute-start.10) | collective-permute-done | bytes 65568 | tf_op jit(solution)/shard_map/ppermute | solution.py:32
  28.4 1.2 collective-permute-done.11.rest_7_
  29.6 4.6 %copy-done = bf16[24,16,128,128]{3,2,1,0:T(8,128)(2,1)S(1)} copy-done((bf16[24,16,128,128]{3,2,1,0:T(8,128)(2,1)S(1)}, bf16[24,16,128,128]{3,2,1,0:T(8,128)(2,1)}, u32[]{:S(2)}) %copy-start) | copy-done | bytes 12582936
  34.2 2.1 %shard_map.79 = (bf16[6,128,128]{2,1,0:T(8,128)(2,1)S(1)}, bf16[52,128,128]{2,1,0:T(8,128)(2,1)S(1)}, bf16[6,16,128,128]{3,2,1,0:T(8,128)(2,1)S(1)}) custom-call(s32[24,16]{1,0:T(8,128)S(4)} %get-tuple-element.56.src, bf16[24,16,128,128]{3,2,1,0:T(8,128)(2,1)S(1)} %copy-done, bf16[24,128,128]{2,1,0:T(8,128)(2,1)S(1)} %get-tuple-element.57.own_ref.rest_0_, ...), custom_call_target="tpu_custom_call" | custom-call | flops 402653184 | bytes 4194304 | tf_op jit(solution)/shard_map/pallas_call | solution.py:80
  36.3 2.4 %copy-done.1 = bf16[24,16,128,128]{3,2,1,0:T(8,128)(2,1)S(1)} copy-done((bf16[24,16,128,128]{3,2,1,0:T(8,128)(2,1)S(1)}, bf16[24,16,128,128]{3,2,1,0:T(8,128)(2,1)}, u32[]{:S(2)}) %copy-start.1) | copy-done | bytes 12582936
  38.8 2.0 %shard_map.82 = (bf16[6,128,128]{2,1,0:T(8,128)(2,1)S(1)}, bf16[6,16,128,128]{3,2,1,0:T(8,128)(2,1)S(1)}) custom-call(s32[24,16]{1,0:T(8,128)S(4)} %get-tuple-element.56.src, bf16[24,16,128,128]{3,2,1,0:T(8,128)(2,1)S(1)} %copy-done.1, bf16[52,128,128]{2,1,0:T(8,128)(2,1)S(1)} %get-tuple-element.70.rest_0_), custom_call_target="tpu_custom_call" | custom-call | flops 402653184 | bytes 4194304 | tf_op jit(solution)/shard_map/pallas_call | solution.py:80
  40.8 2.0 %shard_map.81 = (bf16[6,128,128]{2,1,0:T(8,128)(2,1)S(1)}, bf16[6,16,128,128]{3,2,1,0:T(8,128)(2,1)S(1)}) custom-call(s32[24,16]{1,0:T(8,128)S(4)} %get-tuple-element.56.src, bf16[24,16,128,128]{3,2,1,0:T(8,128)(2,1)S(1)} %copy-done.1, bf16[52,128,128]{2,1,0:T(8,128)(2,1)S(1)} %get-tuple-element.70.rest_0_), custom_call_target="tpu_custom_call" | custom-call | flops 402653184 | bytes 4194304 | tf_op jit(solution)/shard_map/pallas_call | solution.py:80
  42.9 2.6 %collective-permute-start.13 = (bf16[6,128,128]{2,1,0:T(8,128)(2,1)S(1)}, bf16[6,128,128]{2,1,0:T(8,128)(2,1)S(1)}, u32[]{:S(2)}, u32[]{:S(2)}) collective-permute-start(bf16[6,128,128]{2,1,0:T(8,128)(2,1)S(1)} %get-tuple-element.76), channel_id=1, source_target_pairs={{0,2},{1,3},{2,0},{3,1},{4,6},{5,7},{6,4},{7,5},{8,10},{9,11},{10,... | collective-permute-start | bytes 589832 | tf_op jit(solution)/shard_map/ppermute | solution.py:32
  45.5 1.3 collective-permute-start.12
  47.5 2.0 %shard_map.80 = (bf16[6,128,128]{2,1,0:T(8,128)(2,1)S(1)}, bf16[6,16,128,128]{3,2,1,0:T(8,128)(2,1)S(1)}) custom-call(s32[24,16]{1,0:T(8,128)S(4)} %get-tuple-element.56.src, bf16[24,16,128,128]{3,2,1,0:T(8,128)(2,1)S(1)} %copy-done.1, bf16[52,128,128]{2,1,0:T(8,128)(2,1)S(1)} %get-tuple-element.70.rest_0_), custom_call_target="tpu_custom_call" | custom-call | flops 402653184 | bytes 4194304 | tf_op jit(solution)/shard_map/pallas_call | solution.py:80
  49.6 7.0 %collective-permute-done.13.refs_2_ = bf16[6,128,128]{2,1,0:T(8,128)(2,1)S(1)} collective-permute-done((bf16[6,128,128]{2,1,0:T(8,128)(2,1)S(1)}, bf16[6,128,128]{2,1,0:T(8,128)(2,1)S(1)}, u32[]{:S(2)}, u32[]{:S(2)}) %collective-permute-start.13) | collective-permute-done | bytes 196640 | tf_op jit(solution)/shard_map/ppermute | solution.py:32
  56.6 3.8 %collective-permute-done.14.refs_3_ = bf16[6,128,128]{2,1,0:T(8,128)(2,1)S(1)} collective-permute-done((bf16[6,128,128]{2,1,0:T(8,128)(2,1)S(1)}, bf16[6,128,128]{2,1,0:T(8,128)(2,1)S(1)}, u32[]{:S(2)}, u32[]{:S(2)}) %collective-permute-start.14) | collective-permute-done | bytes 196640 | tf_op jit(solution)/shard_map/ppermute | solution.py:32
  60.3 2.0 %shard_map.83 = (bf16[6,128,512]{2,1,0:T(8,128)(2,1)S(1)}, bf16[6,128,128]{2,1,0:T(8,128)(2,1)S(1)}) custom-call(bf16[6,128,128]{2,1,0:T(8,128)(2,1)S(1)} %get-tuple-element.74.refs_0_, bf16[6,128,128]{2,1,0:T(8,128)(2,1)S(1)} %collective-permute-done.12.refs_1_, bf16[6,128,128]{2,1,0:T(8,128)(2,1)S(1)} %collective-permute-done.13.refs_2_, ...), custom_call_target="tpu_custom_call" | custom-call | flops 503316480 | bytes 4194304 | tf_op jit(solution)/shard_map/pallas_call | solution.py:80
  62.3 5.8 %collective-permute-start.17 = (bf16[6,128,128]{2,1,0:T(8,128)(2,1)S(1)}, bf16[6,128,128]{2,1,0:T(8,128)(2,1)S(1)}, u32[]{:S(2)}, u32[]{:S(2)}) collective-permute-start(bf16[6,128,128]{2,1,0:T(8,128)(2,1)S(1)} %get-tuple-element.80), channel_id=1, source_target_pairs={{0,2},{1,3},{2,0},{3,1},{4,6},{5,7},{6,4},{7,5},{8,10},{9,11},{10,... | collective-permute-start | bytes 589832 | tf_op jit(solution)/shard_map/ppermute | solution.py:32
  68.9 4.0 %collective-permute-start.15 = (bf16[6,128,128]{2,1,0:T(8,128)(2,1)S(1)}, bf16[6,128,128]{2,1,0:T(8,128)(2,1)S(1)}, u32[]{:S(2)}, u32[]{:S(2)}) collective-permute-start(bf16[6,128,128]{2,1,0:T(8,128)(2,1)S(1)} %shard_map.84), channel_id=1, source_target_pairs={{0,3},{1,0},{2,1},{3,2},{4,7},{5,4},{6,5},{7,6},{8,11},{9,8},{10,9... | collective-permute-start | bytes 589832 | tf_op jit(solution)/shard_map/ppermute | solution.py:32
  73.3 1.2 shard_map.87.rest_0_
  74.6 7.3 %collective-permute-done.17.b_ref = bf16[6,128,128]{2,1,0:T(8,128)(2,1)S(1)} collective-permute-done((bf16[6,128,128]{2,1,0:T(8,128)(2,1)S(1)}, bf16[6,128,128]{2,1,0:T(8,128)(2,1)S(1)}, u32[]{:S(2)}, u32[]{:S(2)}) %collective-permute-start.17) | collective-permute-done | bytes 196640 | tf_op jit(solution)/shard_map/ppermute | solution.py:32
  81.9 1.1 shard_map.88.rest_0_
  83.0 1.1 shard_map.89.rest_0_
  84.1 1.2 shard_map.90
  85.4 1.4 collective-permute-start.18
  87.1 1.9 %collective-permute-start.21 = (bf16[2,128,128]{2,1,0:T(8,128)(2,1)S(1)}, bf16[2,128,128]{2,1,0:T(8,128)(2,1)S(1)}, u32[]{:S(2)}, u32[]{:S(2)}) collective-permute-start(bf16[2,128,128]{2,1,0:T(8,128)(2,1)S(1)} %get-tuple-element.85), channel_id=1, source_target_pairs={{0,12},{4,16},{8,20},{12,24},{16,28},{20,0},{24,4},{28,8},{1,13},{... | collective-permute-start | bytes 196616 | tf_op jit(solution)/shard_map/ppermute | solution.py:32
  89.9 3.2 %collective-permute-done.20.rest_0_ = bf16[2,128,128]{2,1,0:T(8,128)(2,1)S(1)} collective-permute-done((bf16[2,128,128]{2,1,0:T(8,128)(2,1)S(1)}, bf16[2,128,128]{2,1,0:T(8,128)(2,1)S(1)}, u32[]{:S(2)}, u32[]{:S(2)}) %collective-permute-start.20) | collective-permute-done | bytes 65568 | tf_op jit(solution)/shard_map/ppermute | solution.py:32
  93.2 2.4 %collective-permute-start.23 = (bf16[2,128,128]{2,1,0:T(8,128)(2,1)S(1)}, bf16[2,128,128]{2,1,0:T(8,128)(2,1)S(1)}, u32[]{:S(2)}, u32[]{:S(2)}) collective-permute-start(bf16[2,128,128]{2,1,0:T(8,128)(2,1)S(1)} %get-tuple-element.87), channel_id=1, source_target_pairs={{0,20},{4,24},{8,28},{12,0},{16,4},{20,8},{24,12},{28,16},{1,21},{... | collective-permute-start | bytes 196616 | tf_op jit(solution)/shard_map/ppermute | solution.py:32
  97.4 2.7 %collective-permute-done.24.rest_4_ = bf16[2,128,128]{2,1,0:T(8,128)(2,1)S(1)} collective-permute-done((bf16[2,128,128]{2,1,0:T(8,128)(2,1)S(1)}, bf16[2,128,128]{2,1,0:T(8,128)(2,1)S(1)}, u32[]{:S(2)}, u32[]{:S(2)}) %collective-permute-start.24) | collective-permute-done | bytes 65568 | tf_op jit(solution)/shard_map/ppermute | solution.py:32
  100.2 1.0 shard_map.91
  101.3 2.6 %collective-permute-start.26 = (bf16[6,128,128]{2,1,0:T(8,128)(2,1)S(1)}, bf16[6,128,128]{2,1,0:T(8,128)(2,1)S(1)}, u32[]{:S(2)}, u32[]{:S(2)}) collective-permute-start(bf16[6,128,128]{2,1,0:T(8,128)(2,1)S(1)} %get-tuple-element.91), channel_id=1, source_target_pairs={{0,28},{4,0},{8,4},{12,8},{16,12},{20,16},{24,20},{28,24},{1,29},{... | collective-permute-start | bytes 589832 | tf_op jit(solution)/shard_map/ppermute | solution.py:32
  104.4 1.2 collective-permute-start.29
  105.6 5.3 %collective-permute-done.27.rest_3_ = bf16[2,128,128]{2,1,0:T(8,128)(2,1)S(1)} collective-permute-done((bf16[2,128,128]{2,1,0:T(8,128)(2,1)S(1)}, bf16[2,128,128]{2,1,0:T(8,128)(2,1)S(1)}, u32[]{:S(2)}, u32[]{:S(2)}) %collective-permute-start.27) | collective-permute-done | bytes 65568 | tf_op jit(solution)/shard_map/ppermute | solution.py:32
  110.9 1.4 collective-permute-start.31
  112.3 2.4 %collective-permute-done.30.rest_6_ = bf16[2,128,128]{2,1,0:T(8,128)(2,1)S(1)} collective-permute-done((bf16[2,128,128]{2,1,0:T(8,128)(2,1)S(1)}, bf16[2,128,128]{2,1,0:T(8,128)(2,1)S(1)}, u32[]{:S(2)}, u32[]{:S(2)}) %collective-permute-start.30) | collective-permute-done | bytes 65568 | tf_op jit(solution)/shard_map/ppermute | solution.py:32
  114.7 1.2 collective-permute-done.31.rest_7_
  115.8 1.1 shard_map.92
  116.9 1.0 shard_map.95
  117.9 1.0 shard_map.94
  119.7 2.3 %collective-permute-start.34 = (bf16[6,128,128]{2,1,0:T(8,128)(2,1)S(1)}, bf16[6,128,128]{2,1,0:T(8,128)(2,1)S(1)}, u32[]{:S(2)}, u32[]{:S(2)}) collective-permute-start(bf16[6,128,128]{2,1,0:T(8,128)(2,1)S(1)} %shard_map.95), channel_id=1, source_target_pairs={{0,1},{1,2},{2,3},{3,0},{4,5},{5,6},{6,7},{7,4},{8,9},{9,10},{10,1... | collective-permute-start | bytes 589832 | tf_op jit(solution)/shard_map/ppermute | solution.py:32
  122.0 1.2 collective-permute-start.33
  124.2 3.2 %collective-permute-done.32.refs_1_ = bf16[6,128,128]{2,1,0:T(8,128)(2,1)S(1)} collective-permute-done((bf16[6,128,128]{2,1,0:T(8,128)(2,1)S(1)}, bf16[6,128,128]{2,1,0:T(8,128)(2,1)S(1)}, u32[]{:S(2)}, u32[]{:S(2)}) %collective-permute-start.32) | collective-permute-done | bytes 196640 | tf_op jit(solution)/shard_map/ppermute | solution.py:32
  127.4 5.0 %collective-permute-done.34.refs_3_ = bf16[6,128,128]{2,1,0:T(8,128)(2,1)S(1)} collective-permute-done((bf16[6,128,128]{2,1,0:T(8,128)(2,1)S(1)}, bf16[6,128,128]{2,1,0:T(8,128)(2,1)S(1)}, u32[]{:S(2)}, u32[]{:S(2)}) %collective-permute-start.34) | collective-permute-done | bytes 196640 | tf_op jit(solution)/shard_map/ppermute | solution.py:32
  132.4 8.3 %collective-permute-done.33.refs_2_ = bf16[6,128,128]{2,1,0:T(8,128)(2,1)S(1)} collective-permute-done((bf16[6,128,128]{2,1,0:T(8,128)(2,1)S(1)}, bf16[6,128,128]{2,1,0:T(8,128)(2,1)S(1)}, u32[]{:S(2)}, u32[]{:S(2)}) %collective-permute-start.33) | collective-permute-done | bytes 196640 | tf_op jit(solution)/shard_map/ppermute | solution.py:32
  140.7 2.6 %shard_map.96 = (bf16[6,128,512]{2,1,0:T(8,128)(2,1)S(1)}, bf16[6,128,128]{2,1,0:T(8,128)(2,1)S(1)}, f32[768,512]{1,0:T(8,128)}) custom-call(bf16[6,128,128]{2,1,0:T(8,128)(2,1)S(1)} %shard_map.93.refs_0_, bf16[6,128,128]{2,1,0:T(8,128)(2,1)S(1)} %collective-permute-done.32.refs_1_, bf16[6,128,128]{2,1,0:T(8,128)(2,1)S(1)} %collective-permute-done.33.refs_2_, ...), custom_call_target="tpu_custom_call" | custom-call | flops 503316480 | bytes 4194304 | tf_op jit(solution)/shard_map/pallas_call | solution.py:80
  145.1 3.0 %collective-permute-start.35 = (bf16[6,128,128]{2,1,0:T(8,128)(2,1)S(1)}, bf16[6,128,128]{2,1,0:T(8,128)(2,1)S(1)}, u32[]{:S(2)}, u32[]{:S(2)}) collective-permute-start(bf16[6,128,128]{2,1,0:T(8,128)(2,1)S(1)} %shard_map.97), channel_id=1, source_target_pairs={{0,3},{1,0},{2,1},{3,2},{4,7},{5,4},{6,5},{7,6},{8,11},{9,8},{10,9... | collective-permute-start | bytes 589832 | tf_op jit(solution)/shard_map/ppermute | solution.py:32
  148.5 1.2 shard_map.100.rest_0_
  149.7 7.7 %collective-permute-done.37.b_ref = bf16[6,128,128]{2,1,0:T(8,128)(2,1)S(1)} collective-permute-done((bf16[6,128,128]{2,1,0:T(8,128)(2,1)S(1)}, bf16[6,128,128]{2,1,0:T(8,128)(2,1)S(1)}, u32[]{:S(2)}, u32[]{:S(2)}) %collective-permute-start.37) | collective-permute-done | bytes 196640 | tf_op jit(solution)/shard_map/ppermute | solution.py:32
  157.4 1.1 shard_map.101.rest_0_
  158.5 1.1 shard_map.102.rest_0_
  159.8 1.2 shard_map.103
  161.1 1.4 collective-permute-start.38
  163.3 1.5 collective-permute-start.41
  165.8 3.3 %collective-permute-done.40.rest_0_ = bf16[2,128,128]{2,1,0:T(8,128)(2,1)S(1)} collective-permute-done((bf16[2,128,128]{2,1,0:T(8,128)(2,1)S(1)}, bf16[2,128,128]{2,1,0:T(8,128)(2,1)S(1)}, u32[]{:S(2)}, u32[]{:S(2)}) %collective-permute-start.40) | collective-permute-done | bytes 65568 | tf_op jit(solution)/shard_map/ppermute | solution.py:32
  169.1 2.5 %collective-permute-start.43 = (bf16[2,128,128]{2,1,0:T(8,128)(2,1)S(1)}, bf16[2,128,128]{2,1,0:T(8,128)(2,1)S(1)}, u32[]{:S(2)}, u32[]{:S(2)}) collective-permute-start(bf16[2,128,128]{2,1,0:T(8,128)(2,1)S(1)} %get-tuple-element.108), channel_id=1, source_target_pairs={{0,20},{4,24},{8,28},{12,0},{16,4},{20,8},{24,12},{28,16},{1,21},{... | collective-permute-start | bytes 196616 | tf_op jit(solution)/shard_map/ppermute | solution.py:32
  173.6 2.5 %collective-permute-done.44.rest_4_ = bf16[2,128,128]{2,1,0:T(8,128)(2,1)S(1)} collective-permute-done((bf16[2,128,128]{2,1,0:T(8,128)(2,1)S(1)}, bf16[2,128,128]{2,1,0:T(8,128)(2,1)S(1)}, u32[]{:S(2)}, u32[]{:S(2)}) %collective-permute-start.44) | collective-permute-done | bytes 65568 | tf_op jit(solution)/shard_map/ppermute | solution.py:32
  176.1 2.1 %shard_map.104 = f32[24,128,128]{2,1,0:T(8,128)} custom-call(bf16[24,128,128]{2,1,0:T(8,128)(2,1)S(1)} %get-tuple-element.102.own_ref, bf16[6,128,128]{2,1,0:T(8,128)(2,1)S(1)} %collective-permute-done.38.right_ref, bf16[6,128,128]{2,1,0:T(8,128)(2,1)S(1)} %collective-permute-done.39.left_ref, f32[24,128,128]{2,1,0:T(8,128)S(1)} %bitcast.4, ...), custom_call_target="tpu_custom_call" | custom-call | bytes 6291456 | tf_op jit(solution)/shard_map/pallas_call | solution.py:80
  (67 shorter events, 17.3 us)
Async XLA Ops:
  1.4 1.4 copy-start.5
  4.5 25.1 %collective-permute-start = (bf16[6,128,128]{2,1,0:T(8,128)(2,1)S(1)}, bf16[6,128,128]{2,1,0:T(8,128)(2,1)S(1)}, u32[]{:S(2)}, u32[]{:S(2)}) collective-permute-start(bf16[6,128,128]{2,1,0:T(8,128)(2,1)S(1)} %get-tuple-element.58), channel_id=1, source_target_pairs={{0,4},{4,8},{8,12},{12,16},{16,20},{20,24},{24,28},{28,0},{1,5},{5... | collective-permute-start | bytes 589832 | tf_op jit(solution)/shard_map/ppermute | solution.py:32
  5.1 24.6 %collective-permute-start.1 = (bf16[6,128,128]{2,1,0:T(8,128)(2,1)S(1)}, bf16[6,128,128]{2,1,0:T(8,128)(2,1)S(1)}, u32[]{:S(2)}, u32[]{:S(2)}) collective-permute-start(bf16[6,128,128]{2,1,0:T(8,128)(2,1)S(1)} %get-tuple-element.59), channel_id=1, source_target_pairs={{0,28},{4,0},{8,4},{12,8},{16,12},{20,16},{24,20},{28,24},{1,29},{... | collective-permute-start | bytes 589832 | tf_op jit(solution)/shard_map/ppermute | solution.py:32
  8.0 6.2 %collective-permute-start.2 = (s32[2]{0:T(128)S(1)}, s32[2]{0:T(128)S(1)}, u32[]{:S(2)}, u32[]{:S(2)}) collective-permute-start(s32[2]{0:T(128)S(1)} %get-tuple-element.60), channel_id=1, source_target_pairs={{0,24},{4,28},{8,0},{12,4},{16,8},{20,12},{24,16},{28,20},{1,25},{... | collective-permute-start | bytes 32 | tf_op jit(solution)/shard_map/ppermute | solution.py:32
  10.2 4.0 %collective-permute-start.3 = (s32[2]{0:T(128)S(1)}, s32[2]{0:T(128)S(1)}, u32[]{:S(2)}, u32[]{:S(2)}) collective-permute-start(s32[2]{0:T(128)S(1)} %get-tuple-element.61), channel_id=1, source_target_pairs={{0,20},{4,24},{8,28},{12,0},{16,4},{20,8},{24,12},{28,16},{1,21},{... | collective-permute-start | bytes 32 | tf_op jit(solution)/shard_map/ppermute | solution.py:32
  10.3 5.5 %collective-permute-start.4 = (s32[2]{0:T(128)S(1)}, s32[2]{0:T(128)S(1)}, u32[]{:S(2)}, u32[]{:S(2)}) collective-permute-start(s32[2]{0:T(128)S(1)} %get-tuple-element.62), channel_id=1, source_target_pairs={{0,16},{4,20},{8,24},{12,28},{16,0},{20,4},{24,8},{28,12},{1,17},{... | collective-permute-start | bytes 32 | tf_op jit(solution)/shard_map/ppermute | solution.py:32
  14.2 3.0 %collective-permute-start.5 = (s32[2]{0:T(128)S(1)}, s32[2]{0:T(128)S(1)}, u32[]{:S(2)}, u32[]{:S(2)}) collective-permute-start(s32[2]{0:T(128)S(1)} %get-tuple-element.63), channel_id=1, source_target_pairs={{0,12},{4,16},{8,20},{12,24},{16,28},{20,0},{24,4},{28,8},{1,13},{... | collective-permute-start | bytes 32 | tf_op jit(solution)/shard_map/ppermute | solution.py:32
  14.2 4.5 %collective-permute-start.6 = (s32[2]{0:T(128)S(1)}, s32[2]{0:T(128)S(1)}, u32[]{:S(2)}, u32[]{:S(2)}) collective-permute-start(s32[2]{0:T(128)S(1)} %get-tuple-element.64), channel_id=1, source_target_pairs={{0,8},{4,12},{8,16},{12,20},{16,24},{20,28},{24,0},{28,4},{1,9},{5... | collective-permute-start | bytes 32 | tf_op jit(solution)/shard_map/ppermute | solution.py:32
  19.3 5.3 %collective-permute-start.7 = (bf16[2,128,128]{2,1,0:T(8,128)(2,1)S(1)}, bf16[2,128,128]{2,1,0:T(8,128)(2,1)S(1)}, u32[]{:S(2)}, u32[]{:S(2)}) collective-permute-start(bf16[2,128,128]{2,1,0:T(8,128)(2,1)S(1)} %get-tuple-element.65), channel_id=1, source_target_pairs={{0,8},{4,12},{8,16},{12,20},{16,24},{20,28},{24,0},{28,4},{1,9},{5... | collective-permute-start | bytes 196616 | tf_op jit(solution)/shard_map/ppermute | solution.py:32
  20.0 4.7 %collective-permute-start.8 = (bf16[2,128,128]{2,1,0:T(8,128)(2,1)S(1)}, bf16[2,128,128]{2,1,0:T(8,128)(2,1)S(1)}, u32[]{:S(2)}, u32[]{:S(2)}) collective-permute-start(bf16[2,128,128]{2,1,0:T(8,128)(2,1)S(1)} %get-tuple-element.66), channel_id=1, source_target_pairs={{0,12},{4,16},{8,20},{12,24},{16,28},{20,0},{24,4},{28,8},{1,13},{... | collective-permute-start | bytes 196616 | tf_op jit(solution)/shard_map/ppermute | solution.py:32
  21.1 5.3 %collective-permute-start.9 = (bf16[2,128,128]{2,1,0:T(8,128)(2,1)S(1)}, bf16[2,128,128]{2,1,0:T(8,128)(2,1)S(1)}, u32[]{:S(2)}, u32[]{:S(2)}) collective-permute-start(bf16[2,128,128]{2,1,0:T(8,128)(2,1)S(1)} %get-tuple-element.67), channel_id=1, source_target_pairs={{0,16},{4,20},{8,24},{12,28},{16,0},{20,4},{24,8},{28,12},{1,17},{... | collective-permute-start | bytes 196616 | tf_op jit(solution)/shard_map/ppermute | solution.py:32
  24.6 3.8 %collective-permute-start.10 = (bf16[2,128,128]{2,1,0:T(8,128)(2,1)S(1)}, bf16[2,128,128]{2,1,0:T(8,128)(2,1)S(1)}, u32[]{:S(2)}, u32[]{:S(2)}) collective-permute-start(bf16[2,128,128]{2,1,0:T(8,128)(2,1)S(1)} %get-tuple-element.68), channel_id=1, source_target_pairs={{0,20},{4,24},{8,28},{12,0},{16,4},{20,8},{24,12},{28,16},{1,21},{... | collective-permute-start | bytes 196616 | tf_op jit(solution)/shard_map/ppermute | solution.py:32
  24.7 5.0 %collective-permute-start.11 = (bf16[2,128,128]{2,1,0:T(8,128)(2,1)S(1)}, bf16[2,128,128]{2,1,0:T(8,128)(2,1)S(1)}, u32[]{:S(2)}, u32[]{:S(2)}) collective-permute-start(bf16[2,128,128]{2,1,0:T(8,128)(2,1)S(1)} %get-tuple-element.69), channel_id=1, source_target_pairs={{0,24},{4,28},{8,0},{12,4},{16,8},{20,12},{24,16},{28,20},{1,25},{... | collective-permute-start | bytes 196616 | tf_op jit(solution)/shard_map/ppermute | solution.py:32
  29.6 4.6 %copy-start = (bf16[24,16,128,128]{3,2,1,0:T(8,128)(2,1)S(1)}, bf16[24,16,128,128]{3,2,1,0:T(8,128)(2,1)}, u32[]{:S(2)}) copy-start(bf16[24,16,128,128]{3,2,1,0:T(8,128)(2,1)} %kern_ref.7) | copy-start | bytes 37748740
  34.2 4.6 %copy-start.1 = (bf16[24,16,128,128]{3,2,1,0:T(8,128)(2,1)S(1)}, bf16[24,16,128,128]{3,2,1,0:T(8,128)(2,1)}, u32[]{:S(2)}) copy-start(bf16[24,16,128,128]{3,2,1,0:T(8,128)(2,1)} %kern_ref.7) | copy-start | bytes 37748740
  42.9 13.7 %collective-permute-start.13 = (bf16[6,128,128]{2,1,0:T(8,128)(2,1)S(1)}, bf16[6,128,128]{2,1,0:T(8,128)(2,1)S(1)}, u32[]{:S(2)}, u32[]{:S(2)}) collective-permute-start(bf16[6,128,128]{2,1,0:T(8,128)(2,1)S(1)} %get-tuple-element.76), channel_id=1, source_target_pairs={{0,2},{1,3},{2,0},{3,1},{4,6},{5,7},{6,4},{7,5},{8,10},{9,11},{10,... | collective-permute-start | bytes 589832 | tf_op jit(solution)/shard_map/ppermute | solution.py:32
  45.5 11.1 %collective-permute-start.12 = (bf16[6,128,128]{2,1,0:T(8,128)(2,1)S(1)}, bf16[6,128,128]{2,1,0:T(8,128)(2,1)S(1)}, u32[]{:S(2)}, u32[]{:S(2)}) collective-permute-start(bf16[6,128,128]{2,1,0:T(8,128)(2,1)S(1)} %get-tuple-element.75), channel_id=1, source_target_pairs={{0,3},{1,0},{2,1},{3,2},{4,7},{5,4},{6,5},{7,6},{8,11},{9,8},{10,9... | collective-permute-start | bytes 589832 | tf_op jit(solution)/shard_map/ppermute | solution.py:32
  46.9 13.5 %copy-start.2 = (bf16[512,512]{1,0:T(8,128)(2,1)S(1)}, bf16[512,512]{1,0:T(8,128)(2,1)}, u32[]{:S(2)}) copy-start(bf16[512,512]{1,0:T(8,128)(2,1)} %k_ref.11) | copy-start | bytes 1572868
  46.9 13.5 %copy-start.4 = (f32[768,512]{1,0:T(8,128)S(1)}, f32[768,512]{1,0:T(8,128)}, u32[]{:S(2)}) copy-start(f32[768,512]{1,0:T(8,128)} %refs_5_.3) | copy-start | bytes 4718596
  46.9 13.5 %collective-permute-start.14 = (bf16[6,128,128]{2,1,0:T(8,128)(2,1)S(1)}, bf16[6,128,128]{2,1,0:T(8,128)(2,1)S(1)}, u32[]{:S(2)}, u32[]{:S(2)}) collective-permute-start(bf16[6,128,128]{2,1,0:T(8,128)(2,1)S(1)} %get-tuple-element.77), channel_id=1, source_target_pairs={{0,1},{1,2},{2,3},{3,0},{4,5},{5,6},{6,7},{7,4},{8,9},{9,10},{10,1... | collective-permute-start | bytes 589832 | tf_op jit(solution)/shard_map/ppermute | solution.py:32
  62.3 19.6 %collective-permute-start.17 = (bf16[6,128,128]{2,1,0:T(8,128)(2,1)S(1)}, bf16[6,128,128]{2,1,0:T(8,128)(2,1)S(1)}, u32[]{:S(2)}, u32[]{:S(2)}) collective-permute-start(bf16[6,128,128]{2,1,0:T(8,128)(2,1)S(1)} %get-tuple-element.80), channel_id=1, source_target_pairs={{0,2},{1,3},{2,0},{3,1},{4,6},{5,7},{6,4},{7,5},{8,10},{9,11},{10,... | collective-permute-start | bytes 589832 | tf_op jit(solution)/shard_map/ppermute | solution.py:32
  68.5 14.5 %collective-permute-start.16 = (bf16[6,128,128]{2,1,0:T(8,128)(2,1)S(1)}, bf16[6,128,128]{2,1,0:T(8,128)(2,1)S(1)}, u32[]{:S(2)}, u32[]{:S(2)}) collective-permute-start(bf16[6,128,128]{2,1,0:T(8,128)(2,1)S(1)} %shard_map.85), channel_id=1, source_target_pairs={{0,1},{1,2},{2,3},{3,0},{4,5},{5,6},{6,7},{7,4},{8,9},{9,10},{10,1... | collective-permute-start | bytes 589832 | tf_op jit(solution)/shard_map/ppermute | solution.py:32
  68.9 15.2 %collective-permute-start.15 = (bf16[6,128,128]{2,1,0:T(8,128)(2,1)S(1)}, bf16[6,128,128]{2,1,0:T(8,128)(2,1)S(1)}, u32[]{:S(2)}, u32[]{:S(2)}) collective-permute-start(bf16[6,128,128]{2,1,0:T(8,128)(2,1)S(1)} %shard_map.84), channel_id=1, source_target_pairs={{0,3},{1,0},{2,1},{3,2},{4,7},{5,4},{6,5},{7,6},{8,11},{9,8},{10,9... | collective-permute-start | bytes 589832 | tf_op jit(solution)/shard_map/ppermute | solution.py:32
  84.1 16.0 %copy-start.3 = (f32[3072,128]{1,0:T(8,128)S(1)}, f32[3072,128]{1,0:T(8,128)}, u32[]{:S(2)}) copy-start(f32[3072,128]{1,0:T(8,128)} %param.11) | copy-start | bytes 4718596
  85.4 14.8 %collective-permute-start.18 = (bf16[6,128,128]{2,1,0:T(8,128)(2,1)S(1)}, bf16[6,128,128]{2,1,0:T(8,128)(2,1)S(1)}, u32[]{:S(2)}, u32[]{:S(2)}) collective-permute-start(bf16[6,128,128]{2,1,0:T(8,128)(2,1)S(1)} %get-tuple-element.82), channel_id=1, source_target_pairs={{0,28},{4,0},{8,4},{12,8},{16,12},{20,16},{24,20},{28,24},{1,29},{... | collective-permute-start | bytes 589832 | tf_op jit(solution)/shard_map/ppermute | solution.py:32
  86.7 13.4 %collective-permute-start.19 = (bf16[6,128,128]{2,1,0:T(8,128)(2,1)S(1)}, bf16[6,128,128]{2,1,0:T(8,128)(2,1)S(1)}, u32[]{:S(2)}, u32[]{:S(2)}) collective-permute-start(bf16[6,128,128]{2,1,0:T(8,128)(2,1)S(1)} %get-tuple-element.83), channel_id=1, source_target_pairs={{0,4},{4,8},{8,12},{12,16},{16,20},{20,24},{24,28},{28,0},{1,5},{5... | collective-permute-start | bytes 589832 | tf_op jit(solution)/shard_map/ppermute | solution.py:32
  86.7 6.4 %collective-permute-start.20 = (bf16[2,128,128]{2,1,0:T(8,128)(2,1)S(1)}, bf16[2,128,128]{2,1,0:T(8,128)(2,1)S(1)}, u32[]{:S(2)}, u32[]{:S(2)}) collective-permute-start(bf16[2,128,128]{2,1,0:T(8,128)(2,1)S(1)} %get-tuple-element.84), channel_id=1, source_target_pairs={{0,8},{4,12},{8,16},{12,20},{16,24},{20,28},{24,0},{28,4},{1,9},{5... | collective-permute-start | bytes 196616 | tf_op jit(solution)/shard_map/ppermute | solution.py:32
  87.1 8.8 %collective-permute-start.21 = (bf16[2,128,128]{2,1,0:T(8,128)(2,1)S(1)}, bf16[2,128,128]{2,1,0:T(8,128)(2,1)S(1)}, u32[]{:S(2)}, u32[]{:S(2)}) collective-permute-start(bf16[2,128,128]{2,1,0:T(8,128)(2,1)S(1)} %get-tuple-element.85), channel_id=1, source_target_pairs={{0,12},{4,16},{8,20},{12,24},{16,28},{20,0},{24,4},{28,8},{1,13},{... | collective-permute-start | bytes 196616 | tf_op jit(solution)/shard_map/ppermute | solution.py:32
  89.0 7.8 %collective-permute-start.22 = (bf16[2,128,128]{2,1,0:T(8,128)(2,1)S(1)}, bf16[2,128,128]{2,1,0:T(8,128)(2,1)S(1)}, u32[]{:S(2)}, u32[]{:S(2)}) collective-permute-start(bf16[2,128,128]{2,1,0:T(8,128)(2,1)S(1)} %get-tuple-element.86), channel_id=1, source_target_pairs={{0,16},{4,20},{8,24},{12,28},{16,0},{20,4},{24,8},{28,12},{1,17},{... | collective-permute-start | bytes 196616 | tf_op jit(solution)/shard_map/ppermute | solution.py:32
  93.2 4.3 %collective-permute-start.23 = (bf16[2,128,128]{2,1,0:T(8,128)(2,1)S(1)}, bf16[2,128,128]{2,1,0:T(8,128)(2,1)S(1)}, u32[]{:S(2)}, u32[]{:S(2)}) collective-permute-start(bf16[2,128,128]{2,1,0:T(8,128)(2,1)S(1)} %get-tuple-element.87), channel_id=1, source_target_pairs={{0,20},{4,24},{8,28},{12,0},{16,4},{20,8},{24,12},{28,16},{1,21},{... | collective-permute-start | bytes 196616 | tf_op jit(solution)/shard_map/ppermute | solution.py:32
  95.9 4.3 %collective-permute-start.24 = (bf16[2,128,128]{2,1,0:T(8,128)(2,1)S(1)}, bf16[2,128,128]{2,1,0:T(8,128)(2,1)S(1)}, u32[]{:S(2)}, u32[]{:S(2)}) collective-permute-start(bf16[2,128,128]{2,1,0:T(8,128)(2,1)S(1)} %get-tuple-element.88), channel_id=1, source_target_pairs={{0,24},{4,28},{8,0},{12,4},{16,8},{20,12},{24,16},{28,20},{1,25},{... | collective-permute-start | bytes 196616 | tf_op jit(solution)/shard_map/ppermute | solution.py:32
  101.2 14.6 %collective-permute-start.25 = (bf16[6,128,128]{2,1,0:T(8,128)(2,1)S(1)}, bf16[6,128,128]{2,1,0:T(8,128)(2,1)S(1)}, u32[]{:S(2)}, u32[]{:S(2)}) collective-permute-start(bf16[6,128,128]{2,1,0:T(8,128)(2,1)S(1)} %get-tuple-element.90), channel_id=1, source_target_pairs={{0,4},{4,8},{8,12},{12,16},{16,20},{20,24},{24,28},{28,0},{1,5},{5... | collective-permute-start | bytes 589832 | tf_op jit(solution)/shard_map/ppermute | solution.py:32
  101.3 14.6 %collective-permute-start.26 = (bf16[6,128,128]{2,1,0:T(8,128)(2,1)S(1)}, bf16[6,128,128]{2,1,0:T(8,128)(2,1)S(1)}, u32[]{:S(2)}, u32[]{:S(2)}) collective-permute-start(bf16[6,128,128]{2,1,0:T(8,128)(2,1)S(1)} %get-tuple-element.91), channel_id=1, source_target_pairs={{0,28},{4,0},{8,4},{12,8},{16,12},{20,16},{24,20},{28,24},{1,29},{... | collective-permute-start | bytes 589832 | tf_op jit(solution)/shard_map/ppermute | solution.py:32
  103.9 7.0 %collective-permute-start.27 = (bf16[2,128,128]{2,1,0:T(8,128)(2,1)S(1)}, bf16[2,128,128]{2,1,0:T(8,128)(2,1)S(1)}, u32[]{:S(2)}, u32[]{:S(2)}) collective-permute-start(bf16[2,128,128]{2,1,0:T(8,128)(2,1)S(1)} %get-tuple-element.92), channel_id=1, source_target_pairs={{0,8},{4,12},{8,16},{12,20},{16,24},{20,28},{24,0},{28,4},{1,9},{5... | collective-permute-start | bytes 196616 | tf_op jit(solution)/shard_map/ppermute | solution.py:32
  104.4 6.4 %collective-permute-start.28 = (bf16[2,128,128]{2,1,0:T(8,128)(2,1)S(1)}, bf16[2,128,128]{2,1,0:T(8,128)(2,1)S(1)}, u32[]{:S(2)}, u32[]{:S(2)}) collective-permute-start(bf16[2,128,128]{2,1,0:T(8,128)(2,1)S(1)} %get-tuple-element.93), channel_id=1, source_target_pairs={{0,12},{4,16},{8,20},{12,24},{16,28},{20,0},{24,4},{28,8},{1,13},{... | collective-permute-start | bytes 196616 | tf_op jit(solution)/shard_map/ppermute | solution.py:32
  104.4 7.9 %collective-permute-start.29 = (bf16[2,128,128]{2,1,0:T(8,128)(2,1)S(1)}, bf16[2,128,128]{2,1,0:T(8,128)(2,1)S(1)}, u32[]{:S(2)}, u32[]{:S(2)}) collective-permute-start(bf16[2,128,128]{2,1,0:T(8,128)(2,1)S(1)} %get-tuple-element.94), channel_id=1, source_target_pairs={{0,16},{4,20},{8,24},{12,28},{16,0},{20,4},{24,8},{28,12},{1,17},{... | collective-permute-start | bytes 196616 | tf_op jit(solution)/shard_map/ppermute | solution.py:32
  110.8 3.8 %collective-permute-start.30 = (bf16[2,128,128]{2,1,0:T(8,128)(2,1)S(1)}, bf16[2,128,128]{2,1,0:T(8,128)(2,1)S(1)}, u32[]{:S(2)}, u32[]{:S(2)}) collective-permute-start(bf16[2,128,128]{2,1,0:T(8,128)(2,1)S(1)} %get-tuple-element.95), channel_id=1, source_target_pairs={{0,20},{4,24},{8,28},{12,0},{16,4},{20,8},{24,12},{28,16},{1,21},{... | collective-permute-start | bytes 196616 | tf_op jit(solution)/shard_map/ppermute | solution.py:32
  110.9 5.0 %collective-permute-start.31 = (bf16[2,128,128]{2,1,0:T(8,128)(2,1)S(1)}, bf16[2,128,128]{2,1,0:T(8,128)(2,1)S(1)}, u32[]{:S(2)}, u32[]{:S(2)}) collective-permute-start(bf16[2,128,128]{2,1,0:T(8,128)(2,1)S(1)} %get-tuple-element.96), channel_id=1, source_target_pairs={{0,24},{4,28},{8,0},{12,4},{16,8},{20,12},{24,16},{28,20},{1,25},{... | collective-permute-start | bytes 196616 | tf_op jit(solution)/shard_map/ppermute | solution.py:32
  118.9 8.5 %collective-permute-start.32 = (bf16[6,128,128]{2,1,0:T(8,128)(2,1)S(1)}, bf16[6,128,128]{2,1,0:T(8,128)(2,1)S(1)}, u32[]{:S(2)}, u32[]{:S(2)}) collective-permute-start(bf16[6,128,128]{2,1,0:T(8,128)(2,1)S(1)} %shard_map.94), channel_id=1, source_target_pairs={{0,3},{1,0},{2,1},{3,2},{4,7},{5,4},{6,5},{7,6},{8,11},{9,8},{10,9... | collective-permute-start | bytes 589832 | tf_op jit(solution)/shard_map/ppermute | solution.py:32
  119.7 12.8 %collective-permute-start.34 = (bf16[6,128,128]{2,1,0:T(8,128)(2,1)S(1)}, bf16[6,128,128]{2,1,0:T(8,128)(2,1)S(1)}, u32[]{:S(2)}, u32[]{:S(2)}) collective-permute-start(bf16[6,128,128]{2,1,0:T(8,128)(2,1)S(1)} %shard_map.95), channel_id=1, source_target_pairs={{0,1},{1,2},{2,3},{3,0},{4,5},{5,6},{6,7},{7,4},{8,9},{9,10},{10,1... | collective-permute-start | bytes 589832 | tf_op jit(solution)/shard_map/ppermute | solution.py:32
  122.0 18.7 %collective-permute-start.33 = (bf16[6,128,128]{2,1,0:T(8,128)(2,1)S(1)}, bf16[6,128,128]{2,1,0:T(8,128)(2,1)S(1)}, u32[]{:S(2)}, u32[]{:S(2)}) collective-permute-start(bf16[6,128,128]{2,1,0:T(8,128)(2,1)S(1)} %get-tuple-element.98), channel_id=1, source_target_pairs={{0,2},{1,3},{2,0},{3,1},{4,6},{5,7},{6,4},{7,5},{8,10},{9,11},{10,... | collective-permute-start | bytes 589832 | tf_op jit(solution)/shard_map/ppermute | solution.py:32
  143.3 14.0 %collective-permute-start.37 = (bf16[6,128,128]{2,1,0:T(8,128)(2,1)S(1)}, bf16[6,128,128]{2,1,0:T(8,128)(2,1)S(1)}, u32[]{:S(2)}, u32[]{:S(2)}) collective-permute-start(bf16[6,128,128]{2,1,0:T(8,128)(2,1)S(1)} %get-tuple-element.101), channel_id=1, source_target_pairs={{0,2},{1,3},{2,0},{3,1},{4,6},{5,7},{6,4},{7,5},{8,10},{9,11},{10,... | collective-permute-start | bytes 589832 | tf_op jit(solution)/shard_map/ppermute | solution.py:32
  143.8 14.6 %collective-permute-start.36 = (bf16[6,128,128]{2,1,0:T(8,128)(2,1)S(1)}, bf16[6,128,128]{2,1,0:T(8,128)(2,1)S(1)}, u32[]{:S(2)}, u32[]{:S(2)}) collective-permute-start(bf16[6,128,128]{2,1,0:T(8,128)(2,1)S(1)} %shard_map.98), channel_id=1, source_target_pairs={{0,1},{1,2},{2,3},{3,0},{4,5},{5,6},{6,7},{7,4},{8,9},{9,10},{10,1... | collective-permute-start | bytes 589832 | tf_op jit(solution)/shard_map/ppermute | solution.py:32
  145.1 14.7 %collective-permute-start.35 = (bf16[6,128,128]{2,1,0:T(8,128)(2,1)S(1)}, bf16[6,128,128]{2,1,0:T(8,128)(2,1)S(1)}, u32[]{:S(2)}, u32[]{:S(2)}) collective-permute-start(bf16[6,128,128]{2,1,0:T(8,128)(2,1)S(1)} %shard_map.97), channel_id=1, source_target_pairs={{0,3},{1,0},{2,1},{3,2},{4,7},{5,4},{6,5},{7,6},{8,11},{9,8},{10,9... | collective-permute-start | bytes 589832 | tf_op jit(solution)/shard_map/ppermute | solution.py:32
  161.1 15.0 %collective-permute-start.38 = (bf16[6,128,128]{2,1,0:T(8,128)(2,1)S(1)}, bf16[6,128,128]{2,1,0:T(8,128)(2,1)S(1)}, u32[]{:S(2)}, u32[]{:S(2)}) collective-permute-start(bf16[6,128,128]{2,1,0:T(8,128)(2,1)S(1)} %get-tuple-element.103), channel_id=1, source_target_pairs={{0,28},{4,0},{8,4},{12,8},{16,12},{20,16},{24,20},{28,24},{1,29},{... | collective-permute-start | bytes 589832 | tf_op jit(solution)/shard_map/ppermute | solution.py:32
  162.4 13.6 %collective-permute-start.39 = (bf16[6,128,128]{2,1,0:T(8,128)(2,1)S(1)}, bf16[6,128,128]{2,1,0:T(8,128)(2,1)S(1)}, u32[]{:S(2)}, u32[]{:S(2)}) collective-permute-start(bf16[6,128,128]{2,1,0:T(8,128)(2,1)S(1)} %get-tuple-element.104), channel_id=1, source_target_pairs={{0,4},{4,8},{8,12},{12,16},{16,20},{20,24},{24,28},{28,0},{1,5},{5... | collective-permute-start | bytes 589832 | tf_op jit(solution)/shard_map/ppermute | solution.py:32
  162.4 6.7 %collective-permute-start.40 = (bf16[2,128,128]{2,1,0:T(8,128)(2,1)S(1)}, bf16[2,128,128]{2,1,0:T(8,128)(2,1)S(1)}, u32[]{:S(2)}, u32[]{:S(2)}) collective-permute-start(bf16[2,128,128]{2,1,0:T(8,128)(2,1)S(1)} %get-tuple-element.105), channel_id=1, source_target_pairs={{0,8},{4,12},{8,16},{12,20},{16,24},{20,28},{24,0},{28,4},{1,9},{5... | collective-permute-start | bytes 196616 | tf_op jit(solution)/shard_map/ppermute | solution.py:32
  163.3 8.3 %collective-permute-start.41 = (bf16[2,128,128]{2,1,0:T(8,128)(2,1)S(1)}, bf16[2,128,128]{2,1,0:T(8,128)(2,1)S(1)}, u32[]{:S(2)}, u32[]{:S(2)}) collective-permute-start(bf16[2,128,128]{2,1,0:T(8,128)(2,1)S(1)} %get-tuple-element.106), channel_id=1, source_target_pairs={{0,12},{4,16},{8,20},{12,24},{16,28},{20,0},{24,4},{28,8},{1,13},{... | collective-permute-start | bytes 196616 | tf_op jit(solution)/shard_map/ppermute | solution.py:32
  164.9 7.8 %collective-permute-start.42 = (bf16[2,128,128]{2,1,0:T(8,128)(2,1)S(1)}, bf16[2,128,128]{2,1,0:T(8,128)(2,1)S(1)}, u32[]{:S(2)}, u32[]{:S(2)}) collective-permute-start(bf16[2,128,128]{2,1,0:T(8,128)(2,1)S(1)} %get-tuple-element.107), channel_id=1, source_target_pairs={{0,16},{4,20},{8,24},{12,28},{16,0},{20,4},{24,8},{28,12},{1,17},{... | collective-permute-start | bytes 196616 | tf_op jit(solution)/shard_map/ppermute | solution.py:32
  169.1 4.4 %collective-permute-start.43 = (bf16[2,128,128]{2,1,0:T(8,128)(2,1)S(1)}, bf16[2,128,128]{2,1,0:T(8,128)(2,1)S(1)}, u32[]{:S(2)}, u32[]{:S(2)}) collective-permute-start(bf16[2,128,128]{2,1,0:T(8,128)(2,1)S(1)} %get-tuple-element.108), channel_id=1, source_target_pairs={{0,20},{4,24},{8,28},{12,0},{16,4},{20,8},{24,12},{28,16},{1,21},{... | collective-permute-start | bytes 196616 | tf_op jit(solution)/shard_map/ppermute | solution.py:32
  171.7 4.4 %collective-permute-start.44 = (bf16[2,128,128]{2,1,0:T(8,128)(2,1)S(1)}, bf16[2,128,128]{2,1,0:T(8,128)(2,1)S(1)}, u32[]{:S(2)}, u32[]{:S(2)}) collective-permute-start(bf16[2,128,128]{2,1,0:T(8,128)(2,1)S(1)} %get-tuple-element.109), channel_id=1, source_target_pairs={{0,24},{4,28},{8,0},{12,4},{16,8},{20,12},{24,16},{28,20},{1,25},{... | collective-permute-start | bytes 196616 | tf_op jit(solution)/shard_map/ppermute | solution.py:32
where the time goes:
time: 179 us; the launch traced here: 178 us
  waiting for transfers between devices  79.2 us (44%)
  starting transfers between devices  55.2 us (31%)
  Pallas kernels  33.7 us (19%)
  local copies, waits for them, and re-layouts  9.2 us (5%)
    ppermute x45, waiting for transfers between devices, shifted(): lax.ppermute(value, axis, [(i, (i + steps) % count) for i in range(count)])  79.2 us
    ppermute x45, starting transfers between devices, shifted(): lax.ppermute(value, axis, [(i, (i + steps) % count) for i in range(count)])  55.2 us
    pallas_call x28, Pallas kernels, call(): pl.pallas_call(kernel, out_shape=out_shape, in_specs=in_specs, out_specs=...  33.7 us
    unnamed x13, local copies, waits for them, and re-layouts  9.2 us
  transfers between devices with their start and end apart: 45, of which 27 were waited for; matrix products, arithmetic and copies ran while one was open for 0% of the time, Pallas kernels for 7%

commit v1 on v0

--- a/solution.py
+++ b/solution.py
@@ -14,6 +14,7 @@
 SMEM = pl.BlockSpec(memory_space=pltpu.SMEM)
 INDEX = pl.BlockSpec(memory_space=pltpu.SMEM)
 ANY = pl.BlockSpec(memory_space=pl.ANY)
+HBM = pl.BlockSpec(memory_space=pltpu.HBM)
 PARAMS = pltpu.CompilerParams(vmem_limit_bytes=16 << 20)
 F32, BF16 = jnp.float32, jnp.bfloat16
 MOST_SHIFTS = 8
@@ -21,6 +22,10 @@
 
 def in_smem(value):
     return pltpu.with_memory_space_constraint(value, pltpu.SMEM)
+
+
+def in_hbm(value):
+    return pltpu.with_memory_space_constraint(value, pltpu.HBM)
 
 
 def here(value):
@@ -77,6 +82,7 @@
 def call(kernel, out_shape, in_specs, args, cost, scratch=(), aliases={}, out_specs=None):
     args = [here(a) if spec is VMEM else a for spec, a in zip(in_specs, args)]
     args = [in_smem(a) if spec is INDEX else a for spec, a in zip(in_specs, args)]
+    args = [in_hbm(a) if spec is HBM else a for spec, a in zip(in_specs, args)]
     return pl.pallas_call(
         kernel,
         out_shape=out_shape,
@@ -135,7 +141,7 @@
         [pltpu.SMEM(kern_cols.shape, jnp.int32)]
         + [ask] * n_ask
         + [plan.blocks(n, BF16) for n in (rows, near, near)],
-        [VMEM, ANY],
+        [VMEM, HBM],
         [kern_cols, start_v],
         plan.cost(0, 3 << 20),
         [
@@ -192,7 +198,7 @@
     out = call(
         kernel,
         out_shape,
-        [INDEX, ANY if first_time else VMEM] + [VMEM] * n_in,
+        [INDEX, HBM if first_time else VMEM] + [VMEM] * n_in,
         [sources, kern] + (list(inputs) if gathers else [table]),
         plan.cost(share * degree, 4 << 20),
         [pltpu.SemaphoreType.DMA((share,))] if first_time else (),

time: 179 us -> 174 us (0.972)
  local copies, waits for them, and re-layouts: 9.2 us -> 0.78 us
  Pallas kernels: 33.7 us -> 38 us
    unnamed x13 -> x7, local copies, waits for them, and re-layouts: 9.2 us -> 0.78 us
    pallas_call x28, Pallas kernels: 33.7 us -> 38 us  [call(): pl.pallas_call(kernel, out_shape=out_shape, in_specs=in_specs, out_specs=...]
  transfers between devices with their start and end apart: 45 -> 45, of which waited for: 27 -> 27; matrix products, arithmetic and copies ran while one was open for 0% -> 0% of each run, Pallas kernels for 7% -> 8%
where the time goes in v1:
time: 174 us; the launch traced here: 173 us
  waiting for transfers between devices  78.3 us (45%)
  starting transfers between devices  55.2 us (32%)
  Pallas kernels  38 us (22%)
    ppermute x45, waiting for transfers between devices, shifted(): lax.ppermute(value, axis, [(i, (i + steps) % count) for i in range(count)])  78.3 us
    ppermute x45, starting transfers between devices, shifted(): lax.ppermute(value, axis, [(i, (i + steps) % count) for i in range(count)])  55.2 us
    pallas_call x28, Pallas kernels, call(): pl.pallas_call(kernel, out_shape=out_shape, in_specs=in_specs, out_specs=...  38 us
  transfers between devices with their start and end apart: 45, of which 27 were waited for; matrix products, arithmetic and copies ran while one was open for 0% of the time, Pallas kernels for 8%

profile of v1, /device:TPU:0, one launch (start us, length us, event | category | flops | bytes accessed | tf_op | source)
XLA Modules:
  0.0 173.3 jit_solution(17496244676729740000)
XLA Ops:
  1.4 2.8 %shard_map.77 = (s32[24,16]{1,0:T(8,128)S(4)}, s32[2]{0:T(128)S(1)}, s32[2]{0:T(128)S(1)}, s32[2]{0:T(128)S(1)}, s32[2]{0:T(128)S(1)}, /*index=5*/s32[2]{0:T(128...) custom-call(s32[24,16]{1,0:T(8,128)S(1)} %copy.14.cols_ref, ...), custom_call_target="tpu_custom_call" | custom-call | bytes 3145728 | tf_op jit(solution)/shard_map/pallas_call | solution.py:86
  4.7 2.9 %collective-permute-start.1 = (bf16[6,128,128]{2,1,0:T(8,128)(2,1)S(1)}, bf16[6,128,128]{2,1,0:T(8,128)(2,1)S(1)}, u32[]{:S(2)}, u32[]{:S(2)}) collective-permute-start(bf16[6,128,128]{2,1,0:T(8,128)(2,1)S(1)} %get-tuple-element.59), channel_id=1, source_target_pairs={{0,28},{4,0},{8,4},{12,8},{16,12},{20,16},{24,20},{28,24},{1,29},{... | collective-permute-start | bytes 589832 | tf_op jit(solution)/shard_map/ppermute | solution.py:37
  7.7 2.2 %collective-permute-start.2 = (s32[2]{0:T(128)S(1)}, s32[2]{0:T(128)S(1)}, u32[]{:S(2)}, u32[]{:S(2)}) collective-permute-start(s32[2]{0:T(128)S(1)} %get-tuple-element.60), channel_id=1, source_target_pairs={{0,24},{4,28},{8,0},{12,4},{16,8},{20,12},{24,16},{28,20},{1,25},{... | collective-permute-start | bytes 32 | tf_op jit(solution)/shard_map/ppermute | solution.py:37
  10.4 3.5 %collective-permute-done.2.rest_0_.rest_5_ = s32[2]{0:T(128)S(1)} collective-permute-done((s32[2]{0:T(128)S(1)}, s32[2]{0:T(128)S(1)}, u32[]{:S(2)}, u32[]{:S(2)}) %collective-permute-start.2) | collective-permute-done | bytes 40 | tf_op jit(solution)/shard_map/ppermute | solution.py:37
  13.9 1.5 collective-permute-start.6
  15.4 1.5 collective-permute-done.5.rest_3_.rest_8_
  16.9 1.5 collective-permute-done.6.rest_4_.rest_9_
  19.6 1.2 collective-permute-start.8
  21.1 3.2 %collective-permute-done.7.rest_3_ = bf16[2,128,128]{2,1,0:T(8,128)(2,1)S(1)} collective-permute-done((bf16[2,128,128]{2,1,0:T(8,128)(2,1)S(1)}, bf16[2,128,128]{2,1,0:T(8,128)(2,1)S(1)}, u32[]{:S(2)}, u32[]{:S(2)}) %collective-permute-start.7) | collective-permute-done | bytes 65568 | tf_op jit(solution)/shard_map/ppermute | solution.py:37
  24.3 1.4 collective-permute-start.11
  26.1 2.0 %collective-permute-done.10.rest_6_ = bf16[2,128,128]{2,1,0:T(8,128)(2,1)S(1)} collective-permute-done((bf16[2,128,128]{2,1,0:T(8,128)(2,1)S(1)}, bf16[2,128,128]{2,1,0:T(8,128)(2,1)S(1)}, u32[]{:S(2)}, u32[]{:S(2)}) %collective-permute-start.10) | collective-permute-done | bytes 65568 | tf_op jit(solution)/shard_map/ppermute | solution.py:37
  28.1 1.2 collective-permute-done.11.rest_7_
  29.3 2.9 %shard_map.79 = (bf16[6,128,128]{2,1,0:T(8,128)(2,1)S(1)}, bf16[52,128,128]{2,1,0:T(8,128)(2,1)S(1)}, bf16[6,16,128,128]{3,2,1,0:T(8,128)(2,1)S(1)}) custom-call(s32[24,16]{1,0:T(8,128)S(4)} %get-tuple-element.56.src, bf16[24,16,128,128]{3,2,1,0:T(8,128)(2,1)} %kern_ref.7, bf16[24,128,128]{2,1,0:T(8,128)(2,1)S(1)} %get-tuple-element.57.own_ref.rest_0_, ...), custom_call_target="tpu_custom_call" | custom-call | flops 402653184 | bytes 4194304 | tf_op jit(solution)/shard_map/pallas_call | solution.py:86
  32.2 2.9 %shard_map.82 = (bf16[6,128,128]{2,1,0:T(8,128)(2,1)S(1)}, bf16[6,16,128,128]{3,2,1,0:T(8,128)(2,1)S(1)}) custom-call(s32[24,16]{1,0:T(8,128)S(4)} %get-tuple-element.56.src, bf16[24,16,128,128]{3,2,1,0:T(8,128)(2,1)} %kern_ref.7, bf16[52,128,128]{2,1,0:T(8,128)(2,1)S(1)} %get-tuple-element.70.rest_0_), custom_call_target="tpu_custom_call" | custom-call | flops 402653184 | bytes 4194304 | tf_op jit(solution)/shard_map/pallas_call | solution.py:86
  35.0 2.9 %shard_map.81 = (bf16[6,128,128]{2,1,0:T(8,128)(2,1)S(1)}, bf16[6,16,128,128]{3,2,1,0:T(8,128)(2,1)S(1)}) custom-call(s32[24,16]{1,0:T(8,128)S(4)} %get-tuple-element.56.src, bf16[24,16,128,128]{3,2,1,0:T(8,128)(2,1)} %kern_ref.7, bf16[52,128,128]{2,1,0:T(8,128)(2,1)S(1)} %get-tuple-element.70.rest_0_), custom_call_target="tpu_custom_call" | custom-call | flops 402653184 | bytes 4194304 | tf_op jit(solution)/shard_map/pallas_call | solution.py:86
  37.9 2.6 %collective-permute-start.13 = (bf16[6,128,128]{2,1,0:T(8,128)(2,1)S(1)}, bf16[6,128,128]{2,1,0:T(8,128)(2,1)S(1)}, u32[]{:S(2)}, u32[]{:S(2)}) collective-permute-start(bf16[6,128,128]{2,1,0:T(8,128)(2,1)S(1)} %get-tuple-element.76), channel_id=1, source_target_pairs={{0,2},{1,3},{2,0},{3,1},{4,6},{5,7},{6,4},{7,5},{8,10},{9,11},{10,... | collective-permute-start | bytes 589832 | tf_op jit(solution)/shard_map/ppermute | solution.py:37
  40.6 1.3 collective-permute-start.12
  42.6 2.9 %shard_map.80 = (bf16[6,128,128]{2,1,0:T(8,128)(2,1)S(1)}, bf16[6,16,128,128]{3,2,1,0:T(8,128)(2,1)S(1)}) custom-call(s32[24,16]{1,0:T(8,128)S(4)} %get-tuple-element.56.src, bf16[24,16,128,128]{3,2,1,0:T(8,128)(2,1)} %kern_ref.7, bf16[52,128,128]{2,1,0:T(8,128)(2,1)S(1)} %get-tuple-element.70.rest_0_), custom_call_target="tpu_custom_call" | custom-call | flops 402653184 | bytes 4194304 | tf_op jit(solution)/shard_map/pallas_call | solution.py:86
  45.5 6.2 %collective-permute-done.13.refs_2_ = bf16[6,128,128]{2,1,0:T(8,128)(2,1)S(1)} collective-permute-done((bf16[6,128,128]{2,1,0:T(8,128)(2,1)S(1)}, bf16[6,128,128]{2,1,0:T(8,128)(2,1)S(1)}, u32[]{:S(2)}, u32[]{:S(2)}) %collective-permute-start.13) | collective-permute-done | bytes 196640 | tf_op jit(solution)/shard_map/ppermute | solution.py:37
  51.6 3.7 %collective-permute-done.14.refs_3_ = bf16[6,128,128]{2,1,0:T(8,128)(2,1)S(1)} collective-permute-done((bf16[6,128,128]{2,1,0:T(8,128)(2,1)S(1)}, bf16[6,128,128]{2,1,0:T(8,128)(2,1)S(1)}, u32[]{:S(2)}, u32[]{:S(2)}) %collective-permute-start.14) | collective-permute-done | bytes 196640 | tf_op jit(solution)/shard_map/ppermute | solution.py:37
  55.4 2.0 %shard_map.83 = (bf16[6,128,512]{2,1,0:T(8,128)(2,1)S(1)}, bf16[6,128,128]{2,1,0:T(8,128)(2,1)S(1)}) custom-call(bf16[6,128,128]{2,1,0:T(8,128)(2,1)S(1)} %get-tuple-element.74.refs_0_, bf16[6,128,128]{2,1,0:T(8,128)(2,1)S(1)} %collective-permute-done.12.refs_1_, bf16[6,128,128]{2,1,0:T(8,128)(2,1)S(1)} %collective-permute-done.13.refs_2_, ...), custom_call_target="tpu_custom_call" | custom-call | flops 503316480 | bytes 4194304 | tf_op jit(solution)/shard_map/pallas_call | solution.py:86
  57.4 5.8 %collective-permute-start.17 = (bf16[6,128,128]{2,1,0:T(8,128)(2,1)S(1)}, bf16[6,128,128]{2,1,0:T(8,128)(2,1)S(1)}, u32[]{:S(2)}, u32[]{:S(2)}) collective-permute-start(bf16[6,128,128]{2,1,0:T(8,128)(2,1)S(1)} %get-tuple-element.80), channel_id=1, source_target_pairs={{0,2},{1,3},{2,0},{3,1},{4,6},{5,7},{6,4},{7,5},{8,10},{9,11},{10,... | collective-permute-start | bytes 589832 | tf_op jit(solution)/shard_map/ppermute | solution.py:37
  64.0 4.0 %collective-permute-start.15 = (bf16[6,128,128]{2,1,0:T(8,128)(2,1)S(1)}, bf16[6,128,128]{2,1,0:T(8,128)(2,1)S(1)}, u32[]{:S(2)}, u32[]{:S(2)}) collective-permute-start(bf16[6,128,128]{2,1,0:T(8,128)(2,1)S(1)} %shard_map.84), channel_id=1, source_target_pairs={{0,3},{1,0},{2,1},{3,2},{4,7},{5,4},{6,5},{7,6},{8,11},{9,8},{10,9... | collective-permute-start | bytes 589832 | tf_op jit(solution)/shard_map/ppermute | solution.py:37
  68.4 1.2 shard_map.87.rest_0_
  69.6 7.3 %collective-permute-done.17.b_ref = bf16[6,128,128]{2,1,0:T(8,128)(2,1)S(1)} collective-permute-done((bf16[6,128,128]{2,1,0:T(8,128)(2,1)S(1)}, bf16[6,128,128]{2,1,0:T(8,128)(2,1)S(1)}, u32[]{:S(2)}, u32[]{:S(2)}) %collective-permute-start.17) | collective-permute-done | bytes 196640 | tf_op jit(solution)/shard_map/ppermute | solution.py:37
  77.0 1.1 shard_map.88.rest_0_
  78.1 1.1 shard_map.89.rest_0_
  79.2 1.2 shard_map.90
  80.4 1.4 collective-permute-start.18
  82.1 1.9 %collective-permute-start.21 = (bf16[2,128,128]{2,1,0:T(8,128)(2,1)S(1)}, bf16[2,128,128]{2,1,0:T(8,128)(2,1)S(1)}, u32[]{:S(2)}, u32[]{:S(2)}) collective-permute-start(bf16[2,128,128]{2,1,0:T(8,128)(2,1)S(1)} %get-tuple-element.85), channel_id=1, source_target_pairs={{0,12},{4,16},{8,20},{12,24},{16,28},{20,0},{24,4},{28,8},{1,13},{... | collective-permute-start | bytes 196616 | tf_op jit(solution)/shard_map/ppermute | solution.py:37
  85.0 3.2 %collective-permute-done.20.rest_0_ = bf16[2,128,128]{2,1,0:T(8,128)(2,1)S(1)} collective-permute-done((bf16[2,128,128]{2,1,0:T(8,128)(2,1)S(1)}, bf16[2,128,128]{2,1,0:T(8,128)(2,1)S(1)}, u32[]{:S(2)}, u32[]{:S(2)}) %collective-permute-start.20) | collective-permute-done | bytes 65568 | tf_op jit(solution)/shard_map/ppermute | solution.py:37
  88.2 2.4 %collective-permute-start.23 = (bf16[2,128,128]{2,1,0:T(8,128)(2,1)S(1)}, bf16[2,128,128]{2,1,0:T(8,128)(2,1)S(1)}, u32[]{:S(2)}, u32[]{:S(2)}) collective-permute-start(bf16[2,128,128]{2,1,0:T(8,128)(2,1)S(1)} %get-tuple-element.87), channel_id=1, source_target_pairs={{0,20},{4,24},{8,28},{12,0},{16,4},{20,8},{24,12},{28,16},{1,21},{... | collective-permute-start | bytes 196616 | tf_op jit(solution)/shard_map/ppermute | solution.py:37
  91.0 1.0 collective-permute-done.22.rest_2_
  92.5 2.7 %collective-permute-done.24.rest_4_ = bf16[2,128,128]{2,1,0:T(8,128)(2,1)S(1)} collective-permute-done((bf16[2,128,128]{2,1,0:T(8,128)(2,1)S(1)}, bf16[2,128,128]{2,1,0:T(8,128)(2,1)S(1)}, u32[]{:S(2)}, u32[]{:S(2)}) %collective-permute-start.24) | collective-permute-done | bytes 65568 | tf_op jit(solution)/shard_map/ppermute | solution.py:37
  95.2 1.0 shard_map.91
  96.3 2.6 %collective-permute-start.26 = (bf16[6,128,128]{2,1,0:T(8,128)(2,1)S(1)}, bf16[6,128,128]{2,1,0:T(8,128)(2,1)S(1)}, u32[]{:S(2)}, u32[]{:S(2)}) collective-permute-start(bf16[6,128,128]{2,1,0:T(8,128)(2,1)S(1)} %get-tuple-element.91), channel_id=1, source_target_pairs={{0,28},{4,0},{8,4},{12,8},{16,12},{20,16},{24,20},{28,24},{1,29},{... | collective-permute-start | bytes 589832 | tf_op jit(solution)/shard_map/ppermute | solution.py:37
  99.5 1.2 collective-permute-start.29
  100.7 5.3 %collective-permute-done.27.rest_3_ = bf16[2,128,128]{2,1,0:T(8,128)(2,1)S(1)} collective-permute-done((bf16[2,128,128]{2,1,0:T(8,128)(2,1)S(1)}, bf16[2,128,128]{2,1,0:T(8,128)(2,1)S(1)}, u32[]{:S(2)}, u32[]{:S(2)}) %collective-permute-start.27) | collective-permute-done | bytes 65568 | tf_op jit(solution)/shard_map/ppermute | solution.py:37
  105.9 1.4 collective-permute-start.31
  107.4 2.4 %collective-permute-done.30.rest_6_ = bf16[2,128,128]{2,1,0:T(8,128)(2,1)S(1)} collective-permute-done((bf16[2,128,128]{2,1,0:T(8,128)(2,1)S(1)}, bf16[2,128,128]{2,1,0:T(8,128)(2,1)S(1)}, u32[]{:S(2)}, u32[]{:S(2)}) %collective-permute-start.30) | collective-permute-done | bytes 65568 | tf_op jit(solution)/shard_map/ppermute | solution.py:37
  109.7 1.2 collective-permute-done.31.rest_7_
  110.9 1.1 shard_map.92
  112.0 1.0 shard_map.95
  113.0 1.0 shard_map.94
  114.7 2.3 %collective-permute-start.34 = (bf16[6,128,128]{2,1,0:T(8,128)(2,1)S(1)}, bf16[6,128,128]{2,1,0:T(8,128)(2,1)S(1)}, u32[]{:S(2)}, u32[]{:S(2)}) collective-permute-start(bf16[6,128,128]{2,1,0:T(8,128)(2,1)S(1)} %shard_map.95), channel_id=1, source_target_pairs={{0,1},{1,2},{2,3},{3,0},{4,5},{5,6},{6,7},{7,4},{8,9},{9,10},{10,1... | collective-permute-start | bytes 589832 | tf_op jit(solution)/shard_map/ppermute | solution.py:37
  117.1 1.2 collective-permute-start.33
  118.3 1.0 shard_map.93.refs_0_
  119.2 3.2 %collective-permute-done.32.refs_1_ = bf16[6,128,128]{2,1,0:T(8,128)(2,1)S(1)} collective-permute-done((bf16[6,128,128]{2,1,0:T(8,128)(2,1)S(1)}, bf16[6,128,128]{2,1,0:T(8,128)(2,1)S(1)}, u32[]{:S(2)}, u32[]{:S(2)}) %collective-permute-start.32) | collective-permute-done | bytes 196640 | tf_op jit(solution)/shard_map/ppermute | solution.py:37
  122.4 5.1 %collective-permute-done.34.refs_3_ = bf16[6,128,128]{2,1,0:T(8,128)(2,1)S(1)} collective-permute-done((bf16[6,128,128]{2,1,0:T(8,128)(2,1)S(1)}, bf16[6,128,128]{2,1,0:T(8,128)(2,1)S(1)}, u32[]{:S(2)}, u32[]{:S(2)}) %collective-permute-start.34) | collective-permute-done | bytes 196640 | tf_op jit(solution)/shard_map/ppermute | solution.py:37
  127.5 8.3 %collective-permute-done.33.refs_2_ = bf16[6,128,128]{2,1,0:T(8,128)(2,1)S(1)} collective-permute-done((bf16[6,128,128]{2,1,0:T(8,128)(2,1)S(1)}, bf16[6,128,128]{2,1,0:T(8,128)(2,1)S(1)}, u32[]{:S(2)}, u32[]{:S(2)}) %collective-permute-start.33) | collective-permute-done | bytes 196640 | tf_op jit(solution)/shard_map/ppermute | solution.py:37
  135.8 2.6 %shard_map.96 = (bf16[6,128,512]{2,1,0:T(8,128)(2,1)S(1)}, bf16[6,128,128]{2,1,0:T(8,128)(2,1)S(1)}, f32[768,512]{1,0:T(8,128)}) custom-call(bf16[6,128,128]{2,1,0:T(8,128)(2,1)S(1)} %shard_map.93.refs_0_, bf16[6,128,128]{2,1,0:T(8,128)(2,1)S(1)} %collective-permute-done.32.refs_1_, bf16[6,128,128]{2,1,0:T(8,128)(2,1)S(1)} %collective-permute-done.33.refs_2_, ...), custom_call_target="tpu_custom_call" | custom-call | flops 503316480 | bytes 4194304 | tf_op jit(solution)/shard_map/pallas_call | solution.py:86
  140.1 3.0 %collective-permute-start.35 = (bf16[6,128,128]{2,1,0:T(8,128)(2,1)S(1)}, bf16[6,128,128]{2,1,0:T(8,128)(2,1)S(1)}, u32[]{:S(2)}, u32[]{:S(2)}) collective-permute-start(bf16[6,128,128]{2,1,0:T(8,128)(2,1)S(1)} %shard_map.97), channel_id=1, source_target_pairs={{0,3},{1,0},{2,1},{3,2},{4,7},{5,4},{6,5},{7,6},{8,11},{9,8},{10,9... | collective-permute-start | bytes 589832 | tf_op jit(solution)/shard_map/ppermute | solution.py:37
  143.5 1.2 shard_map.100.rest_0_
  144.8 7.7 %collective-permute-done.37.b_ref = bf16[6,128,128]{2,1,0:T(8,128)(2,1)S(1)} collective-permute-done((bf16[6,128,128]{2,1,0:T(8,128)(2,1)S(1)}, bf16[6,128,128]{2,1,0:T(8,128)(2,1)S(1)}, u32[]{:S(2)}, u32[]{:S(2)}) %collective-permute-start.37) | collective-permute-done | bytes 196640 | tf_op jit(solution)/shard_map/ppermute | solution.py:37
  152.4 1.1 shard_map.101.rest_0_
  153.5 1.1 shard_map.102.rest_0_
  154.9 1.2 shard_map.103
  156.1 1.4 collective-permute-start.38
  158.4 1.5 collective-permute-start.41
  159.9 1.0 collective-permute-start.42
  160.9 3.3 %collective-permute-done.40.rest_0_ = bf16[2,128,128]{2,1,0:T(8,128)(2,1)S(1)} collective-permute-done((bf16[2,128,128]{2,1,0:T(8,128)(2,1)S(1)}, bf16[2,128,128]{2,1,0:T(8,128)(2,1)S(1)}, u32[]{:S(2)}, u32[]{:S(2)}) %collective-permute-start.40) | collective-permute-done | bytes 65568 | tf_op jit(solution)/shard_map/ppermute | solution.py:37
  164.2 2.5 %collective-permute-start.43 = (bf16[2,128,128]{2,1,0:T(8,128)(2,1)S(1)}, bf16[2,128,128]{2,1,0:T(8,128)(2,1)S(1)}, u32[]{:S(2)}, u32[]{:S(2)}) collective-permute-start(bf16[2,128,128]{2,1,0:T(8,128)(2,1)S(1)} %get-tuple-element.108), channel_id=1, source_target_pairs={{0,20},{4,24},{8,28},{12,0},{16,4},{20,8},{24,12},{28,16},{1,21},{... | collective-permute-start | bytes 196616 | tf_op jit(solution)/shard_map/ppermute | solution.py:37
  168.7 2.5 %collective-permute-done.44.rest_4_ = bf16[2,128,128]{2,1,0:T(8,128)(2,1)S(1)} collective-permute-done((bf16[2,128,128]{2,1,0:T(8,128)(2,1)S(1)}, bf16[2,128,128]{2,1,0:T(8,128)(2,1)S(1)}, u32[]{:S(2)}, u32[]{:S(2)}) %collective-permute-start.44) | collective-permute-done | bytes 65568 | tf_op jit(solution)/shard_map/ppermute | solution.py:37
  171.1 2.1 %shard_map.104 = f32[24,128,128]{2,1,0:T(8,128)} custom-call(bf16[24,128,128]{2,1,0:T(8,128)(2,1)S(1)} %get-tuple-element.102.own_ref, bf16[6,128,128]{2,1,0:T(8,128)(2,1)S(1)} %collective-permute-done.38.right_ref, bf16[6,128,128]{2,1,0:T(8,128)(2,1)S(1)} %collective-permute-done.39.left_ref, f32[24,128,128]{2,1,0:T(8,128)S(1)} %bitcast.4, ...), custom_call_target="tpu_custom_call" | custom-call | bytes 6291456 | tf_op jit(solution)/shard_map/pallas_call | solution.py:86
  (61 shorter events, 14.4 us)
Async XLA Ops:
  4.2 25.1 %collective-permute-start = (bf16[6,128,128]{2,1,0:T(8,128)(2,1)S(1)}, bf16[6,128,128]{2,1,0:T(8,128)(2,1)S(1)}, u32[]{:S(2)}, u32[]{:S(2)}) collective-permute-start(bf16[6,128,128]{2,1,0:T(8,128)(2,1)S(1)} %get-tuple-element.58), channel_id=1, source_target_pairs={{0,4},{4,8},{8,12},{12,16},{16,20},{20,24},{24,28},{28,0},{1,5},{5... | collective-permute-start | bytes 589832 | tf_op jit(solution)/shard_map/ppermute | solution.py:37
  4.7 24.6 %collective-permute-start.1 = (bf16[6,128,128]{2,1,0:T(8,128)(2,1)S(1)}, bf16[6,128,128]{2,1,0:T(8,128)(2,1)S(1)}, u32[]{:S(2)}, u32[]{:S(2)}) collective-permute-start(bf16[6,128,128]{2,1,0:T(8,128)(2,1)S(1)} %get-tuple-element.59), channel_id=1, source_target_pairs={{0,28},{4,0},{8,4},{12,8},{16,12},{20,16},{24,20},{28,24},{1,29},{... | collective-permute-start | bytes 589832 | tf_op jit(solution)/shard_map/ppermute | solution.py:37
  7.7 6.2 %collective-permute-start.2 = (s32[2]{0:T(128)S(1)}, s32[2]{0:T(128)S(1)}, u32[]{:S(2)}, u32[]{:S(2)}) collective-permute-start(s32[2]{0:T(128)S(1)} %get-tuple-element.60), channel_id=1, source_target_pairs={{0,24},{4,28},{8,0},{12,4},{16,8},{20,12},{24,16},{28,20},{1,25},{... | collective-permute-start | bytes 32 | tf_op jit(solution)/shard_map/ppermute | solution.py:37
  9.9 4.0 %collective-permute-start.3 = (s32[2]{0:T(128)S(1)}, s32[2]{0:T(128)S(1)}, u32[]{:S(2)}, u32[]{:S(2)}) collective-permute-start(s32[2]{0:T(128)S(1)} %get-tuple-element.61), channel_id=1, source_target_pairs={{0,20},{4,24},{8,28},{12,0},{16,4},{20,8},{24,12},{28,16},{1,21},{... | collective-permute-start | bytes 32 | tf_op jit(solution)/shard_map/ppermute | solution.py:37
  9.9 5.5 %collective-permute-start.4 = (s32[2]{0:T(128)S(1)}, s32[2]{0:T(128)S(1)}, u32[]{:S(2)}, u32[]{:S(2)}) collective-permute-start(s32[2]{0:T(128)S(1)} %get-tuple-element.62), channel_id=1, source_target_pairs={{0,16},{4,20},{8,24},{12,28},{16,0},{20,4},{24,8},{28,12},{1,17},{... | collective-permute-start | bytes 32 | tf_op jit(solution)/shard_map/ppermute | solution.py:37
  13.9 3.0 %collective-permute-start.5 = (s32[2]{0:T(128)S(1)}, s32[2]{0:T(128)S(1)}, u32[]{:S(2)}, u32[]{:S(2)}) collective-permute-start(s32[2]{0:T(128)S(1)} %get-tuple-element.63), channel_id=1, source_target_pairs={{0,12},{4,16},{8,20},{12,24},{16,28},{20,0},{24,4},{28,8},{1,13},{... | collective-permute-start | bytes 32 | tf_op jit(solution)/shard_map/ppermute | solution.py:37
  13.9 4.5 %collective-permute-start.6 = (s32[2]{0:T(128)S(1)}, s32[2]{0:T(128)S(1)}, u32[]{:S(2)}, u32[]{:S(2)}) collective-permute-start(s32[2]{0:T(128)S(1)} %get-tuple-element.64), channel_id=1, source_target_pairs={{0,8},{4,12},{8,16},{12,20},{16,24},{20,28},{24,0},{28,4},{1,9},{5... | collective-permute-start | bytes 32 | tf_op jit(solution)/shard_map/ppermute | solution.py:37
  19.0 5.3 %collective-permute-start.7 = (bf16[2,128,128]{2,1,0:T(8,128)(2,1)S(1)}, bf16[2,128,128]{2,1,0:T(8,128)(2,1)S(1)}, u32[]{:S(2)}, u32[]{:S(2)}) collective-permute-start(bf16[2,128,128]{2,1,0:T(8,128)(2,1)S(1)} %get-tuple-element.65), channel_id=1, source_target_pairs={{0,8},{4,12},{8,16},{12,20},{16,24},{20,28},{24,0},{28,4},{1,9},{5... | collective-permute-start | bytes 196616 | tf_op jit(solution)/shard_map/ppermute | solution.py:37
  19.6 4.7 %collective-permute-start.8 = (bf16[2,128,128]{2,1,0:T(8,128)(2,1)S(1)}, bf16[2,128,128]{2,1,0:T(8,128)(2,1)S(1)}, u32[]{:S(2)}, u32[]{:S(2)}) collective-permute-start(bf16[2,128,128]{2,1,0:T(8,128)(2,1)S(1)} %get-tuple-element.66), channel_id=1, source_target_pairs={{0,12},{4,16},{8,20},{12,24},{16,28},{20,0},{24,4},{28,8},{1,13},{... | collective-permute-start | bytes 196616 | tf_op jit(solution)/shard_map/ppermute | solution.py:37
  20.8 5.3 %collective-permute-start.9 = (bf16[2,128,128]{2,1,0:T(8,128)(2,1)S(1)}, bf16[2,128,128]{2,1,0:T(8,128)(2,1)S(1)}, u32[]{:S(2)}, u32[]{:S(2)}) collective-permute-start(bf16[2,128,128]{2,1,0:T(8,128)(2,1)S(1)} %get-tuple-element.67), channel_id=1, source_target_pairs={{0,16},{4,20},{8,24},{12,28},{16,0},{20,4},{24,8},{28,12},{1,17},{... | collective-permute-start | bytes 196616 | tf_op jit(solution)/shard_map/ppermute | solution.py:37
  24.3 3.8 %collective-permute-start.10 = (bf16[2,128,128]{2,1,0:T(8,128)(2,1)S(1)}, bf16[2,128,128]{2,1,0:T(8,128)(2,1)S(1)}, u32[]{:S(2)}, u32[]{:S(2)}) collective-permute-start(bf16[2,128,128]{2,1,0:T(8,128)(2,1)S(1)} %get-tuple-element.68), channel_id=1, source_target_pairs={{0,20},{4,24},{8,28},{12,0},{16,4},{20,8},{24,12},{28,16},{1,21},{... | collective-permute-start | bytes 196616 | tf_op jit(solution)/shard_map/ppermute | solution.py:37
  24.3 5.0 %collective-permute-start.11 = (bf16[2,128,128]{2,1,0:T(8,128)(2,1)S(1)}, bf16[2,128,128]{2,1,0:T(8,128)(2,1)S(1)}, u32[]{:S(2)}, u32[]{:S(2)}) collective-permute-start(bf16[2,128,128]{2,1,0:T(8,128)(2,1)S(1)} %get-tuple-element.69), channel_id=1, source_target_pairs={{0,24},{4,28},{8,0},{12,4},{16,8},{20,12},{24,16},{28,20},{1,25},{... | collective-permute-start | bytes 196616 | tf_op jit(solution)/shard_map/ppermute | solution.py:37
  37.9 13.7 %collective-permute-start.13 = (bf16[6,128,128]{2,1,0:T(8,128)(2,1)S(1)}, bf16[6,128,128]{2,1,0:T(8,128)(2,1)S(1)}, u32[]{:S(2)}, u32[]{:S(2)}) collective-permute-start(bf16[6,128,128]{2,1,0:T(8,128)(2,1)S(1)} %get-tuple-element.76), channel_id=1, source_target_pairs={{0,2},{1,3},{2,0},{3,1},{4,6},{5,7},{6,4},{7,5},{8,10},{9,11},{10,... | collective-permute-start | bytes 589832 | tf_op jit(solution)/shard_map/ppermute | solution.py:37
  40.6 11.1 %collective-permute-start.12 = (bf16[6,128,128]{2,1,0:T(8,128)(2,1)S(1)}, bf16[6,128,128]{2,1,0:T(8,128)(2,1)S(1)}, u32[]{:S(2)}, u32[]{:S(2)}) collective-permute-start(bf16[6,128,128]{2,1,0:T(8,128)(2,1)S(1)} %get-tuple-element.75), channel_id=1, source_target_pairs={{0,3},{1,0},{2,1},{3,2},{4,7},{5,4},{6,5},{7,6},{8,11},{9,8},{10,9... | collective-permute-start | bytes 589832 | tf_op jit(solution)/shard_map/ppermute | solution.py:37
  41.9 13.5 %copy-start = (bf16[512,512]{1,0:T(8,128)(2,1)S(1)}, bf16[512,512]{1,0:T(8,128)(2,1)}, u32[]{:S(2)}) copy-start(bf16[512,512]{1,0:T(8,128)(2,1)} %k_ref.11) | copy-start | bytes 1572868
  41.9 13.5 %copy-start.2 = (f32[768,512]{1,0:T(8,128)S(1)}, f32[768,512]{1,0:T(8,128)}, u32[]{:S(2)}) copy-start(f32[768,512]{1,0:T(8,128)} %refs_5_.3) | copy-start | bytes 4718596
  41.9 13.5 %collective-permute-start.14 = (bf16[6,128,128]{2,1,0:T(8,128)(2,1)S(1)}, bf16[6,128,128]{2,1,0:T(8,128)(2,1)S(1)}, u32[]{:S(2)}, u32[]{:S(2)}) collective-permute-start(bf16[6,128,128]{2,1,0:T(8,128)(2,1)S(1)} %get-tuple-element.77), channel_id=1, source_target_pairs={{0,1},{1,2},{2,3},{3,0},{4,5},{5,6},{6,7},{7,4},{8,9},{9,10},{10,1... | collective-permute-start | bytes 589832 | tf_op jit(solution)/shard_map/ppermute | solution.py:37
  57.4 19.6 %collective-permute-start.17 = (bf16[6,128,128]{2,1,0:T(8,128)(2,1)S(1)}, bf16[6,128,128]{2,1,0:T(8,128)(2,1)S(1)}, u32[]{:S(2)}, u32[]{:S(2)}) collective-permute-start(bf16[6,128,128]{2,1,0:T(8,128)(2,1)S(1)} %get-tuple-element.80), channel_id=1, source_target_pairs={{0,2},{1,3},{2,0},{3,1},{4,6},{5,7},{6,4},{7,5},{8,10},{9,11},{10,... | collective-permute-start | bytes 589832 | tf_op jit(solution)/shard_map/ppermute | solution.py:37
  63.5 14.5 %collective-permute-start.16 = (bf16[6,128,128]{2,1,0:T(8,128)(2,1)S(1)}, bf16[6,128,128]{2,1,0:T(8,128)(2,1)S(1)}, u32[]{:S(2)}, u32[]{:S(2)}) collective-permute-start(bf16[6,128,128]{2,1,0:T(8,128)(2,1)S(1)} %shard_map.85), channel_id=1, source_target_pairs={{0,1},{1,2},{2,3},{3,0},{4,5},{5,6},{6,7},{7,4},{8,9},{9,10},{10,1... | collective-permute-start | bytes 589832 | tf_op jit(solution)/shard_map/ppermute | solution.py:37
  64.0 15.2 %collective-permute-start.15 = (bf16[6,128,128]{2,1,0:T(8,128)(2,1)S(1)}, bf16[6,128,128]{2,1,0:T(8,128)(2,1)S(1)}, u32[]{:S(2)}, u32[]{:S(2)}) collective-permute-start(bf16[6,128,128]{2,1,0:T(8,128)(2,1)S(1)} %shard_map.84), channel_id=1, source_target_pairs={{0,3},{1,0},{2,1},{3,2},{4,7},{5,4},{6,5},{7,6},{8,11},{9,8},{10,9... | collective-permute-start | bytes 589832 | tf_op jit(solution)/shard_map/ppermute | solution.py:37
  79.2 16.1 %copy-start.1 = (f32[3072,128]{1,0:T(8,128)S(1)}, f32[3072,128]{1,0:T(8,128)}, u32[]{:S(2)}) copy-start(f32[3072,128]{1,0:T(8,128)} %param.11) | copy-start | bytes 4718596
  80.4 14.8 %collective-permute-start.18 = (bf16[6,128,128]{2,1,0:T(8,128)(2,1)S(1)}, bf16[6,128,128]{2,1,0:T(8,128)(2,1)S(1)}, u32[]{:S(2)}, u32[]{:S(2)}) collective-permute-start(bf16[6,128,128]{2,1,0:T(8,128)(2,1)S(1)} %get-tuple-element.82), channel_id=1, source_target_pairs={{0,28},{4,0},{8,4},{12,8},{16,12},{20,16},{24,20},{28,24},{1,29},{... | collective-permute-start | bytes 589832 | tf_op jit(solution)/shard_map/ppermute | solution.py:37
  81.8 13.4 %collective-permute-start.19 = (bf16[6,128,128]{2,1,0:T(8,128)(2,1)S(1)}, bf16[6,128,128]{2,1,0:T(8,128)(2,1)S(1)}, u32[]{:S(2)}, u32[]{:S(2)}) collective-permute-start(bf16[6,128,128]{2,1,0:T(8,128)(2,1)S(1)} %get-tuple-element.83), channel_id=1, source_target_pairs={{0,4},{4,8},{8,12},{12,16},{16,20},{20,24},{24,28},{28,0},{1,5},{5... | collective-permute-start | bytes 589832 | tf_op jit(solution)/shard_map/ppermute | solution.py:37
  81.8 6.4 %collective-permute-start.20 = (bf16[2,128,128]{2,1,0:T(8,128)(2,1)S(1)}, bf16[2,128,128]{2,1,0:T(8,128)(2,1)S(1)}, u32[]{:S(2)}, u32[]{:S(2)}) collective-permute-start(bf16[2,128,128]{2,1,0:T(8,128)(2,1)S(1)} %get-tuple-element.84), channel_id=1, source_target_pairs={{0,8},{4,12},{8,16},{12,20},{16,24},{20,28},{24,0},{28,4},{1,9},{5... | collective-permute-start | bytes 196616 | tf_op jit(solution)/shard_map/ppermute | solution.py:37
  82.1 8.8 %collective-permute-start.21 = (bf16[2,128,128]{2,1,0:T(8,128)(2,1)S(1)}, bf16[2,128,128]{2,1,0:T(8,128)(2,1)S(1)}, u32[]{:S(2)}, u32[]{:S(2)}) collective-permute-start(bf16[2,128,128]{2,1,0:T(8,128)(2,1)S(1)} %get-tuple-element.85), channel_id=1, source_target_pairs={{0,12},{4,16},{8,20},{12,24},{16,28},{20,0},{24,4},{28,8},{1,13},{... | collective-permute-start | bytes 196616 | tf_op jit(solution)/shard_map/ppermute | solution.py:37
  84.1 7.8 %collective-permute-start.22 = (bf16[2,128,128]{2,1,0:T(8,128)(2,1)S(1)}, bf16[2,128,128]{2,1,0:T(8,128)(2,1)S(1)}, u32[]{:S(2)}, u32[]{:S(2)}) collective-permute-start(bf16[2,128,128]{2,1,0:T(8,128)(2,1)S(1)} %get-tuple-element.86), channel_id=1, source_target_pairs={{0,16},{4,20},{8,24},{12,28},{16,0},{20,4},{24,8},{28,12},{1,17},{... | collective-permute-start | bytes 196616 | tf_op jit(solution)/shard_map/ppermute | solution.py:37
  88.2 4.3 %collective-permute-start.23 = (bf16[2,128,128]{2,1,0:T(8,128)(2,1)S(1)}, bf16[2,128,128]{2,1,0:T(8,128)(2,1)S(1)}, u32[]{:S(2)}, u32[]{:S(2)}) collective-permute-start(bf16[2,128,128]{2,1,0:T(8,128)(2,1)S(1)} %get-tuple-element.87), channel_id=1, source_target_pairs={{0,20},{4,24},{8,28},{12,0},{16,4},{20,8},{24,12},{28,16},{1,21},{... | collective-permute-start | bytes 196616 | tf_op jit(solution)/shard_map/ppermute | solution.py:37
  90.9 4.3 %collective-permute-start.24 = (bf16[2,128,128]{2,1,0:T(8,128)(2,1)S(1)}, bf16[2,128,128]{2,1,0:T(8,128)(2,1)S(1)}, u32[]{:S(2)}, u32[]{:S(2)}) collective-permute-start(bf16[2,128,128]{2,1,0:T(8,128)(2,1)S(1)} %get-tuple-element.88), channel_id=1, source_target_pairs={{0,24},{4,28},{8,0},{12,4},{16,8},{20,12},{24,16},{28,20},{1,25},{... | collective-permute-start | bytes 196616 | tf_op jit(solution)/shard_map/ppermute | solution.py:37
  96.3 14.6 %collective-permute-start.25 = (bf16[6,128,128]{2,1,0:T(8,128)(2,1)S(1)}, bf16[6,128,128]{2,1,0:T(8,128)(2,1)S(1)}, u32[]{:S(2)}, u32[]{:S(2)}) collective-permute-start(bf16[6,128,128]{2,1,0:T(8,128)(2,1)S(1)} %get-tuple-element.90), channel_id=1, source_target_pairs={{0,4},{4,8},{8,12},{12,16},{16,20},{20,24},{24,28},{28,0},{1,5},{5... | collective-permute-start | bytes 589832 | tf_op jit(solution)/shard_map/ppermute | solution.py:37
  96.3 14.6 %collective-permute-start.26 = (bf16[6,128,128]{2,1,0:T(8,128)(2,1)S(1)}, bf16[6,128,128]{2,1,0:T(8,128)(2,1)S(1)}, u32[]{:S(2)}, u32[]{:S(2)}) collective-permute-start(bf16[6,128,128]{2,1,0:T(8,128)(2,1)S(1)} %get-tuple-element.91), channel_id=1, source_target_pairs={{0,28},{4,0},{8,4},{12,8},{16,12},{20,16},{24,20},{28,24},{1,29},{... | collective-permute-start | bytes 589832 | tf_op jit(solution)/shard_map/ppermute | solution.py:37
  99.0 7.0 %collective-permute-start.27 = (bf16[2,128,128]{2,1,0:T(8,128)(2,1)S(1)}, bf16[2,128,128]{2,1,0:T(8,128)(2,1)S(1)}, u32[]{:S(2)}, u32[]{:S(2)}) collective-permute-start(bf16[2,128,128]{2,1,0:T(8,128)(2,1)S(1)} %get-tuple-element.92), channel_id=1, source_target_pairs={{0,8},{4,12},{8,16},{12,20},{16,24},{20,28},{24,0},{28,4},{1,9},{5... | collective-permute-start | bytes 196616 | tf_op jit(solution)/shard_map/ppermute | solution.py:37
  99.5 6.4 %collective-permute-start.28 = (bf16[2,128,128]{2,1,0:T(8,128)(2,1)S(1)}, bf16[2,128,128]{2,1,0:T(8,128)(2,1)S(1)}, u32[]{:S(2)}, u32[]{:S(2)}) collective-permute-start(bf16[2,128,128]{2,1,0:T(8,128)(2,1)S(1)} %get-tuple-element.93), channel_id=1, source_target_pairs={{0,12},{4,16},{8,20},{12,24},{16,28},{20,0},{24,4},{28,8},{1,13},{... | collective-permute-start | bytes 196616 | tf_op jit(solution)/shard_map/ppermute | solution.py:37
  99.5 7.9 %collective-permute-start.29 = (bf16[2,128,128]{2,1,0:T(8,128)(2,1)S(1)}, bf16[2,128,128]{2,1,0:T(8,128)(2,1)S(1)}, u32[]{:S(2)}, u32[]{:S(2)}) collective-permute-start(bf16[2,128,128]{2,1,0:T(8,128)(2,1)S(1)} %get-tuple-element.94), channel_id=1, source_target_pairs={{0,16},{4,20},{8,24},{12,28},{16,0},{20,4},{24,8},{28,12},{1,17},{... | collective-permute-start | bytes 196616 | tf_op jit(solution)/shard_map/ppermute | solution.py:37
  105.9 3.8 %collective-permute-start.30 = (bf16[2,128,128]{2,1,0:T(8,128)(2,1)S(1)}, bf16[2,128,128]{2,1,0:T(8,128)(2,1)S(1)}, u32[]{:S(2)}, u32[]{:S(2)}) collective-permute-start(bf16[2,128,128]{2,1,0:T(8,128)(2,1)S(1)} %get-tuple-element.95), channel_id=1, source_target_pairs={{0,20},{4,24},{8,28},{12,0},{16,4},{20,8},{24,12},{28,16},{1,21},{... | collective-permute-start | bytes 196616 | tf_op jit(solution)/shard_map/ppermute | solution.py:37
  105.9 5.0 %collective-permute-start.31 = (bf16[2,128,128]{2,1,0:T(8,128)(2,1)S(1)}, bf16[2,128,128]{2,1,0:T(8,128)(2,1)S(1)}, u32[]{:S(2)}, u32[]{:S(2)}) collective-permute-start(bf16[2,128,128]{2,1,0:T(8,128)(2,1)S(1)} %get-tuple-element.96), channel_id=1, source_target_pairs={{0,24},{4,28},{8,0},{12,4},{16,8},{20,12},{24,16},{28,20},{1,25},{... | collective-permute-start | bytes 196616 | tf_op jit(solution)/shard_map/ppermute | solution.py:37
  113.9 8.5 %collective-permute-start.32 = (bf16[6,128,128]{2,1,0:T(8,128)(2,1)S(1)}, bf16[6,128,128]{2,1,0:T(8,128)(2,1)S(1)}, u32[]{:S(2)}, u32[]{:S(2)}) collective-permute-start(bf16[6,128,128]{2,1,0:T(8,128)(2,1)S(1)} %shard_map.94), channel_id=1, source_target_pairs={{0,3},{1,0},{2,1},{3,2},{4,7},{5,4},{6,5},{7,6},{8,11},{9,8},{10,9... | collective-permute-start | bytes 589832 | tf_op jit(solution)/shard_map/ppermute | solution.py:37
  114.7 12.8 %collective-permute-start.34 = (bf16[6,128,128]{2,1,0:T(8,128)(2,1)S(1)}, bf16[6,128,128]{2,1,0:T(8,128)(2,1)S(1)}, u32[]{:S(2)}, u32[]{:S(2)}) collective-permute-start(bf16[6,128,128]{2,1,0:T(8,128)(2,1)S(1)} %shard_map.95), channel_id=1, source_target_pairs={{0,1},{1,2},{2,3},{3,0},{4,5},{5,6},{6,7},{7,4},{8,9},{9,10},{10,1... | collective-permute-start | bytes 589832 | tf_op jit(solution)/shard_map/ppermute | solution.py:37
  117.1 18.7 %collective-permute-start.33 = (bf16[6,128,128]{2,1,0:T(8,128)(2,1)S(1)}, bf16[6,128,128]{2,1,0:T(8,128)(2,1)S(1)}, u32[]{:S(2)}, u32[]{:S(2)}) collective-permute-start(bf16[6,128,128]{2,1,0:T(8,128)(2,1)S(1)} %get-tuple-element.98), channel_id=1, source_target_pairs={{0,2},{1,3},{2,0},{3,1},{4,6},{5,7},{6,4},{7,5},{8,10},{9,11},{10,... | collective-permute-start | bytes 589832 | tf_op jit(solution)/shard_map/ppermute | solution.py:37
  138.4 14.0 %collective-permute-start.37 = (bf16[6,128,128]{2,1,0:T(8,128)(2,1)S(1)}, bf16[6,128,128]{2,1,0:T(8,128)(2,1)S(1)}, u32[]{:S(2)}, u32[]{:S(2)}) collective-permute-start(bf16[6,128,128]{2,1,0:T(8,128)(2,1)S(1)} %get-tuple-element.101), channel_id=1, source_target_pairs={{0,2},{1,3},{2,0},{3,1},{4,6},{5,7},{6,4},{7,5},{8,10},{9,11},{10,... | collective-permute-start | bytes 589832 | tf_op jit(solution)/shard_map/ppermute | solution.py:37
  138.9 14.7 %collective-permute-start.36 = (bf16[6,128,128]{2,1,0:T(8,128)(2,1)S(1)}, bf16[6,128,128]{2,1,0:T(8,128)(2,1)S(1)}, u32[]{:S(2)}, u32[]{:S(2)}) collective-permute-start(bf16[6,128,128]{2,1,0:T(8,128)(2,1)S(1)} %shard_map.98), channel_id=1, source_target_pairs={{0,1},{1,2},{2,3},{3,0},{4,5},{5,6},{6,7},{7,4},{8,9},{9,10},{10,1... | collective-permute-start | bytes 589832 | tf_op jit(solution)/shard_map/ppermute | solution.py:37
  140.1 14.8 %collective-permute-start.35 = (bf16[6,128,128]{2,1,0:T(8,128)(2,1)S(1)}, bf16[6,128,128]{2,1,0:T(8,128)(2,1)S(1)}, u32[]{:S(2)}, u32[]{:S(2)}) collective-permute-start(bf16[6,128,128]{2,1,0:T(8,128)(2,1)S(1)} %shard_map.97), channel_id=1, source_target_pairs={{0,3},{1,0},{2,1},{3,2},{4,7},{5,4},{6,5},{7,6},{8,11},{9,8},{10,9... | collective-permute-start | bytes 589832 | tf_op jit(solution)/shard_map/ppermute | solution.py:37
  156.1 15.0 %collective-permute-start.38 = (bf16[6,128,128]{2,1,0:T(8,128)(2,1)S(1)}, bf16[6,128,128]{2,1,0:T(8,128)(2,1)S(1)}, u32[]{:S(2)}, u32[]{:S(2)}) collective-permute-start(bf16[6,128,128]{2,1,0:T(8,128)(2,1)S(1)} %get-tuple-element.103), channel_id=1, source_target_pairs={{0,28},{4,0},{8,4},{12,8},{16,12},{20,16},{24,20},{28,24},{1,29},{... | collective-permute-start | bytes 589832 | tf_op jit(solution)/shard_map/ppermute | solution.py:37
  157.5 13.6 %collective-permute-start.39 = (bf16[6,128,128]{2,1,0:T(8,128)(2,1)S(1)}, bf16[6,128,128]{2,1,0:T(8,128)(2,1)S(1)}, u32[]{:S(2)}, u32[]{:S(2)}) collective-permute-start(bf16[6,128,128]{2,1,0:T(8,128)(2,1)S(1)} %get-tuple-element.104), channel_id=1, source_target_pairs={{0,4},{4,8},{8,12},{12,16},{16,20},{20,24},{24,28},{28,0},{1,5},{5... | collective-permute-start | bytes 589832 | tf_op jit(solution)/shard_map/ppermute | solution.py:37
  157.5 6.7 %collective-permute-start.40 = (bf16[2,128,128]{2,1,0:T(8,128)(2,1)S(1)}, bf16[2,128,128]{2,1,0:T(8,128)(2,1)S(1)}, u32[]{:S(2)}, u32[]{:S(2)}) collective-permute-start(bf16[2,128,128]{2,1,0:T(8,128)(2,1)S(1)} %get-tuple-element.105), channel_id=1, source_target_pairs={{0,8},{4,12},{8,16},{12,20},{16,24},{20,28},{24,0},{28,4},{1,9},{5... | collective-permute-start | bytes 196616 | tf_op jit(solution)/shard_map/ppermute | solution.py:37
  158.4 8.3 %collective-permute-start.41 = (bf16[2,128,128]{2,1,0:T(8,128)(2,1)S(1)}, bf16[2,128,128]{2,1,0:T(8,128)(2,1)S(1)}, u32[]{:S(2)}, u32[]{:S(2)}) collective-permute-start(bf16[2,128,128]{2,1,0:T(8,128)(2,1)S(1)} %get-tuple-element.106), channel_id=1, source_target_pairs={{0,12},{4,16},{8,20},{12,24},{16,28},{20,0},{24,4},{28,8},{1,13},{... | collective-permute-start | bytes 196616 | tf_op jit(solution)/shard_map/ppermute | solution.py:37
  159.9 7.8 %collective-permute-start.42 = (bf16[2,128,128]{2,1,0:T(8,128)(2,1)S(1)}, bf16[2,128,128]{2,1,0:T(8,128)(2,1)S(1)}, u32[]{:S(2)}, u32[]{:S(2)}) collective-permute-start(bf16[2,128,128]{2,1,0:T(8,128)(2,1)S(1)} %get-tuple-element.107), channel_id=1, source_target_pairs={{0,16},{4,20},{8,24},{12,28},{16,0},{20,4},{24,8},{28,12},{1,17},{... | collective-permute-start | bytes 196616 | tf_op jit(solution)/shard_map/ppermute | solution.py:37
  164.2 4.5 %collective-permute-start.43 = (bf16[2,128,128]{2,1,0:T(8,128)(2,1)S(1)}, bf16[2,128,128]{2,1,0:T(8,128)(2,1)S(1)}, u32[]{:S(2)}, u32[]{:S(2)}) collective-permute-start(bf16[2,128,128]{2,1,0:T(8,128)(2,1)S(1)} %get-tuple-element.108), channel_id=1, source_target_pairs={{0,20},{4,24},{8,28},{12,0},{16,4},{20,8},{24,12},{28,16},{1,21},{... | collective-permute-start | bytes 196616 | tf_op jit(solution)/shard_map/ppermute | solution.py:37
  166.8 4.4 %collective-permute-start.44 = (bf16[2,128,128]{2,1,0:T(8,128)(2,1)S(1)}, bf16[2,128,128]{2,1,0:T(8,128)(2,1)S(1)}, u32[]{:S(2)}, u32[]{:S(2)}) collective-permute-start(bf16[2,128,128]{2,1,0:T(8,128)(2,1)S(1)} %get-tuple-element.109), channel_id=1, source_target_pairs={{0,24},{4,28},{8,0},{12,4},{16,8},{20,12},{24,16},{28,20},{1,25},{... | collective-permute-start | bytes 196616 | tf_op jit(solution)/shard_map/ppermute | solution.py:37

commit v2 on v1

--- a/solution.py
+++ b/solution.py
@@ -18,6 +18,7 @@
 PARAMS = pltpu.CompilerParams(vmem_limit_bytes=16 << 20)
 F32, BF16 = jnp.float32, jnp.bfloat16
 MOST_SHIFTS = 8
+CHUNKS = 2
 
 
 def in_smem(value):
@@ -52,7 +53,8 @@
         self.table = self.far_base + self.peers * self.far
         self.share = self.rows // self.states
         self.shifts = range(2, self.peers - 1) if self.peers <= MOST_SHIFTS else None
-        self.order = sorted(range(1, self.states), key=lambda p: abs(2 * p - self.states))
+        self.chunks = CHUNKS if self.share % CHUNKS == 0 else 1
+        self.group = self.share // self.chunks
 
     def blocks(self, count, dtype):
         return pltpu.VMEM((count, self.size, self.cols), dtype)
@@ -75,8 +77,9 @@
         flops = 2 * matmul_blocks * self.size * self.size * self.cols
         return pl.CostEstimate(flops=flops, bytes_accessed=nbytes, transcendentals=0)
 
-    def rows_of(self, p):
-        return lax.rem(lax.axis_index("state") - p + self.states, self.states) * self.share
+    def rows_of(self, p, chunk):
+        share = lax.rem(lax.axis_index("state") - p + self.states, self.states)
+        return share * self.share + chunk * self.group
 
 
 def call(kernel, out_shape, in_specs, args, cost, scratch=(), aliases={}, out_specs=None):
@@ -154,21 +157,25 @@
     return out[0], list(out[1 : 1 + n_ask]), out[1 + n_ask :]
 
 
-def forward(plan, p, sources, kern, inputs, table, first_time):
-    share, degree, near, rows = plan.share, plan.degree, plan.near, plan.rows
+def forward(plan, chunk, sources, kern, inputs, table, first_time):
+    group, degree, near, rows = plan.group, plan.degree, plan.near, plan.rows
+    states = plan.states
     gathers = table is None
     n_in = len(inputs) if gathers else 1
 
     def kernel(src, kern_ref, *rest):
         ins, outs = rest[:n_in], rest[n_in:]
-        out, tbl = outs[0], outs[1] if gathers else ins[0]
-        first = plan.rows_of(p)
+        tbl = outs[states] if gathers else ins[0]
+        firsts = [plan.rows_of(p, chunk) for p in range(states)]
         held = kern_ref
         if first_time:
             held, sem = outs[-2:]
             loads = [
-                pltpu.make_async_copy(kern_ref.at[first + g], held.at[g], sem.at[g])
-                for g in range(share)
+                pltpu.make_async_copy(
+                    kern_ref.at[firsts[p] + g], held.at[p * group + g], sem.at[p * group + g]
+                )
+                for p in range(states)
+                for g in range(group)
             ]
             for load in loads:
                 load.start()
@@ -182,28 +189,29 @@
                 tbl[near + t] = own_ref[t]
             for slot, i, t in plan.far_slots(-1):
                 tbl[plan.far_base + slot] = far_refs[i][t]
-        for g in range(share):
-            if first_time:
-                loads[g].wait()
-            row = first + g
-            lhs = jnp.concatenate([held[g, k] for k in range(degree)], axis=1)
-            rhs = jnp.concatenate([tbl[src[row, k]] for k in range(degree)], axis=0)
-            out[g] = jnp.dot(lhs, rhs, preferred_element_type=F32).astype(BF16)
-
-    out_shape = [plan.blocks(share, BF16)]
+        for p in range(states):
+            for g in range(group):
+                at, row = p * group + g, firsts[p] + g
+                if first_time:
+                    loads[at].wait()
+                lhs = jnp.concatenate([held[at, k] for k in range(degree)], axis=1)
+                rhs = jnp.concatenate([tbl[src[row, k]] for k in range(degree)], axis=0)
+                outs[p][g] = jnp.dot(lhs, rhs, preferred_element_type=F32).astype(BF16)
+
+    out_shape = [plan.blocks(group, BF16)] * states
     if gathers:
         out_shape.append(plan.blocks(plan.table, BF16))
     if first_time:
-        out_shape.append(pltpu.VMEM((share, *kern.shape[1:]), BF16))
+        out_shape.append(pltpu.VMEM((states * group, *kern.shape[1:]), BF16))
     out = call(
         kernel,
         out_shape,
         [INDEX, HBM if first_time else VMEM] + [VMEM] * n_in,
         [sources, kern] + (list(inputs) if gathers else [table]),
-        plan.cost(share * degree, 4 << 20),
-        [pltpu.SemaphoreType.DMA((share,))] if first_time else (),
-    )
-    return out[0], out[1] if gathers else table, out[-1] if first_time else kern
+        plan.cost(states * group * degree, 6 << 20),
+        [pltpu.SemaphoreType.DMA((states * group,))] if first_time else (),
+    )
+    return out[:states], out[states] if gathers else table, out[-1] if first_time else kern
 
 
 def turned(plan, k_ref, p):
@@ -211,84 +219,81 @@
     return k_ref[:, pl.ds(pl.multiple_of(at, plan.cols), plan.cols)]
 
 
-def mix(plan, pieces, state_kernel, mu, p_first, final):
-    states, share, size = plan.states, plan.share, plan.size
+def mix(plan, chunk, pieces, state_kernel, mu, u_so_far, final):
+    states, group, size, cols = plan.states, plan.group, plan.size, plan.cols
+    passed = final and u_so_far is not None
 
     def kernel(*refs):
         a_refs, (k_ref, mu_ref), rest = refs[:states], refs[states : states + 2], refs[states + 2 :]
-        rounded, out = rest[:2]
-        k_in = jnp.concatenate([turned(plan, k_ref, p) for p in range(states)], axis=1)
-        k_out = turned(plan, k_ref, p_first)
+        if passed:
+            rest = rest[1:]
+        outs, rest = rest[:states], rest[states:]
+        k_all = jnp.concatenate([turned(plan, k_ref, p) for p in range(states)], axis=1)
         copies = []
-        for g in range(share):
+        for g in range(group):
             a = jnp.concatenate([ref[g] for ref in a_refs], axis=1)
-            mixed = lax.dot_general(a, k_in, (((1,), (1,)), ((), ())), preferred_element_type=F32)
-            u = mu_ref[pl.ds(g * size, size), :] / mixed
+            mixed = lax.dot_general(a, k_all, (((1,), (1,)), ((), ())), preferred_element_type=F32)
+            at = (chunk * group + g) * size
+            u = mu_ref[pl.ds(at, size), :] / mixed
             if final:
-                u_ref, u_buf, sem = rest[2:]
+                u_ref, u_buf, sem = rest
                 u_buf[g] = u
-                copy = pltpu.make_async_copy(
-                    u_buf.at[g], u_ref.at[pl.ds(g * size, size), :], sem.at[g]
-                )
+                copy = pltpu.make_async_copy(u_buf.at[g], u_ref.at[pl.ds(at, size), :], sem.at[g])
                 copy.start()
                 copies.append(copy)
-            u = u.astype(BF16)
-            rounded[g] = u
-            out[g] = jnp.dot(u, k_out, preferred_element_type=F32).astype(BF16)
+            b = jnp.dot(u.astype(BF16), k_all, preferred_element_type=F32).astype(BF16)
+            for p in range(states):
+                outs[p][g] = b[:, p * cols : (p + 1) * cols]
         for copy in copies:
             copy.wait()
 
-    width = mu.shape[1]
-    out_shape = [pltpu.VMEM((share, size, width), BF16), plan.blocks(share, BF16)]
-    out_specs, scratch = [VMEM] * 2, []
+    args, in_specs = [*pieces, state_kernel, mu], [VMEM] * (states + 2)
+    out_shape = [plan.blocks(group, BF16)] * states
+    out_specs, scratch, aliases = [VMEM] * states, [], {}
     if final:
-        out_shape.append(jax.ShapeDtypeStruct(mu.shape, F32))
-        out_specs.append(ANY)
-        scratch = [pltpu.VMEM((share, size, width), F32), pltpu.SemaphoreType.DMA((share,))]
-    return call(
+        out_shape = out_shape + [jax.ShapeDtypeStruct(mu.shape, F32)]
+        out_specs = out_specs + [ANY]
+        scratch = [pltpu.VMEM((group, size, mu.shape[1]), F32), pltpu.SemaphoreType.DMA((group,))]
+        if passed:
+            aliases = {len(args): states}
+            args.append(u_so_far)
+            in_specs.append(ANY)
+    out = call(
         kernel,
         out_shape,
-        [VMEM] * (states + 2),
-        [*pieces, state_kernel, mu],
-        plan.cost(share * states * (states + 1), 4 << 20),
+        in_specs,
+        args,
+        plan.cost(2 * group * states * states, 3 << 20),
         scratch,
-        out_specs=out_specs,
-    )
-
-
-def mix_back(plan, p, rounded, state_kernel):
-    def kernel(u_ref, k_ref, out):
-        k_out = turned(plan, k_ref, p)
-        for g in range(plan.share):
-            out[g] = jnp.dot(u_ref[g], k_out, preferred_element_type=F32).astype(BF16)
-
-    return call(
-        kernel,
-        [plan.blocks(plan.share, BF16)],
-        [VMEM] * 2,
-        [rounded, state_kernel],
-        plan.cost(plan.share * plan.states, 1 << 20),
-    )[0]
-
-
-def backward(plan, p, sources, kern, piece, so_far, last):
-    share, degree, near, rows = plan.share, plan.degree, plan.near, plan.rows
+        aliases,
+        out_specs,
+    )
+    return out[:states], out[states] if final else None
+
+
+def backward(plan, chunk, sources, kern, pieces, so_far):
+    group, degree, near, rows = plan.group, plan.degree, plan.near, plan.rows
+    states = plan.states
     n_acc = 0 if so_far is None else 1
-
-    def kernel(src, kern_ref, b_ref, *rest):
-        rest = rest[n_acc:]
+    last = chunk == plan.chunks - 1
+
+    def kernel(src, kern_ref, *rest):
+        b_refs, rest = rest[:states], rest[states + n_acc :]
         acc = rest[-1]
         if not n_acc:
             acc[...] = jnp.zeros_like(acc)
-        first = plan.rows_of(p)
-        for g in range(share):
-            row = first + g
-            b = b_ref[g]
-            for k in range(degree):
-                part = lax.dot_general(
-                    kern_ref[g, k], b, (((0,), (0,)), ((), ())), preferred_element_type=F32
-                )
-                acc[src[row, k]] += part
+        for p in range(states):
+            first = plan.rows_of(p, chunk)
+            for g in range(group):
+                b = b_refs[p][g]
+                for k in range(degree):
+                    part = lax.dot_general(
+                        kern_ref[p * group + g, k],
+                        b,
+                        (((0,), (0,)), ((), ())),
+                        preferred_element_type=F32,
+                    )
+                    acc[src[first + g, k]] += part
         if not last:
             return
         own, left, right, far = rest[0], rest[1], rest[2], rest[3:-1]
@@ -306,11 +311,11 @@
     return call(
         kernel,
         out_shape + [plan.blocks(plan.table, F32)],
-        [INDEX] + [VMEM] * (2 + n_acc),
-        [sources, kern, piece] + ([] if so_far is None else [so_far]),
-        plan.cost(share * degree, 5 << 20),
+        [INDEX] + [VMEM] * (1 + states + n_acc),
+        [sources, kern, *pieces] + ([] if so_far is None else [so_far]),
+        plan.cost(states * group * degree, 10 << 20),
         (),
-        {3: len(out_shape)} if n_acc else {},
+        {2 + states: len(out_shape)} if n_acc else {},
     )
 
 
@@ -404,24 +409,19 @@
     from_left, from_right = send_near(head, tail)
     far = send_far(plan, far)
     inputs, table = [own, from_left, from_right, *far], None
-    pieces = [None] * plan.states
-    for p in [*plan.order, 0]:
-        part, table, kept[p] = forward(
-            plan, p, sources, kern if first_time else kept[p], inputs, table, first_time
+    spread, returned = [], []
+    for c in range(plan.chunks):
+        parts, table, kept[c] = forward(
+            plan, c, sources, kern if first_time else kept[c], inputs, table, first_time
         )
-        pieces[p] = shifted(part, "state", -p) if p else part
-    out = mix(plan, pieces, state_kernel, mu, plan.order[0], final)
-    rounded, part, potential_u = out[0], out[1], out[-1]
-    pieces = [None] * plan.states
-    for p in [*plan.order, 0]:
-        if p != plan.order[0]:
-            part = mix_back(plan, p, rounded, state_kernel)
-        pieces[p] = shifted(part, "state", p) if p else part
+        spread.append([parts[0]] + [shifted(parts[p], "state", -p) for p in range(1, plan.states)])
+    potential_u = None
+    for c in range(plan.chunks):
+        parts, potential_u = mix(plan, c, spread[c], state_kernel, mu, potential_u, final)
+        returned.append([parts[0]] + [shifted(parts[p], "state", p) for p in range(1, plan.states)])
     total = None
-    for p in [0, *plan.order]:
-        out = backward(
-            plan, p, sources, kept[p], pieces[p], total, p == plan.order[-1]
-        )
+    for c in range(plan.chunks):
+        out = backward(plan, c, sources, kept[c], returned[c], total)
         total = out[-1]
     own_part, to_left, to_right, to_far = out[0], out[1], out[2], out[3:-1]
     from_left, from_right = send_near(to_left, to_right)
@@ -434,7 +434,7 @@
     plan = Plan(kern_blocks, start_v)
     shape = (plan.rows, plan.size, plan.cols)
     nu = nu.reshape(shape)
-    kept = [None] * plan.states
+    kept = [None] * plan.chunks
     for sweep in range(ITERS):
         if sweep == 0:
             sources, asks, (own, head, tail) = begin(plan, kern_cols, start_v.reshape(shape))

time: 174 us -> 162 us (0.931)
  waiting for transfers between devices: 78.3 us -> 53.6 us
  starting transfers between devices: 55.2 us -> 72.3 us
  Pallas kernels: 38 us -> 34.3 us
    ppermute x45 -> x57, waiting for transfers between devices: 78.3 us -> 53.6 us  [shifted(): lax.ppermute(value, axis, [(i, (i + steps) % count) for i in range(count)])]
    ppermute x45 -> x57, starting transfers between devices: 55.2 us -> 72.3 us  [shifted(): lax.ppermute(value, axis, [(i, (i + steps) % count) for i in range(count)])]
    pallas_call x28 -> x16, Pallas kernels: 38 us -> 34.3 us  [call(): pl.pallas_call(kernel, out_shape=out_shape, in_specs=in_specs, out_specs=...]
  transfers between devices with their start and end apart: 45 -> 57, of which waited for: 27 -> 25; matrix products, arithmetic and copies ran while one was open for 0% -> 0% of each run, Pallas kernels for 8% -> 11%
where the time goes in v2:
time: 162 us
  starting transfers between devices  72.3 us (45%)
  waiting for transfers between devices  53.6 us (33%)
  Pallas kernels  34.3 us (21%)
    ppermute x57, starting transfers between devices, shifted(): lax.ppermute(value, axis, [(i, (i + steps) % count) for i in range(count)])  72.3 us
    ppermute x57, waiting for transfers between devices, shifted(): lax.ppermute(value, axis, [(i, (i + steps) % count) for i in range(count)])  53.6 us
    pallas_call x16, Pallas kernels, call(): pl.pallas_call(kernel, out_shape=out_shape, in_specs=in_specs, out_specs=...  34.3 us
  transfers between devices with their start and end apart: 57, of which 25 were waited for; matrix products, arithmetic and copies ran while one was open for 0% of the time, Pallas kernels for 11%

profile of v2, /device:TPU:0, one launch (start us, length us, event | category | flops | bytes accessed | tf_op | source)
XLA Modules:
  0.0 161.9 jit_solution(6639389855818908954)
XLA Ops:
  1.4 2.8 %shard_map.77 = (s32[24,16]{1,0:T(8,128)S(4)}, s32[2]{0:T(128)S(1)}, s32[2]{0:T(128)S(1)}, s32[2]{0:T(128)S(1)}, s32[2]{0:T(128)S(1)}, /*index=5*/s32[2]{0:T(128...) custom-call(s32[24,16]{1,0:T(8,128)S(1)} %copy.11.cols_ref, ...), custom_call_target="tpu_custom_call" | custom-call | bytes 3145728 | tf_op jit(solution)/shard_map/pallas_call | solution.py:89
  4.7 2.9 %collective-permute-start.1 = (bf16[6,128,128]{2,1,0:T(8,128)(2,1)S(1)}, bf16[6,128,128]{2,1,0:T(8,128)(2,1)S(1)}, u32[]{:S(2)}, u32[]{:S(2)}) collective-permute-start(bf16[6,128,128]{2,1,0:T(8,128)(2,1)S(1)} %get-tuple-element.81), channel_id=1, source_target_pairs={{0,28},{4,0},{8,4},{12,8},{16,12},{20,16},{24,20},{28,24},{1,29},{... | collective-permute-start | bytes 589832 | tf_op jit(solution)/shard_map/ppermute | solution.py:38
  7.7 2.2 %collective-permute-start.2 = (s32[2]{0:T(128)S(1)}, s32[2]{0:T(128)S(1)}, u32[]{:S(2)}, u32[]{:S(2)}) collective-permute-start(s32[2]{0:T(128)S(1)} %get-tuple-element.82), channel_id=1, source_target_pairs={{0,24},{4,28},{8,0},{12,4},{16,8},{20,12},{24,16},{28,20},{1,25},{... | collective-permute-start | bytes 32 | tf_op jit(solution)/shard_map/ppermute | solution.py:38
  10.4 3.5 %collective-permute-done.2.rest_0_.rest_5_ = s32[2]{0:T(128)S(1)} collective-permute-done((s32[2]{0:T(128)S(1)}, s32[2]{0:T(128)S(1)}, u32[]{:S(2)}, u32[]{:S(2)}) %collective-permute-start.2) | collective-permute-done | bytes 40 | tf_op jit(solution)/shard_map/ppermute | solution.py:38
  13.9 1.5 collective-permute-start.6
  15.4 1.5 collective-permute-done.5.rest_3_.rest_8_
  16.9 1.5 collective-permute-done.6.rest_4_.rest_9_
  19.6 1.2 collective-permute-start.8
  21.1 3.2 %collective-permute-done.7.rest_3_ = bf16[2,128,128]{2,1,0:T(8,128)(2,1)S(1)} collective-permute-done((bf16[2,128,128]{2,1,0:T(8,128)(2,1)S(1)}, bf16[2,128,128]{2,1,0:T(8,128)(2,1)S(1)}, u32[]{:S(2)}, u32[]{:S(2)}) %collective-permute-start.7) | collective-permute-done | bytes 65568 | tf_op jit(solution)/shard_map/ppermute | solution.py:38
  24.3 1.4 collective-permute-start.11
  26.1 2.0 %collective-permute-done.10.rest_6_ = bf16[2,128,128]{2,1,0:T(8,128)(2,1)S(1)} collective-permute-done((bf16[2,128,128]{2,1,0:T(8,128)(2,1)S(1)}, bf16[2,128,128]{2,1,0:T(8,128)(2,1)S(1)}, u32[]{:S(2)}, u32[]{:S(2)}) %collective-permute-start.10) | collective-permute-done | bytes 65568 | tf_op jit(solution)/shard_map/ppermute | solution.py:38
  28.1 1.2 collective-permute-done.11.rest_7_
  29.3 4.8 %shard_map.79 = (bf16[3,128,128]{2,1,0:T(8,128)(2,1)S(1)}, bf16[3,128,128]{2,1,0:T(8,128)(2,1)S(1)}, bf16[3,128,128]{2,1,0:T(8,128)(2,1)S(1)}, bf16[3,128,128]{2...) custom-call(s32[24,16]{1,0:T(8,128)S(4)} %get-tuple-element.78.src, ...), custom_call_target="tpu_custom_call" | custom-call | flops 805306368 | bytes 6291456 | tf_op jit(solution)/shard_map/pallas_call | solution.py:89
  34.1 3.6 %collective-permute-start.18 = (bf16[3,128,128]{2,1,0:T(8,128)(2,1)S(1)}, bf16[3,128,128]{2,1,0:T(8,128)(2,1)S(1)}, u32[]{:S(2)}, u32[]{:S(2)}) collective-permute-start(bf16[3,128,128]{2,1,0:T(8,128)(2,1)S(1)} %get-tuple-element.104), channel_id=1, source_target_pairs={{0,3},{1,0},{2,1},{3,2},{4,7},{5,4},{6,5},{7,6},{8,11},{9,8},{10,9... | collective-permute-start | bytes 294920 | tf_op jit(solution)/shard_map/ppermute | solution.py:38
  37.7 1.0 collective-permute-start.20
  38.7 4.9 %shard_map.80 = (bf16[3,128,128]{2,1,0:T(8,128)(2,1)S(1)}, bf16[3,128,128]{2,1,0:T(8,128)(2,1)S(1)}, bf16[3,128,128]{2,1,0:T(8,128)(2,1)S(1)}, bf16[3,128,128]{2...) custom-call(s32[24,16]{1,0:T(8,128)S(4)} %get-tuple-element.78.src, bf16[24,16,128,128]{3,2,1,0:T(8,128)(2,1)} %kern_ref.3, ...), custom_call_target="tpu_custom_call" | custom-call | flops 805306368 | bytes 6291456 | tf_op jit(solution)/shard_map/pallas_call | solution.py:89
  43.7 2.9 %collective-permute-start.12 = (bf16[3,128,128]{2,1,0:T(8,128)(2,1)S(1)}, bf16[3,128,128]{2,1,0:T(8,128)(2,1)S(1)}, u32[]{:S(2)}, u32[]{:S(2)}) collective-permute-start(bf16[3,128,128]{2,1,0:T(8,128)(2,1)S(1)} %get-tuple-element.96), channel_id=1, source_target_pairs={{0,3},{1,0},{2,1},{3,2},{4,7},{5,4},{6,5},{7,6},{8,11},{9,8},{10,9... | collective-permute-start | bytes 294920 | tf_op jit(solution)/shard_map/ppermute | solution.py:38
  46.5 1.1 collective-permute-start.13
  47.7 1.2 shard_map.82
  48.9 2.4 %collective-permute-start.21 = (bf16[3,128,128]{2,1,0:T(8,128)(2,1)S(1)}, bf16[3,128,128]{2,1,0:T(8,128)(2,1)S(1)}, u32[]{:S(2)}, u32[]{:S(2)}) collective-permute-start(bf16[3,128,128]{2,1,0:T(8,128)(2,1)S(1)} %get-tuple-element.108), channel_id=1, source_target_pairs={{0,1},{1,2},{2,3},{3,0},{4,5},{5,6},{6,7},{7,4},{8,9},{9,10},{10,1... | collective-permute-start | bytes 294920 | tf_op jit(solution)/shard_map/ppermute | solution.py:38
  51.3 2.0 %collective-permute-start.22 = (bf16[3,128,128]{2,1,0:T(8,128)(2,1)S(1)}, bf16[3,128,128]{2,1,0:T(8,128)(2,1)S(1)}, u32[]{:S(2)}, u32[]{:S(2)}) collective-permute-start(bf16[3,128,128]{2,1,0:T(8,128)(2,1)S(1)} %get-tuple-element.109), channel_id=1, source_target_pairs={{0,2},{1,3},{2,0},{3,1},{4,6},{5,7},{6,4},{7,5},{8,10},{9,11},{10,... | collective-permute-start | bytes 294920 | tf_op jit(solution)/shard_map/ppermute | solution.py:38
  54.0 7.3 %collective-permute-done.13.refs_2_ = bf16[3,128,128]{2,1,0:T(8,128)(2,1)S(1)} collective-permute-done((bf16[3,128,128]{2,1,0:T(8,128)(2,1)S(1)}, bf16[3,128,128]{2,1,0:T(8,128)(2,1)S(1)}, u32[]{:S(2)}, u32[]{:S(2)}) %collective-permute-start.13) | collective-permute-done | bytes 98336 | tf_op jit(solution)/shard_map/ppermute | solution.py:38
  61.3 1.2 shard_map.81
  62.7 3.7 %collective-permute-start.17 = (bf16[3,128,128]{2,1,0:T(8,128)(2,1)S(1)}, bf16[3,128,128]{2,1,0:T(8,128)(2,1)S(1)}, u32[]{:S(2)}, u32[]{:S(2)}) collective-permute-start(bf16[3,128,128]{2,1,0:T(8,128)(2,1)S(1)} %get-tuple-element.102), channel_id=1, source_target_pairs={{0,3},{1,0},{2,1},{3,2},{4,7},{5,4},{6,5},{7,6},{8,11},{9,8},{10,9... | collective-permute-start | bytes 294920 | tf_op jit(solution)/shard_map/ppermute | solution.py:38
  66.4 2.1 %shard_map.83.rest_4_ = f32[52,128,128]{2,1,0:T(8,128)S(1)} custom-call(s32[24,16]{1,0:T(8,128)S(4)} %get-tuple-element.78.src, bf16[12,16,128,128]{3,2,1,0:T(8,128)(2,1)S(1)} %get-tuple-element.94.kern_ref, bf16[3,128,128]{2,1,0:T(8,128)(2,1)S(1)} %get-tuple-element.107.rest_0_, bf16[3,128,128]{2,1,0:T(8,128)(2,1)S(1)} %collective-permute-done.21.rest_1_, ...), custom_call_target="tpu_custom_call" | custom-call | flops 805306368 | bytes 10485760 | tf_op jit(solution)/shard_map/pallas_call | solution.py:89
  68.6 0.9 collective-permute-done.15.rest_1_
  69.5 2.0 %collective-permute-done.16.rest_2_ = bf16[3,128,128]{2,1,0:T(8,128)(2,1)S(1)} collective-permute-done((bf16[3,128,128]{2,1,0:T(8,128)(2,1)S(1)}, bf16[3,128,128]{2,1,0:T(8,128)(2,1)S(1)}, u32[]{:S(2)}, u32[]{:S(2)}) %collective-permute-start.16) | collective-permute-done | bytes 98336 | tf_op jit(solution)/shard_map/ppermute | solution.py:38
  71.5 2.1 %shard_map.84 = (bf16[24,128,128]{2,1,0:T(8,128)(2,1)S(1)}, bf16[6,128,128]{2,1,0:T(8,128)(2,1)S(1)}, bf16[6,128,128]{2,1,0:T(8,128)(2,1)S(1)}, bf16[2,128,128]{...) custom-call(s32[24,16]{1,0:T(8,128)S(4)} %get-tuple-element.78.src, ...), custom_call_target="tpu_custom_call", output_to_operand_aliasing={{8}: (6, {})} | custom-call | flops 805306368 | bytes 10485760 | tf_op jit(solution)/shard_map/pallas_call | solution.py:89
  74.2 1.2 collective-permute-start.26
  75.4 1.9 %collective-permute-start.27 = (bf16[2,128,128]{2,1,0:T(8,128)(2,1)S(1)}, bf16[2,128,128]{2,1,0:T(8,128)(2,1)S(1)}, u32[]{:S(2)}, u32[]{:S(2)}) collective-permute-start(bf16[2,128,128]{2,1,0:T(8,128)(2,1)S(1)} %get-tuple-element.115), channel_id=1, source_target_pairs={{0,12},{4,16},{8,20},{12,24},{16,28},{20,0},{24,4},{28,8},{1,13},{... | collective-permute-start | bytes 196616 | tf_op jit(solution)/shard_map/ppermute | solution.py:38
  77.9 4.4 %collective-permute-done.26.rest_0_ = bf16[2,128,128]{2,1,0:T(8,128)(2,1)S(1)} collective-permute-done((bf16[2,128,128]{2,1,0:T(8,128)(2,1)S(1)}, bf16[2,128,128]{2,1,0:T(8,128)(2,1)S(1)}, u32[]{:S(2)}, u32[]{:S(2)}) %collective-permute-start.26) | collective-permute-done | bytes 65568 | tf_op jit(solution)/shard_map/ppermute | solution.py:38
  82.2 1.5 collective-permute-start.29
  84.6 1.4 collective-permute-done.29.rest_3_
  85.9 2.1 %collective-permute-done.30.rest_4_ = bf16[2,128,128]{2,1,0:T(8,128)(2,1)S(1)} collective-permute-done((bf16[2,128,128]{2,1,0:T(8,128)(2,1)S(1)}, bf16[2,128,128]{2,1,0:T(8,128)(2,1)S(1)}, u32[]{:S(2)}, u32[]{:S(2)}) %collective-permute-start.30) | collective-permute-done | bytes 65568 | tf_op jit(solution)/shard_map/ppermute | solution.py:38
  88.0 1.0 shard_map.85
  89.1 2.6 %collective-permute-start.32 = (bf16[6,128,128]{2,1,0:T(8,128)(2,1)S(1)}, bf16[6,128,128]{2,1,0:T(8,128)(2,1)S(1)}, u32[]{:S(2)}, u32[]{:S(2)}) collective-permute-start(bf16[6,128,128]{2,1,0:T(8,128)(2,1)S(1)} %get-tuple-element.121), channel_id=1, source_target_pairs={{0,28},{4,0},{8,4},{12,8},{16,12},{20,16},{24,20},{28,24},{1,29},{... | collective-permute-start | bytes 589832 | tf_op jit(solution)/shard_map/ppermute | solution.py:38
  92.2 1.2 collective-permute-start.35
  93.3 5.4 %collective-permute-done.33.rest_3_ = bf16[2,128,128]{2,1,0:T(8,128)(2,1)S(1)} collective-permute-done((bf16[2,128,128]{2,1,0:T(8,128)(2,1)S(1)}, bf16[2,128,128]{2,1,0:T(8,128)(2,1)S(1)}, u32[]{:S(2)}, u32[]{:S(2)}) %collective-permute-start.33) | collective-permute-done | bytes 65568 | tf_op jit(solution)/shard_map/ppermute | solution.py:38
  98.7 1.4 collective-permute-start.37
  100.2 2.3 %collective-permute-done.36.rest_6_ = bf16[2,128,128]{2,1,0:T(8,128)(2,1)S(1)} collective-permute-done((bf16[2,128,128]{2,1,0:T(8,128)(2,1)S(1)}, bf16[2,128,128]{2,1,0:T(8,128)(2,1)S(1)}, u32[]{:S(2)}, u32[]{:S(2)}) %collective-permute-start.36) | collective-permute-done | bytes 65568 | tf_op jit(solution)/shard_map/ppermute | solution.py:38
  102.5 1.2 collective-permute-done.37.rest_7_
  103.7 1.9 %shard_map.86 = (bf16[3,128,128]{2,1,0:T(8,128)(2,1)S(1)}, bf16[3,128,128]{2,1,0:T(8,128)(2,1)S(1)}, bf16[3,128,128]{2,1,0:T(8,128)(2,1)S(1)}, bf16[3,128,128]{2,1,0:T(8,128)(2,1)S(1)}, bf16[52,128,128]{2,1,0:T(8,128)(2,1)S(1)}) custom-call(s32[24,16]{1,0:T(8,128)S(4)} %get-tuple-element.78.src, bf16[12,16,128,128]{3,2,1,0:T(8,128)(2,1)S(1)} %get-tuple-element.94.kern_ref, ...), custom_call_target="tpu_custom_call" | custom-call | flops 805306368 | bytes 6291456 | tf_op jit(solution)/shard_map/pallas_call | solution.py:89
  105.6 3.8 %collective-permute-start.41 = (bf16[3,128,128]{2,1,0:T(8,128)(2,1)S(1)}, bf16[3,128,128]{2,1,0:T(8,128)(2,1)S(1)}, u32[]{:S(2)}, u32[]{:S(2)}) collective-permute-start(bf16[3,128,128]{2,1,0:T(8,128)(2,1)S(1)} %get-tuple-element.133), channel_id=1, source_target_pairs={{0,3},{1,0},{2,1},{3,2},{4,7},{5,4},{6,5},{7,6},{8,11},{9,8},{10,9... | collective-permute-start | bytes 294920 | tf_op jit(solution)/shard_map/ppermute | solution.py:38
  110.1 1.8 %shard_map.87 = (bf16[3,128,128]{2,1,0:T(8,128)(2,1)S(1)}, bf16[3,128,128]{2,1,0:T(8,128)(2,1)S(1)}, bf16[3,128,128]{2,1,0:T(8,128)(2,1)S(1)}, bf16[3,128,128]{2,1,0:T(8,128)(2,1)S(1)}) custom-call(s32[24,16]{1,0:T(8,128)S(4)} %get-tuple-element.78.src, bf16[12,16,128,128]{3,2,1,0:T(8,128)(2,1)S(1)} %get-tuple-element.93.kern_ref, ...), custom_call_target="tpu_custom_call" | custom-call | flops 805306368 | bytes 6291456 | tf_op jit(solution)/shard_map/pallas_call | solution.py:89
  111.9 3.2 %collective-permute-start.38 = (bf16[3,128,128]{2,1,0:T(8,128)(2,1)S(1)}, bf16[3,128,128]{2,1,0:T(8,128)(2,1)S(1)}, u32[]{:S(2)}, u32[]{:S(2)}) collective-permute-start(bf16[3,128,128]{2,1,0:T(8,128)(2,1)S(1)} %get-tuple-element.129), channel_id=1, source_target_pairs={{0,3},{1,0},{2,1},{3,2},{4,7},{5,4},{6,5},{7,6},{8,11},{9,8},{10,9... | collective-permute-start | bytes 294920 | tf_op jit(solution)/shard_map/ppermute | solution.py:38
  115.1 1.1 collective-permute-start.39
  116.2 3.3 %collective-permute-done.42.refs_2_ = bf16[3,128,128]{2,1,0:T(8,128)(2,1)S(1)} collective-permute-done((bf16[3,128,128]{2,1,0:T(8,128)(2,1)S(1)}, bf16[3,128,128]{2,1,0:T(8,128)(2,1)S(1)}, u32[]{:S(2)}, u32[]{:S(2)}) %collective-permute-start.42) | collective-permute-done | bytes 98336 | tf_op jit(solution)/shard_map/ppermute | solution.py:38
  119.5 1.8 %shard_map.88 = (bf16[3,128,128]{2,1,0:T(8,128)(2,1)S(1)}, bf16[3,128,128]{2,1,0:T(8,128)(2,1)S(1)}, bf16[3,128,128]{2,1,0:T(8,128)(2,1)S(1)}, bf16[3,128,128]{2,1,0:T(8,128)(2,1)S(1)}, f32[768,512]{1,0:T(8,128)}) custom-call(bf16[3,128,128]{2,1,0:T(8,128)(2,1)S(1)} %get-tuple-element.132.refs_0_, bf16[3,128,128]{2,1,0:T(8,128)(2,1)S(1)} %collective-permute-done.41.refs_1_, ...), custom_call_target="tpu_custom_call" | custom-call | flops 402653184 | bytes 3145728 | tf_op jit(solution)/shard_map/pallas_call | solution.py:89
  121.3 4.3 %collective-permute-start.47 = (bf16[3,128,128]{2,1,0:T(8,128)(2,1)S(1)}, bf16[3,128,128]{2,1,0:T(8,128)(2,1)S(1)}, u32[]{:S(2)}, u32[]{:S(2)}) collective-permute-start(bf16[3,128,128]{2,1,0:T(8,128)(2,1)S(1)} %get-tuple-element.143), channel_id=1, source_target_pairs={{0,1},{1,2},{2,3},{3,0},{4,5},{5,6},{6,7},{7,4},{8,9},{9,10},{10,1... | collective-permute-start | bytes 294920 | tf_op jit(solution)/shard_map/ppermute | solution.py:38
  125.6 2.0 %collective-permute-start.48 = (bf16[3,128,128]{2,1,0:T(8,128)(2,1)S(1)}, bf16[3,128,128]{2,1,0:T(8,128)(2,1)S(1)}, u32[]{:S(2)}, u32[]{:S(2)}) collective-permute-start(bf16[3,128,128]{2,1,0:T(8,128)(2,1)S(1)} %get-tuple-element.144), channel_id=1, source_target_pairs={{0,2},{1,3},{2,0},{3,1},{4,6},{5,7},{6,4},{7,5},{8,10},{9,11},{10,... | collective-permute-start | bytes 294920 | tf_op jit(solution)/shard_map/ppermute | solution.py:38
  127.6 2.8 %collective-permute-start.49 = (bf16[3,128,128]{2,1,0:T(8,128)(2,1)S(1)}, bf16[3,128,128]{2,1,0:T(8,128)(2,1)S(1)}, u32[]{:S(2)}, u32[]{:S(2)}) collective-permute-start(bf16[3,128,128]{2,1,0:T(8,128)(2,1)S(1)} %get-tuple-element.145), channel_id=1, source_target_pairs={{0,3},{1,0},{2,1},{3,2},{4,7},{5,4},{6,5},{7,6},{8,11},{9,8},{10,9... | collective-permute-start | bytes 294920 | tf_op jit(solution)/shard_map/ppermute | solution.py:38
  130.5 1.8 %shard_map.89 = (bf16[3,128,128]{2,1,0:T(8,128)(2,1)S(1)}, bf16[3,128,128]{2,1,0:T(8,128)(2,1)S(1)}, bf16[3,128,128]{2,1,0:T(8,128)(2,1)S(1)}, bf16[3,128,128]{2,1,0:T(8,128)(2,1)S(1)}, f32[768,512]{1,0:T(8,128)}) custom-call(bf16[3,128,128]{2,1,0:T(8,128)(2,1)S(1)} %get-tuple-element.128.refs_0_, ...), custom_call_target="tpu_custom_call", output_to_operand_aliasing={{4}: (6, {})} | custom-call | flops 402653184 | bytes 3145728 | tf_op jit(solution)/shard_map/pallas_call | solution.py:89
  132.9 3.3 %collective-permute-start.46 = (bf16[3,128,128]{2,1,0:T(8,128)(2,1)S(1)}, bf16[3,128,128]{2,1,0:T(8,128)(2,1)S(1)}, u32[]{:S(2)}, u32[]{:S(2)}) collective-permute-start(bf16[3,128,128]{2,1,0:T(8,128)(2,1)S(1)} %get-tuple-element.141), channel_id=1, source_target_pairs={{0,3},{1,0},{2,1},{3,2},{4,7},{5,4},{6,5},{7,6},{8,11},{9,8},{10,9... | collective-permute-start | bytes 294920 | tf_op jit(solution)/shard_map/ppermute | solution.py:38
  136.2 2.1 %shard_map.90.rest_4_ = f32[52,128,128]{2,1,0:T(8,128)S(1)} custom-call(s32[24,16]{1,0:T(8,128)S(4)} %get-tuple-element.78.src, bf16[12,16,128,128]{3,2,1,0:T(8,128)(2,1)S(1)} %get-tuple-element.94.kern_ref, bf16[3,128,128]{2,1,0:T(8,128)(2,1)S(1)} %get-tuple-element.142.rest_0_, bf16[3,128,128]{2,1,0:T(8,128)(2,1)S(1)} %collective-permute-done.47.rest_1_, ...), custom_call_target="tpu_custom_call" | custom-call | flops 805306368 | bytes 10485760 | tf_op jit(solution)/shard_map/pallas_call | solution.py:89
  138.4 1.5 collective-permute-done.44.rest_1_
  139.8 3.0 %collective-permute-done.45.rest_2_ = bf16[3,128,128]{2,1,0:T(8,128)(2,1)S(1)} collective-permute-done((bf16[3,128,128]{2,1,0:T(8,128)(2,1)S(1)}, bf16[3,128,128]{2,1,0:T(8,128)(2,1)S(1)}, u32[]{:S(2)}, u32[]{:S(2)}) %collective-permute-start.45) | collective-permute-done | bytes 98336 | tf_op jit(solution)/shard_map/ppermute | solution.py:38
  142.8 2.1 %shard_map.91 = (bf16[24,128,128]{2,1,0:T(8,128)(2,1)S(1)}, bf16[6,128,128]{2,1,0:T(8,128)(2,1)S(1)}, bf16[6,128,128]{2,1,0:T(8,128)(2,1)S(1)}, bf16[2,128,128]{...) custom-call(s32[24,16]{1,0:T(8,128)S(4)} %get-tuple-element.78.src, ...), custom_call_target="tpu_custom_call", output_to_operand_aliasing={{8}: (6, {})} | custom-call | flops 805306368 | bytes 10485760 | tf_op jit(solution)/shard_map/pallas_call | solution.py:89
  145.8 1.6 collective-permute-start.52
  147.9 2.0 %collective-permute-start.54 = (bf16[2,128,128]{2,1,0:T(8,128)(2,1)S(1)}, bf16[2,128,128]{2,1,0:T(8,128)(2,1)S(1)}, u32[]{:S(2)}, u32[]{:S(2)}) collective-permute-start(bf16[2,128,128]{2,1,0:T(8,128)(2,1)S(1)} %get-tuple-element.151), channel_id=1, source_target_pairs={{0,16},{4,20},{8,24},{12,28},{16,0},{20,4},{24,8},{28,12},{1,17},{... | collective-permute-start | bytes 196616 | tf_op jit(solution)/shard_map/ppermute | solution.py:38
  149.9 2.1 %collective-permute-done.52.rest_0_ = bf16[2,128,128]{2,1,0:T(8,128)(2,1)S(1)} collective-permute-done((bf16[2,128,128]{2,1,0:T(8,128)(2,1)S(1)}, bf16[2,128,128]{2,1,0:T(8,128)(2,1)S(1)}, u32[]{:S(2)}, u32[]{:S(2)}) %collective-permute-start.52) | collective-permute-done | bytes 65568 | tf_op jit(solution)/shard_map/ppermute | solution.py:38
  152.0 3.5 %collective-permute-start.55 = (bf16[2,128,128]{2,1,0:T(8,128)(2,1)S(1)}, bf16[2,128,128]{2,1,0:T(8,128)(2,1)S(1)}, u32[]{:S(2)}, u32[]{:S(2)}) collective-permute-start(bf16[2,128,128]{2,1,0:T(8,128)(2,1)S(1)} %get-tuple-element.152), channel_id=1, source_target_pairs={{0,20},{4,24},{8,28},{12,0},{16,4},{20,8},{24,12},{28,16},{1,21},{... | collective-permute-start | bytes 196616 | tf_op jit(solution)/shard_map/ppermute | solution.py:38
  155.5 0.9 collective-permute-start.56
  157.3 2.5 %collective-permute-done.56.rest_4_ = bf16[2,128,128]{2,1,0:T(8,128)(2,1)S(1)} collective-permute-done((bf16[2,128,128]{2,1,0:T(8,128)(2,1)S(1)}, bf16[2,128,128]{2,1,0:T(8,128)(2,1)S(1)}, u32[]{:S(2)}, u32[]{:S(2)}) %collective-permute-start.56) | collective-permute-done | bytes 65568 | tf_op jit(solution)/shard_map/ppermute | solution.py:38
  159.8 2.1 %shard_map.92 = f32[24,128,128]{2,1,0:T(8,128)} custom-call(bf16[24,128,128]{2,1,0:T(8,128)(2,1)S(1)} %get-tuple-element.146.own_ref, bf16[6,128,128]{2,1,0:T(8,128)(2,1)S(1)} %collective-permute-done.50.right_ref, bf16[6,128,128]{2,1,0:T(8,128)(2,1)S(1)} %collective-permute-done.51.left_ref, f32[24,128,128]{2,1,0:T(8,128)S(1)} %bitcast.4, ...), custom_call_target="tpu_custom_call" | custom-call | bytes 6291456 | tf_op jit(solution)/shard_map/pallas_call | solution.py:89
  (73 shorter events, 10.9 us)
Async XLA Ops:
  4.2 25.1 %collective-permute-start = (bf16[6,128,128]{2,1,0:T(8,128)(2,1)S(1)}, bf16[6,128,128]{2,1,0:T(8,128)(2,1)S(1)}, u32[]{:S(2)}, u32[]{:S(2)}) collective-permute-start(bf16[6,128,128]{2,1,0:T(8,128)(2,1)S(1)} %get-tuple-element.80), channel_id=1, source_target_pairs={{0,4},{4,8},{8,12},{12,16},{16,20},{20,24},{24,28},{28,0},{1,5},{5... | collective-permute-start | bytes 589832 | tf_op jit(solution)/shard_map/ppermute | solution.py:38
  4.7 24.6 %collective-permute-start.1 = (bf16[6,128,128]{2,1,0:T(8,128)(2,1)S(1)}, bf16[6,128,128]{2,1,0:T(8,128)(2,1)S(1)}, u32[]{:S(2)}, u32[]{:S(2)}) collective-permute-start(bf16[6,128,128]{2,1,0:T(8,128)(2,1)S(1)} %get-tuple-element.81), channel_id=1, source_target_pairs={{0,28},{4,0},{8,4},{12,8},{16,12},{20,16},{24,20},{28,24},{1,29},{... | collective-permute-start | bytes 589832 | tf_op jit(solution)/shard_map/ppermute | solution.py:38
  7.7 6.2 %collective-permute-start.2 = (s32[2]{0:T(128)S(1)}, s32[2]{0:T(128)S(1)}, u32[]{:S(2)}, u32[]{:S(2)}) collective-permute-start(s32[2]{0:T(128)S(1)} %get-tuple-element.82), channel_id=1, source_target_pairs={{0,24},{4,28},{8,0},{12,4},{16,8},{20,12},{24,16},{28,20},{1,25},{... | collective-permute-start | bytes 32 | tf_op jit(solution)/shard_map/ppermute | solution.py:38
  9.9 4.0 %collective-permute-start.3 = (s32[2]{0:T(128)S(1)}, s32[2]{0:T(128)S(1)}, u32[]{:S(2)}, u32[]{:S(2)}) collective-permute-start(s32[2]{0:T(128)S(1)} %get-tuple-element.83), channel_id=1, source_target_pairs={{0,20},{4,24},{8,28},{12,0},{16,4},{20,8},{24,12},{28,16},{1,21},{... | collective-permute-start | bytes 32 | tf_op jit(solution)/shard_map/ppermute | solution.py:38
  9.9 5.5 %collective-permute-start.4 = (s32[2]{0:T(128)S(1)}, s32[2]{0:T(128)S(1)}, u32[]{:S(2)}, u32[]{:S(2)}) collective-permute-start(s32[2]{0:T(128)S(1)} %get-tuple-element.84), channel_id=1, source_target_pairs={{0,16},{4,20},{8,24},{12,28},{16,0},{20,4},{24,8},{28,12},{1,17},{... | collective-permute-start | bytes 32 | tf_op jit(solution)/shard_map/ppermute | solution.py:38
  13.9 3.0 %collective-permute-start.5 = (s32[2]{0:T(128)S(1)}, s32[2]{0:T(128)S(1)}, u32[]{:S(2)}, u32[]{:S(2)}) collective-permute-start(s32[2]{0:T(128)S(1)} %get-tuple-element.85), channel_id=1, source_target_pairs={{0,12},{4,16},{8,20},{12,24},{16,28},{20,0},{24,4},{28,8},{1,13},{... | collective-permute-start | bytes 32 | tf_op jit(solution)/shard_map/ppermute | solution.py:38
  13.9 4.5 %collective-permute-start.6 = (s32[2]{0:T(128)S(1)}, s32[2]{0:T(128)S(1)}, u32[]{:S(2)}, u32[]{:S(2)}) collective-permute-start(s32[2]{0:T(128)S(1)} %get-tuple-element.86), channel_id=1, source_target_pairs={{0,8},{4,12},{8,16},{12,20},{16,24},{20,28},{24,0},{28,4},{1,9},{5... | collective-permute-start | bytes 32 | tf_op jit(solution)/shard_map/ppermute | solution.py:38
  19.0 5.3 %collective-permute-start.7 = (bf16[2,128,128]{2,1,0:T(8,128)(2,1)S(1)}, bf16[2,128,128]{2,1,0:T(8,128)(2,1)S(1)}, u32[]{:S(2)}, u32[]{:S(2)}) collective-permute-start(bf16[2,128,128]{2,1,0:T(8,128)(2,1)S(1)} %get-tuple-element.87), channel_id=1, source_target_pairs={{0,8},{4,12},{8,16},{12,20},{16,24},{20,28},{24,0},{28,4},{1,9},{5... | collective-permute-start | bytes 196616 | tf_op jit(solution)/shard_map/ppermute | solution.py:38
  19.6 4.7 %collective-permute-start.8 = (bf16[2,128,128]{2,1,0:T(8,128)(2,1)S(1)}, bf16[2,128,128]{2,1,0:T(8,128)(2,1)S(1)}, u32[]{:S(2)}, u32[]{:S(2)}) collective-permute-start(bf16[2,128,128]{2,1,0:T(8,128)(2,1)S(1)} %get-tuple-element.88), channel_id=1, source_target_pairs={{0,12},{4,16},{8,20},{12,24},{16,28},{20,0},{24,4},{28,8},{1,13},{... | collective-permute-start | bytes 196616 | tf_op jit(solution)/shard_map/ppermute | solution.py:38
  20.8 5.3 %collective-permute-start.9 = (bf16[2,128,128]{2,1,0:T(8,128)(2,1)S(1)}, bf16[2,128,128]{2,1,0:T(8,128)(2,1)S(1)}, u32[]{:S(2)}, u32[]{:S(2)}) collective-permute-start(bf16[2,128,128]{2,1,0:T(8,128)(2,1)S(1)} %get-tuple-element.89), channel_id=1, source_target_pairs={{0,16},{4,20},{8,24},{12,28},{16,0},{20,4},{24,8},{28,12},{1,17},{... | collective-permute-start | bytes 196616 | tf_op jit(solution)/shard_map/ppermute | solution.py:38
  24.3 3.8 %collective-permute-start.10 = (bf16[2,128,128]{2,1,0:T(8,128)(2,1)S(1)}, bf16[2,128,128]{2,1,0:T(8,128)(2,1)S(1)}, u32[]{:S(2)}, u32[]{:S(2)}) collective-permute-start(bf16[2,128,128]{2,1,0:T(8,128)(2,1)S(1)} %get-tuple-element.90), channel_id=1, source_target_pairs={{0,20},{4,24},{8,28},{12,0},{16,4},{20,8},{24,12},{28,16},{1,21},{... | collective-permute-start | bytes 196616 | tf_op jit(solution)/shard_map/ppermute | solution.py:38
  24.3 5.0 %collective-permute-start.11 = (bf16[2,128,128]{2,1,0:T(8,128)(2,1)S(1)}, bf16[2,128,128]{2,1,0:T(8,128)(2,1)S(1)}, u32[]{:S(2)}, u32[]{:S(2)}) collective-permute-start(bf16[2,128,128]{2,1,0:T(8,128)(2,1)S(1)} %get-tuple-element.91), channel_id=1, source_target_pairs={{0,24},{4,28},{8,0},{12,4},{16,8},{20,12},{24,16},{28,20},{1,25},{... | collective-permute-start | bytes 196616 | tf_op jit(solution)/shard_map/ppermute | solution.py:38
  34.1 13.6 %collective-permute-start.18 = (bf16[3,128,128]{2,1,0:T(8,128)(2,1)S(1)}, bf16[3,128,128]{2,1,0:T(8,128)(2,1)S(1)}, u32[]{:S(2)}, u32[]{:S(2)}) collective-permute-start(bf16[3,128,128]{2,1,0:T(8,128)(2,1)S(1)} %get-tuple-element.104), channel_id=1, source_target_pairs={{0,3},{1,0},{2,1},{3,2},{4,7},{5,4},{6,5},{7,6},{8,11},{9,8},{10,9... | collective-permute-start | bytes 294920 | tf_op jit(solution)/shard_map/ppermute | solution.py:38
  37.7 9.9 %collective-permute-start.19 = (bf16[3,128,128]{2,1,0:T(8,128)(2,1)S(1)}, bf16[3,128,128]{2,1,0:T(8,128)(2,1)S(1)}, u32[]{:S(2)}, u32[]{:S(2)}) collective-permute-start(bf16[3,128,128]{2,1,0:T(8,128)(2,1)S(1)} %get-tuple-element.105), channel_id=1, source_target_pairs={{0,2},{1,3},{2,0},{3,1},{4,6},{5,7},{6,4},{7,5},{8,10},{9,11},{10,... | collective-permute-start | bytes 294920 | tf_op jit(solution)/shard_map/ppermute | solution.py:38
  37.7 9.9 %collective-permute-start.20 = (bf16[3,128,128]{2,1,0:T(8,128)(2,1)S(1)}, bf16[3,128,128]{2,1,0:T(8,128)(2,1)S(1)}, u32[]{:S(2)}, u32[]{:S(2)}) collective-permute-start(bf16[3,128,128]{2,1,0:T(8,128)(2,1)S(1)} %get-tuple-element.106), channel_id=1, source_target_pairs={{0,1},{1,2},{2,3},{3,0},{4,5},{5,6},{6,7},{7,4},{8,9},{9,10},{10,1... | collective-permute-start | bytes 294920 | tf_op jit(solution)/shard_map/ppermute | solution.py:38
  38.7 8.9 %copy-start = (f32[768,512]{1,0:T(8,128)S(1)}, f32[768,512]{1,0:T(8,128)}, u32[]{:S(2)}) copy-start(f32[768,512]{1,0:T(8,128)} %refs_5_.7) | copy-start | bytes 4718596
  38.7 9.0 %copy-start.1 = (bf16[512,512]{1,0:T(8,128)(2,1)S(1)}, bf16[512,512]{1,0:T(8,128)(2,1)}, u32[]{:S(2)}) copy-start(bf16[512,512]{1,0:T(8,128)(2,1)} %refs_4_.7) | copy-start | bytes 1572868
  43.7 9.7 %collective-permute-start.12 = (bf16[3,128,128]{2,1,0:T(8,128)(2,1)S(1)}, bf16[3,128,128]{2,1,0:T(8,128)(2,1)S(1)}, u32[]{:S(2)}, u32[]{:S(2)}) collective-permute-start(bf16[3,128,128]{2,1,0:T(8,128)(2,1)S(1)} %get-tuple-element.96), channel_id=1, source_target_pairs={{0,3},{1,0},{2,1},{3,2},{4,7},{5,4},{6,5},{7,6},{8,11},{9,8},{10,9... | collective-permute-start | bytes 294920 | tf_op jit(solution)/shard_map/ppermute | solution.py:38
  46.5 14.8 %collective-permute-start.13 = (bf16[3,128,128]{2,1,0:T(8,128)(2,1)S(1)}, bf16[3,128,128]{2,1,0:T(8,128)(2,1)S(1)}, u32[]{:S(2)}, u32[]{:S(2)}) collective-permute-start(bf16[3,128,128]{2,1,0:T(8,128)(2,1)S(1)} %get-tuple-element.97), channel_id=1, source_target_pairs={{0,2},{1,3},{2,0},{3,1},{4,6},{5,7},{6,4},{7,5},{8,10},{9,11},{10,... | collective-permute-start | bytes 294920 | tf_op jit(solution)/shard_map/ppermute | solution.py:38
  47.7 13.7 %collective-permute-start.14 = (bf16[3,128,128]{2,1,0:T(8,128)(2,1)S(1)}, bf16[3,128,128]{2,1,0:T(8,128)(2,1)S(1)}, u32[]{:S(2)}, u32[]{:S(2)}) collective-permute-start(bf16[3,128,128]{2,1,0:T(8,128)(2,1)S(1)} %get-tuple-element.98), channel_id=1, source_target_pairs={{0,1},{1,2},{2,3},{3,0},{4,5},{5,6},{6,7},{7,4},{8,9},{9,10},{10,1... | collective-permute-start | bytes 294920 | tf_op jit(solution)/shard_map/ppermute | solution.py:38
  48.9 13.8 %collective-permute-start.21 = (bf16[3,128,128]{2,1,0:T(8,128)(2,1)S(1)}, bf16[3,128,128]{2,1,0:T(8,128)(2,1)S(1)}, u32[]{:S(2)}, u32[]{:S(2)}) collective-permute-start(bf16[3,128,128]{2,1,0:T(8,128)(2,1)S(1)} %get-tuple-element.108), channel_id=1, source_target_pairs={{0,1},{1,2},{2,3},{3,0},{4,5},{5,6},{6,7},{7,4},{8,9},{9,10},{10,1... | collective-permute-start | bytes 294920 | tf_op jit(solution)/shard_map/ppermute | solution.py:38
  51.3 15.1 %collective-permute-start.22 = (bf16[3,128,128]{2,1,0:T(8,128)(2,1)S(1)}, bf16[3,128,128]{2,1,0:T(8,128)(2,1)S(1)}, u32[]{:S(2)}, u32[]{:S(2)}) collective-permute-start(bf16[3,128,128]{2,1,0:T(8,128)(2,1)S(1)} %get-tuple-element.109), channel_id=1, source_target_pairs={{0,2},{1,3},{2,0},{3,1},{4,6},{5,7},{6,4},{7,5},{8,10},{9,11},{10,... | collective-permute-start | bytes 294920 | tf_op jit(solution)/shard_map/ppermute | solution.py:38
  53.3 13.1 %collective-permute-start.23 = (bf16[3,128,128]{2,1,0:T(8,128)(2,1)S(1)}, bf16[3,128,128]{2,1,0:T(8,128)(2,1)S(1)}, u32[]{:S(2)}, u32[]{:S(2)}) collective-permute-start(bf16[3,128,128]{2,1,0:T(8,128)(2,1)S(1)} %get-tuple-element.110), channel_id=1, source_target_pairs={{0,3},{1,0},{2,1},{3,2},{4,7},{5,4},{6,5},{7,6},{8,11},{9,8},{10,9... | collective-permute-start | bytes 294920 | tf_op jit(solution)/shard_map/ppermute | solution.py:38
  62.5 6.9 %collective-permute-start.15 = (bf16[3,128,128]{2,1,0:T(8,128)(2,1)S(1)}, bf16[3,128,128]{2,1,0:T(8,128)(2,1)S(1)}, u32[]{:S(2)}, u32[]{:S(2)}) collective-permute-start(bf16[3,128,128]{2,1,0:T(8,128)(2,1)S(1)} %get-tuple-element.100), channel_id=1, source_target_pairs={{0,1},{1,2},{2,3},{3,0},{4,5},{5,6},{6,7},{7,4},{8,9},{9,10},{10,1... | collective-permute-start | bytes 294920 | tf_op jit(solution)/shard_map/ppermute | solution.py:38
  62.6 8.9 %collective-permute-start.16 = (bf16[3,128,128]{2,1,0:T(8,128)(2,1)S(1)}, bf16[3,128,128]{2,1,0:T(8,128)(2,1)S(1)}, u32[]{:S(2)}, u32[]{:S(2)}) collective-permute-start(bf16[3,128,128]{2,1,0:T(8,128)(2,1)S(1)} %get-tuple-element.101), channel_id=1, source_target_pairs={{0,2},{1,3},{2,0},{3,1},{4,6},{5,7},{6,4},{7,5},{8,10},{9,11},{10,... | collective-permute-start | bytes 294920 | tf_op jit(solution)/shard_map/ppermute | solution.py:38
  62.7 8.8 %collective-permute-start.17 = (bf16[3,128,128]{2,1,0:T(8,128)(2,1)S(1)}, bf16[3,128,128]{2,1,0:T(8,128)(2,1)S(1)}, u32[]{:S(2)}, u32[]{:S(2)}) collective-permute-start(bf16[3,128,128]{2,1,0:T(8,128)(2,1)S(1)} %get-tuple-element.102), channel_id=1, source_target_pairs={{0,3},{1,0},{2,1},{3,2},{4,7},{5,4},{6,5},{7,6},{8,11},{9,8},{10,9... | collective-permute-start | bytes 294920 | tf_op jit(solution)/shard_map/ppermute | solution.py:38
  71.5 16.5 %copy-start.2 = (f32[3072,128]{1,0:T(8,128)S(1)}, f32[3072,128]{1,0:T(8,128)}, u32[]{:S(2)}) copy-start(f32[3072,128]{1,0:T(8,128)} %param.11) | copy-start | bytes 4718596
  73.6 14.4 %collective-permute-start.24 = (bf16[6,128,128]{2,1,0:T(8,128)(2,1)S(1)}, bf16[6,128,128]{2,1,0:T(8,128)(2,1)S(1)}, u32[]{:S(2)}, u32[]{:S(2)}) collective-permute-start(bf16[6,128,128]{2,1,0:T(8,128)(2,1)S(1)} %get-tuple-element.112), channel_id=1, source_target_pairs={{0,28},{4,0},{8,4},{12,8},{16,12},{20,16},{24,20},{28,24},{1,29},{... | collective-permute-start | bytes 589832 | tf_op jit(solution)/shard_map/ppermute | solution.py:38
  74.2 13.8 %collective-permute-start.25 = (bf16[6,128,128]{2,1,0:T(8,128)(2,1)S(1)}, bf16[6,128,128]{2,1,0:T(8,128)(2,1)S(1)}, u32[]{:S(2)}, u32[]{:S(2)}) collective-permute-start(bf16[6,128,128]{2,1,0:T(8,128)(2,1)S(1)} %get-tuple-element.113), channel_id=1, source_target_pairs={{0,4},{4,8},{8,12},{12,16},{16,20},{20,24},{24,28},{28,0},{1,5},{5... | collective-permute-start | bytes 589832 | tf_op jit(solution)/shard_map/ppermute | solution.py:38
  74.2 8.0 %collective-permute-start.26 = (bf16[2,128,128]{2,1,0:T(8,128)(2,1)S(1)}, bf16[2,128,128]{2,1,0:T(8,128)(2,1)S(1)}, u32[]{:S(2)}, u32[]{:S(2)}) collective-permute-start(bf16[2,128,128]{2,1,0:T(8,128)(2,1)S(1)} %get-tuple-element.114), channel_id=1, source_target_pairs={{0,8},{4,12},{8,16},{12,20},{16,24},{20,28},{24,0},{28,4},{1,9},{5... | collective-permute-start | bytes 196616 | tf_op jit(solution)/shard_map/ppermute | solution.py:38
  75.4 8.3 %collective-permute-start.27 = (bf16[2,128,128]{2,1,0:T(8,128)(2,1)S(1)}, bf16[2,128,128]{2,1,0:T(8,128)(2,1)S(1)}, u32[]{:S(2)}, u32[]{:S(2)}) collective-permute-start(bf16[2,128,128]{2,1,0:T(8,128)(2,1)S(1)} %get-tuple-element.115), channel_id=1, source_target_pairs={{0,12},{4,16},{8,20},{12,24},{16,28},{20,0},{24,4},{28,8},{1,13},{... | collective-permute-start | bytes 196616 | tf_op jit(solution)/shard_map/ppermute | solution.py:38
  77.3 7.3 %collective-permute-start.28 = (bf16[2,128,128]{2,1,0:T(8,128)(2,1)S(1)}, bf16[2,128,128]{2,1,0:T(8,128)(2,1)S(1)}, u32[]{:S(2)}, u32[]{:S(2)}) collective-permute-start(bf16[2,128,128]{2,1,0:T(8,128)(2,1)S(1)} %get-tuple-element.116), channel_id=1, source_target_pairs={{0,16},{4,20},{8,24},{12,28},{16,0},{20,4},{24,8},{28,12},{1,17},{... | collective-permute-start | bytes 196616 | tf_op jit(solution)/shard_map/ppermute | solution.py:38
  82.2 3.7 %collective-permute-start.29 = (bf16[2,128,128]{2,1,0:T(8,128)(2,1)S(1)}, bf16[2,128,128]{2,1,0:T(8,128)(2,1)S(1)}, u32[]{:S(2)}, u32[]{:S(2)}) collective-permute-start(bf16[2,128,128]{2,1,0:T(8,128)(2,1)S(1)} %get-tuple-element.117), channel_id=1, source_target_pairs={{0,20},{4,24},{8,28},{12,0},{16,4},{20,8},{24,12},{28,16},{1,21},{... | collective-permute-start | bytes 196616 | tf_op jit(solution)/shard_map/ppermute | solution.py:38
  83.7 4.3 %collective-permute-start.30 = (bf16[2,128,128]{2,1,0:T(8,128)(2,1)S(1)}, bf16[2,128,128]{2,1,0:T(8,128)(2,1)S(1)}, u32[]{:S(2)}, u32[]{:S(2)}) collective-permute-start(bf16[2,128,128]{2,1,0:T(8,128)(2,1)S(1)} %get-tuple-element.118), channel_id=1, source_target_pairs={{0,24},{4,28},{8,0},{12,4},{16,8},{20,12},{24,16},{28,20},{1,25},{... | collective-permute-start | bytes 196616 | tf_op jit(solution)/shard_map/ppermute | solution.py:38
  89.0 14.7 %collective-permute-start.31 = (bf16[6,128,128]{2,1,0:T(8,128)(2,1)S(1)}, bf16[6,128,128]{2,1,0:T(8,128)(2,1)S(1)}, u32[]{:S(2)}, u32[]{:S(2)}) collective-permute-start(bf16[6,128,128]{2,1,0:T(8,128)(2,1)S(1)} %get-tuple-element.120), channel_id=1, source_target_pairs={{0,4},{4,8},{8,12},{12,16},{16,20},{20,24},{24,28},{28,0},{1,5},{5... | collective-permute-start | bytes 589832 | tf_op jit(solution)/shard_map/ppermute | solution.py:38
  89.1 14.6 %collective-permute-start.32 = (bf16[6,128,128]{2,1,0:T(8,128)(2,1)S(1)}, bf16[6,128,128]{2,1,0:T(8,128)(2,1)S(1)}, u32[]{:S(2)}, u32[]{:S(2)}) collective-permute-start(bf16[6,128,128]{2,1,0:T(8,128)(2,1)S(1)} %get-tuple-element.121), channel_id=1, source_target_pairs={{0,28},{4,0},{8,4},{12,8},{16,12},{20,16},{24,20},{28,24},{1,29},{... | collective-permute-start | bytes 589832 | tf_op jit(solution)/shard_map/ppermute | solution.py:38
  91.7 7.0 %collective-permute-start.33 = (bf16[2,128,128]{2,1,0:T(8,128)(2,1)S(1)}, bf16[2,128,128]{2,1,0:T(8,128)(2,1)S(1)}, u32[]{:S(2)}, u32[]{:S(2)}) collective-permute-start(bf16[2,128,128]{2,1,0:T(8,128)(2,1)S(1)} %get-tuple-element.122), channel_id=1, source_target_pairs={{0,8},{4,12},{8,16},{12,20},{16,24},{20,28},{24,0},{28,4},{1,9},{5... | collective-permute-start | bytes 196616 | tf_op jit(solution)/shard_map/ppermute | solution.py:38
  92.2 6.6 %collective-permute-start.34 = (bf16[2,128,128]{2,1,0:T(8,128)(2,1)S(1)}, bf16[2,128,128]{2,1,0:T(8,128)(2,1)S(1)}, u32[]{:S(2)}, u32[]{:S(2)}) collective-permute-start(bf16[2,128,128]{2,1,0:T(8,128)(2,1)S(1)} %get-tuple-element.123), channel_id=1, source_target_pairs={{0,12},{4,16},{8,20},{12,24},{16,28},{20,0},{24,4},{28,8},{1,13},{... | collective-permute-start | bytes 196616 | tf_op jit(solution)/shard_map/ppermute | solution.py:38
  92.2 8.0 %collective-permute-start.35 = (bf16[2,128,128]{2,1,0:T(8,128)(2,1)S(1)}, bf16[2,128,128]{2,1,0:T(8,128)(2,1)S(1)}, u32[]{:S(2)}, u32[]{:S(2)}) collective-permute-start(bf16[2,128,128]{2,1,0:T(8,128)(2,1)S(1)} %get-tuple-element.124), channel_id=1, source_target_pairs={{0,16},{4,20},{8,24},{12,28},{16,0},{20,4},{24,8},{28,12},{1,17},{... | collective-permute-start | bytes 196616 | tf_op jit(solution)/shard_map/ppermute | solution.py:38
  98.7 3.8 %collective-permute-start.36 = (bf16[2,128,128]{2,1,0:T(8,128)(2,1)S(1)}, bf16[2,128,128]{2,1,0:T(8,128)(2,1)S(1)}, u32[]{:S(2)}, u32[]{:S(2)}) collective-permute-start(bf16[2,128,128]{2,1,0:T(8,128)(2,1)S(1)} %get-tuple-element.125), channel_id=1, source_target_pairs={{0,20},{4,24},{8,28},{12,0},{16,4},{20,8},{24,12},{28,16},{1,21},{... | collective-permute-start | bytes 196616 | tf_op jit(solution)/shard_map/ppermute | solution.py:38
  98.7 5.0 %collective-permute-start.37 = (bf16[2,128,128]{2,1,0:T(8,128)(2,1)S(1)}, bf16[2,128,128]{2,1,0:T(8,128)(2,1)S(1)}, u32[]{:S(2)}, u32[]{:S(2)}) collective-permute-start(bf16[2,128,128]{2,1,0:T(8,128)(2,1)S(1)} %get-tuple-element.126), channel_id=1, source_target_pairs={{0,24},{4,28},{8,0},{12,4},{16,8},{20,12},{24,16},{28,20},{1,25},{... | collective-permute-start | bytes 196616 | tf_op jit(solution)/shard_map/ppermute | solution.py:38
  105.6 10.6 %collective-permute-start.41 = (bf16[3,128,128]{2,1,0:T(8,128)(2,1)S(1)}, bf16[3,128,128]{2,1,0:T(8,128)(2,1)S(1)}, u32[]{:S(2)}, u32[]{:S(2)}) collective-permute-start(bf16[3,128,128]{2,1,0:T(8,128)(2,1)S(1)} %get-tuple-element.133), channel_id=1, source_target_pairs={{0,3},{1,0},{2,1},{3,2},{4,7},{5,4},{6,5},{7,6},{8,11},{9,8},{10,9... | collective-permute-start | bytes 294920 | tf_op jit(solution)/shard_map/ppermute | solution.py:38
  109.4 10.1 %collective-permute-start.42 = (bf16[3,128,128]{2,1,0:T(8,128)(2,1)S(1)}, bf16[3,128,128]{2,1,0:T(8,128)(2,1)S(1)}, u32[]{:S(2)}, u32[]{:S(2)}) collective-permute-start(bf16[3,128,128]{2,1,0:T(8,128)(2,1)S(1)} %get-tuple-element.134), channel_id=1, source_target_pairs={{0,2},{1,3},{2,0},{3,1},{4,6},{5,7},{6,4},{7,5},{8,10},{9,11},{10,... | collective-permute-start | bytes 294920 | tf_op jit(solution)/shard_map/ppermute | solution.py:38
  109.4 10.1 %collective-permute-start.43 = (bf16[3,128,128]{2,1,0:T(8,128)(2,1)S(1)}, bf16[3,128,128]{2,1,0:T(8,128)(2,1)S(1)}, u32[]{:S(2)}, u32[]{:S(2)}) collective-permute-start(bf16[3,128,128]{2,1,0:T(8,128)(2,1)S(1)} %get-tuple-element.135), channel_id=1, source_target_pairs={{0,1},{1,2},{2,3},{3,0},{4,5},{5,6},{6,7},{7,4},{8,9},{9,10},{10,1... | collective-permute-start | bytes 294920 | tf_op jit(solution)/shard_map/ppermute | solution.py:38
  111.9 15.7 %collective-permute-start.38 = (bf16[3,128,128]{2,1,0:T(8,128)(2,1)S(1)}, bf16[3,128,128]{2,1,0:T(8,128)(2,1)S(1)}, u32[]{:S(2)}, u32[]{:S(2)}) collective-permute-start(bf16[3,128,128]{2,1,0:T(8,128)(2,1)S(1)} %get-tuple-element.129), channel_id=1, source_target_pairs={{0,3},{1,0},{2,1},{3,2},{4,7},{5,4},{6,5},{7,6},{8,11},{9,8},{10,9... | collective-permute-start | bytes 294920 | tf_op jit(solution)/shard_map/ppermute | solution.py:38
  115.1 15.4 %collective-permute-start.39 = (bf16[3,128,128]{2,1,0:T(8,128)(2,1)S(1)}, bf16[3,128,128]{2,1,0:T(8,128)(2,1)S(1)}, u32[]{:S(2)}, u32[]{:S(2)}) collective-permute-start(bf16[3,128,128]{2,1,0:T(8,128)(2,1)S(1)} %get-tuple-element.130), channel_id=1, source_target_pairs={{0,2},{1,3},{2,0},{3,1},{4,6},{5,7},{6,4},{7,5},{8,10},{9,11},{10,... | collective-permute-start | bytes 294920 | tf_op jit(solution)/shard_map/ppermute | solution.py:38
  116.2 14.3 %collective-permute-start.40 = (bf16[3,128,128]{2,1,0:T(8,128)(2,1)S(1)}, bf16[3,128,128]{2,1,0:T(8,128)(2,1)S(1)}, u32[]{:S(2)}, u32[]{:S(2)}) collective-permute-start(bf16[3,128,128]{2,1,0:T(8,128)(2,1)S(1)} %get-tuple-element.131), channel_id=1, source_target_pairs={{0,1},{1,2},{2,3},{3,0},{4,5},{5,6},{6,7},{7,4},{8,9},{9,10},{10,1... | collective-permute-start | bytes 294920 | tf_op jit(solution)/shard_map/ppermute | solution.py:38
  121.3 11.6 %collective-permute-start.47 = (bf16[3,128,128]{2,1,0:T(8,128)(2,1)S(1)}, bf16[3,128,128]{2,1,0:T(8,128)(2,1)S(1)}, u32[]{:S(2)}, u32[]{:S(2)}) collective-permute-start(bf16[3,128,128]{2,1,0:T(8,128)(2,1)S(1)} %get-tuple-element.143), channel_id=1, source_target_pairs={{0,1},{1,2},{2,3},{3,0},{4,5},{5,6},{6,7},{7,4},{8,9},{9,10},{10,1... | collective-permute-start | bytes 294920 | tf_op jit(solution)/shard_map/ppermute | solution.py:38
  125.6 10.6 %collective-permute-start.48 = (bf16[3,128,128]{2,1,0:T(8,128)(2,1)S(1)}, bf16[3,128,128]{2,1,0:T(8,128)(2,1)S(1)}, u32[]{:S(2)}, u32[]{:S(2)}) collective-permute-start(bf16[3,128,128]{2,1,0:T(8,128)(2,1)S(1)} %get-tuple-element.144), channel_id=1, source_target_pairs={{0,2},{1,3},{2,0},{3,1},{4,6},{5,7},{6,4},{7,5},{8,10},{9,11},{10,... | collective-permute-start | bytes 294920 | tf_op jit(solution)/shard_map/ppermute | solution.py:38
  127.6 8.6 %collective-permute-start.49 = (bf16[3,128,128]{2,1,0:T(8,128)(2,1)S(1)}, bf16[3,128,128]{2,1,0:T(8,128)(2,1)S(1)}, u32[]{:S(2)}, u32[]{:S(2)}) collective-permute-start(bf16[3,128,128]{2,1,0:T(8,128)(2,1)S(1)} %get-tuple-element.145), channel_id=1, source_target_pairs={{0,3},{1,0},{2,1},{3,2},{4,7},{5,4},{6,5},{7,6},{8,11},{9,8},{10,9... | collective-permute-start | bytes 294920 | tf_op jit(solution)/shard_map/ppermute | solution.py:38
  132.3 7.5 %collective-permute-start.44 = (bf16[3,128,128]{2,1,0:T(8,128)(2,1)S(1)}, bf16[3,128,128]{2,1,0:T(8,128)(2,1)S(1)}, u32[]{:S(2)}, u32[]{:S(2)}) collective-permute-start(bf16[3,128,128]{2,1,0:T(8,128)(2,1)S(1)} %get-tuple-element.139), channel_id=1, source_target_pairs={{0,1},{1,2},{2,3},{3,0},{4,5},{5,6},{6,7},{7,4},{8,9},{9,10},{10,1... | collective-permute-start | bytes 294920 | tf_op jit(solution)/shard_map/ppermute | solution.py:38
  132.4 10.4 %collective-permute-start.45 = (bf16[3,128,128]{2,1,0:T(8,128)(2,1)S(1)}, bf16[3,128,128]{2,1,0:T(8,128)(2,1)S(1)}, u32[]{:S(2)}, u32[]{:S(2)}) collective-permute-start(bf16[3,128,128]{2,1,0:T(8,128)(2,1)S(1)} %get-tuple-element.140), channel_id=1, source_target_pairs={{0,2},{1,3},{2,0},{3,1},{4,6},{5,7},{6,4},{7,5},{8,10},{9,11},{10,... | collective-permute-start | bytes 294920 | tf_op jit(solution)/shard_map/ppermute | solution.py:38
  132.9 9.9 %collective-permute-start.46 = (bf16[3,128,128]{2,1,0:T(8,128)(2,1)S(1)}, bf16[3,128,128]{2,1,0:T(8,128)(2,1)S(1)}, u32[]{:S(2)}, u32[]{:S(2)}) collective-permute-start(bf16[3,128,128]{2,1,0:T(8,128)(2,1)S(1)} %get-tuple-element.141), channel_id=1, source_target_pairs={{0,3},{1,0},{2,1},{3,2},{4,7},{5,4},{6,5},{7,6},{8,11},{9,8},{10,9... | collective-permute-start | bytes 294920 | tf_op jit(solution)/shard_map/ppermute | solution.py:38
  144.9 14.9 %collective-permute-start.50 = (bf16[6,128,128]{2,1,0:T(8,128)(2,1)S(1)}, bf16[6,128,128]{2,1,0:T(8,128)(2,1)S(1)}, u32[]{:S(2)}, u32[]{:S(2)}) collective-permute-start(bf16[6,128,128]{2,1,0:T(8,128)(2,1)S(1)} %get-tuple-element.147), channel_id=1, source_target_pairs={{0,28},{4,0},{8,4},{12,8},{16,12},{20,16},{24,20},{28,24},{1,29},{... | collective-permute-start | bytes 589832 | tf_op jit(solution)/shard_map/ppermute | solution.py:38
  145.8 14.0 %collective-permute-start.51 = (bf16[6,128,128]{2,1,0:T(8,128)(2,1)S(1)}, bf16[6,128,128]{2,1,0:T(8,128)(2,1)S(1)}, u32[]{:S(2)}, u32[]{:S(2)}) collective-permute-start(bf16[6,128,128]{2,1,0:T(8,128)(2,1)S(1)} %get-tuple-element.148), channel_id=1, source_target_pairs={{0,4},{4,8},{8,12},{12,16},{16,20},{20,24},{24,28},{28,0},{1,5},{5... | collective-permute-start | bytes 589832 | tf_op jit(solution)/shard_map/ppermute | solution.py:38
  145.8 6.1 %collective-permute-start.52 = (bf16[2,128,128]{2,1,0:T(8,128)(2,1)S(1)}, bf16[2,128,128]{2,1,0:T(8,128)(2,1)S(1)}, u32[]{:S(2)}, u32[]{:S(2)}) collective-permute-start(bf16[2,128,128]{2,1,0:T(8,128)(2,1)S(1)} %get-tuple-element.149), channel_id=1, source_target_pairs={{0,8},{4,12},{8,16},{12,20},{16,24},{20,28},{24,0},{28,4},{1,9},{5... | collective-permute-start | bytes 196616 | tf_op jit(solution)/shard_map/ppermute | solution.py:38
  147.4 8.1 %collective-permute-start.53 = (bf16[2,128,128]{2,1,0:T(8,128)(2,1)S(1)}, bf16[2,128,128]{2,1,0:T(8,128)(2,1)S(1)}, u32[]{:S(2)}, u32[]{:S(2)}) collective-permute-start(bf16[2,128,128]{2,1,0:T(8,128)(2,1)S(1)} %get-tuple-element.150), channel_id=1, source_target_pairs={{0,12},{4,16},{8,20},{12,24},{16,28},{20,0},{24,4},{28,8},{1,13},{... | collective-permute-start | bytes 196616 | tf_op jit(solution)/shard_map/ppermute | solution.py:38
  147.9 8.6 %collective-permute-start.54 = (bf16[2,128,128]{2,1,0:T(8,128)(2,1)S(1)}, bf16[2,128,128]{2,1,0:T(8,128)(2,1)S(1)}, u32[]{:S(2)}, u32[]{:S(2)}) collective-permute-start(bf16[2,128,128]{2,1,0:T(8,128)(2,1)S(1)} %get-tuple-element.151), channel_id=1, source_target_pairs={{0,16},{4,20},{8,24},{12,28},{16,0},{20,4},{24,8},{28,12},{1,17},{... | collective-permute-start | bytes 196616 | tf_op jit(solution)/shard_map/ppermute | solution.py:38
  152.0 5.4 %collective-permute-start.55 = (bf16[2,128,128]{2,1,0:T(8,128)(2,1)S(1)}, bf16[2,128,128]{2,1,0:T(8,128)(2,1)S(1)}, u32[]{:S(2)}, u32[]{:S(2)}) collective-permute-start(bf16[2,128,128]{2,1,0:T(8,128)(2,1)S(1)} %get-tuple-element.152), channel_id=1, source_target_pairs={{0,20},{4,24},{8,28},{12,0},{16,4},{20,8},{24,12},{28,16},{1,21},{... | collective-permute-start | bytes 196616 | tf_op jit(solution)/shard_map/ppermute | solution.py:38
  155.5 4.3 %collective-permute-start.56 = (bf16[2,128,128]{2,1,0:T(8,128)(2,1)S(1)}, bf16[2,128,128]{2,1,0:T(8,128)(2,1)S(1)}, u32[]{:S(2)}, u32[]{:S(2)}) collective-permute-start(bf16[2,128,128]{2,1,0:T(8,128)(2,1)S(1)} %get-tuple-element.153), channel_id=1, source_target_pairs={{0,24},{4,28},{8,0},{12,4},{16,8},{20,12},{24,16},{28,20},{1,25},{... | collective-permute-start | bytes 196616 | tf_op jit(solution)/shard_map/ppermute | solution.py:38
